TPU v7x, 32 devices: a whole 2x2x4 slice. The times are simulated.
32 devices in a mesh: ctx: 8 (over z, x), fsdp: 4 (over y, core).
Axes of the slice: x: 2, y: 2, z: 4, core: 2. Of those that a mesh axis runs over, the one named last changes fastest.
Arguments:
- proj_xbc: bfloat16 [4, 1024, 10240], P('fsdp', 'ctx'), may hold values from -6 to 6
- proj_dt: bfloat16 [4, 1024, 128], P('fsdp', 'ctx'), may hold values from -3 to 3
- proj_gate: bfloat16 [4, 1024, 8192], P('fsdp', 'ctx'), may hold values from -6 to 6
- out_grad: bfloat16 [4, 1024, 8192], P('fsdp', 'ctx'), may hold values from -6 to 6
- conv_weight: float32 [4, 10240], P(None, 'fsdp'), may hold values from -3 to 3
- conv_bias: float32 [10240], P('fsdp'), may hold values from -0.5 to 0.5
- decay_log: float32 [128], P('fsdp'), may hold values from -12 to -3
- step_bias: float32 [128], P('fsdp'), may hold values from -0.5 to 0.5
- skip_gain: float32 [128], P('fsdp'), may hold values from 0.5 to 1.5
- norm_gain: float32 [8192], P('fsdp'), may hold values from 0.5 to 1.5
Outputs:
- grad_xbc: bfloat16 [4, 1024, 10240], P('fsdp', 'ctx')
- grad_dt: float32 [4, 1024, 128], P('fsdp', 'ctx')
- grad_gate: bfloat16 [4, 1024, 8192], P('fsdp', 'ctx')
- grad_conv_weight: float32 [4, 10240], P(None, 'fsdp')
- grad_conv_bias: float32 [10240], P('fsdp')
- grad_decay_log: float32 [128], P('fsdp')
- grad_step_bias: float32 [128], P('fsdp')
- grad_skip_gain: float32 [128], P('fsdp')
- grad_norm_gain: float32 [8192], P('fsdp')
All inputs are finite; a program needn't handle non-finite values.
Results may differ from a plain program's by a relative error of at most 0.012.
Values may be sent and summed in bfloat16 or wider, within the bound.
No kernel may reach another device: no remote copies, remote signals or barrier semaphores. Data moves between devices by JAX's collectives and lax.ppermute only.
A program may use at most 320 MiB of HBM per device.

v0:
```python
import math

import jax
import jax.numpy as jnp
from jax import lax
from jax.experimental import pallas as pl
from jax.experimental.pallas import tpu as pltpu
from jax.sharding import PartitionSpec as P

HEAD_DIM = 64
STATE = 128
GROUPS = 8
KERNEL = 4
EPSILON = 1e-05
HALO = KERNEL - 1
PAD = 8
F32 = jnp.float32
BF16 = jnp.bfloat16
HIGHEST = lax.Precision.HIGHEST


def mm(a, b):
    return jnp.dot(a, b, preferred_element_type=F32)


def mm_nt(a, b):
    return lax.dot_general(a, b, (((1,), (1,)), ((), ())), preferred_element_type=F32)


def sigmoid(v):
    return 0.5 * jnp.tanh(0.5 * v) + 0.5


def softplus(v):
    return jnp.maximum(v, 0.0) + jnp.log(1.0 + jnp.exp(-jnp.abs(v)))


def spread_heads(table, group, per_group):
    heads = table.shape[1]
    table = pltpu.roll(table, lax.rem(heads - group * per_group, heads), 1)
    rows = table.shape[0]
    pair = 128 // HEAD_DIM
    lane = lax.broadcasted_iota(jnp.int32, (rows, 128), 1)
    tiles = []
    for i in range(per_group // pair):
        tile = jnp.broadcast_to(table[:, pair * i : pair * i + 1], (rows, 128))
        for p in range(1, pair):
            col = jnp.broadcast_to(table[:, pair * i + p : pair * i + p + 1], (rows, 128))
            tile = jnp.where(lane >= p * HEAD_DIM, col, tile)
        tiles.append(tile)
    return jnp.concatenate(tiles, axis=1)


def sum_heads(values, group, per_group, heads):
    width = values.shape[1]
    row = lax.broadcasted_iota(jnp.int32, (width, heads), 0) // HEAD_DIM + group * per_group
    col = lax.broadcasted_iota(jnp.int32, (width, heads), 1)
    pick = jnp.where(row == col, 1.0, 0.0).astype(BF16)
    high = values.astype(BF16)
    low = (values - high.astype(F32)).astype(BF16)
    return mm(high, pick) + mm(low, pick)


def lower_mask(n):
    return lax.broadcasted_iota(jnp.int32, (n, n), 0) >= lax.broadcasted_iota(jnp.int32, (n, n), 1)


def upper_mask(n):
    return lax.broadcasted_iota(jnp.int32, (n, n), 0) <= lax.broadcasted_iota(jnp.int32, (n, n), 1)


def conv_pre(x_ref, halo_ref, w_ref, xs):
    length = x_ref.shape[0]
    xs[PAD - HALO : PAD, :] = halo_ref[...].astype(F32)
    xs[PAD : PAD + length, :] = x_ref[...].astype(F32)
    pre = jnp.broadcast_to(w_ref[KERNEL : KERNEL + 1, :], (length, x_ref.shape[1]))
    for k in range(KERNEL):
        pre = pre + w_ref[k : k + 1, :] * xs[PAD - HALO + k : PAD - HALO + k + length, :]
    return pre


def front_kernel(per_group, x_ref, halo_ref, w_ref, dt_ref, sb_ref, dl_ref,
                 mixed_ref, vp_ref, ut_ref, ec_ref, ei_ref, et_ref, xs, ks):
    j = pl.program_id(0)
    length = x_ref.shape[0]

    @pl.when(j == 0)
    def _():
        step = softplus(dt_ref[...].astype(F32) + sb_ref[...])
        ld = -jnp.exp(dl_ref[...]) * step
        tril = jnp.where(lower_mask(length), 1.0, 0.0).astype(F32)
        cum = jnp.dot(tril, ld, precision=HIGHEST, preferred_element_type=F32)
        ec_ref[...] = jnp.exp(cum)
        ei_ref[...] = jnp.exp(-cum) * step

    pre = conv_pre(x_ref, halo_ref, w_ref, xs)
    mixed = (pre * sigmoid(pre)).astype(BF16)
    mixed_ref[...] = mixed

    @pl.when(j == 0)
    def _():
        for g in range(GROUPS):
            ks[g] = mixed[:, g * STATE : (g + 1) * STATE]

    @pl.when(j >= 2)
    def _():
        g = j - 2
        eix = spread_heads(ei_ref[...], g, per_group)
        vp = (mixed.astype(F32) * eix).astype(BF16)
        vp_ref[...] = vp
        et = spread_heads(ec_ref[length - 8 : length, :], g, per_group)[7:8, :]
        et_ref[...] = et
        ut = mm(ks[g].astype(F32).T.astype(BF16), vp) * et
        reps, _, part = ut_ref.shape
        for r in range(reps):
            ut_ref[r] = ut[:, r * part : (r + 1) * part].astype(BF16)


def join_parts(ref):
    if ref.shape[0] == 1:
        return ref[0]
    return jnp.concatenate([ref[r] for r in range(ref.shape[0])], axis=1)


def middle_kernel(per_group, v_ref, k_ref, q_ref, vp_ref, st_ref, ec_ref, gate_ref, og_ref, gain_ref, skip_ref,
                  dy_ref, dyp_ref, gg_ref, gt_ref, rows_ref, a1_ref):
    g = pl.program_id(0)
    length, width = v_ref.shape
    heads = ec_ref.shape[1]
    q = q_ref[...]
    z = jnp.where(lower_mask(length), mm_nt(q, k_ref[...]), 0.0).astype(BF16)
    yn = mm(jnp.concatenate([z, q], axis=1), jnp.concatenate([vp_ref[...], join_parts(st_ref)], axis=0))
    ecx = spread_heads(ec_ref[...], g, per_group)
    v = v_ref[...].astype(F32)
    y = (ecx * yn + skip_ref[...] * v).astype(BF16).astype(F32)
    gate = gate_ref[...].astype(F32)
    og = og_ref[...].astype(F32)
    sig = sigmoid(gate)
    act = gate * sig
    gated = y * act
    scale = lax.rsqrt(jnp.sum(gated * gated, axis=1, keepdims=True) * (1.0 / width) + EPSILON)
    dgn = og * gain_ref[...]
    inner = jnp.sum(dgn * gated, axis=1, keepdims=True) * (1.0 / width)
    dgated = scale * dgn - gated * (scale * scale * scale * inner)
    dyb = (dgated * act).astype(BF16)
    dy_ref[...] = dyb
    gg_ref[...] = (dgated * y * (sig + act * (1.0 - sig))).astype(BF16)
    dy = dyb.astype(F32)
    dyp = (ecx * dy).astype(BF16)
    dyp_ref[...] = dyp
    gt = mm(q.astype(F32).T.astype(BF16), dyp)
    reps, _, part = gt_ref.shape
    for r in range(reps):
        gt_ref[r] = gt[:, r * part : (r + 1) * part].astype(BF16)
    rows_ref[...] = jnp.zeros(rows_ref.shape, F32)
    rows_ref[0:1, :] = jnp.sum(og * gated * scale, axis=0, keepdims=True)
    rows_ref[1:2, :] = jnp.sum(dy * v, axis=0, keepdims=True)

    @pl.when(g == 0)
    def _():
        a1_ref[...] = jnp.zeros(a1_ref.shape, F32)

    a1_ref[...] += sum_heads(dyp.astype(F32) * yn, g, per_group, heads)


def back_kernel(per_group, v_ref, k_ref, q_ref, vp_ref, st_ref, en_ref, dy_ref, dyp_ref, x_ref, halo_ref, w_ref,
                skip_ref, et_ref, ei_ref, a1_ref, dt_ref, sb_ref, dl_ref,
                gx_ref, edge_ref, wr_ref, gdt_ref, hs_ref, xs, gs, gm, dkq, a2, last):
    j = pl.program_id(0)
    length, width = v_ref.shape
    heads = ei_ref.shape[1]

    @pl.when(j == 0)
    def _():
        a2[...] = jnp.zeros(a2.shape, F32)
        last[...] = jnp.zeros(last.shape, F32)
        gs[length:, :] = jnp.zeros((gs.shape[0] - length, gs.shape[1]), F32)

    @pl.when(j < GROUPS)
    def _():
        k = k_ref[...]
        q = q_ref[...]
        vp = vp_ref[...]
        dyp = dyp_ref[...]
        st = join_parts(st_ref)
        en = (et_ref[...] * join_parts(en_ref).astype(F32)).astype(BF16)
        low = lower_mask(length)
        zt = jnp.where(upper_mask(length), mm_nt(k, q), 0.0).astype(BF16)
        dvp = mm(jnp.concatenate([zt, k], axis=1), jnp.concatenate([dyp, en], axis=0))
        eix = spread_heads(ei_ref[...], j, per_group)
        gm[...] = eix * dvp + skip_ref[...] * dy_ref[...].astype(F32)
        a2[...] += sum_heads(vp.astype(F32) * dvp, j, per_group, heads)
        ends = en.astype(F32) * (st.astype(F32) + mm(k.astype(F32).T.astype(BF16), vp))
        ends = jnp.broadcast_to(jnp.sum(ends, axis=0, keepdims=True), (8, width))
        last[...] += sum_heads(ends, j, per_group, heads)
        dz = jnp.where(low, mm_nt(dyp, vp), 0.0)
        dzb = dz.astype(BF16)
        cols = pl.ds(pl.multiple_of(j * STATE, STATE), STATE)
        dkq[0, :, cols] = mm(dz.T.astype(BF16), q) + mm_nt(vp, en)
        dkq[1, :, cols] = mm(dzb, k) + mm_nt(dyp, st)

    @pl.when(j >= GROUPS)
    def _():
        gm[...] = dkq[j - GROUPS]

    pre = conv_pre(x_ref, halo_ref, w_ref, xs)
    sig = sigmoid(pre)
    gp = gm[...] * (sig * (1.0 + pre * (1.0 - sig)))
    gs[0:length, :] = gp
    wr_ref[...] = jnp.zeros(wr_ref.shape, F32)
    total = jnp.zeros(gp.shape, F32)
    for k in range(KERNEL):
        lead = HALO - k
        total = total + w_ref[k : k + 1, :] * gs[lead : lead + length, :]
        wr_ref[k : k + 1, :] = jnp.sum(gp * xs[PAD - HALO + k : PAD - HALO + k + length, :], axis=0, keepdims=True)
    wr_ref[KERNEL : KERNEL + 1, :] = jnp.sum(gp, axis=0, keepdims=True)
    gx_ref[...] = total.astype(BF16)
    edge_ref[...] = jnp.zeros(edge_ref.shape, F32)
    edge_ref[0:HALO, :] = gp[0:HALO, :]
    edge_ref[HALO : 2 * HALO, :] = total[length - HALO : length, :]

    @pl.when(j == pl.num_programs(0) - 1)
    def _():
        raw = dt_ref[...].astype(F32) + sb_ref[...]
        step = softplus(raw)
        rate = jnp.exp(dl_ref[...])
        row = lax.broadcasted_iota(jnp.int32, (length, heads), 0)
        dcum = a1_ref[...] - a2[...] + jnp.where(row == length - 1, last[0:1, :], 0.0)
        triu = jnp.where(upper_mask(length), 1.0, 0.0).astype(F32)
        dld = jnp.dot(triu, dcum, precision=HIGHEST, preferred_element_type=F32)
        gdt = (a2[...] / step - rate * dld) * sigmoid(raw)
        gdt_ref[...] = gdt
        hs_ref[...] = jnp.zeros(hs_ref.shape, F32)
        hs_ref[0:1, :] = jnp.sum(-rate * step * dld, axis=0, keepdims=True)
        hs_ref[1:2, :] = jnp.sum(gdt, axis=0, keepdims=True)


def scan_kernel(backward, u_ref, d_ref, o_ref):
    count = u_ref.shape[0]
    acc = jnp.zeros(u_ref.shape[1:], F32)
    order = range(count - 1, -1, -1) if backward else range(count)
    for i in order:
        o_ref[i] = acc.astype(BF16)
        acc = d_ref[i : i + 1, :] * acc + u_ref[i].astype(F32)


PARAMS = pltpu.CompilerParams(vmem_limit_bytes=48 * 1024 * 1024)


def scan_states(states, decay, backward):
    count, rows, wide = states.shape
    tile = 32
    return pl.pallas_call(
        lambda *refs: scan_kernel(backward, *refs),
        out_shape=jax.ShapeDtypeStruct(states.shape, BF16),
        grid=(rows // tile,),
        in_specs=[
            pl.BlockSpec((count, tile, wide), lambda i: (0, i, 0)),
            pl.BlockSpec((count, wide), lambda i: (0, 0)),
        ],
        out_specs=pl.BlockSpec((count, tile, wide), lambda i: (0, i, 0)),
        compiler_params=PARAMS,
        name="scan_back" if backward else "scan_front",
    )(states, decay)


def body(proj_xbc, proj_dt, proj_gate, out_grad, conv_weight, conv_bias, decay_log, step_bias, skip_gain, norm_gain):
    x, dt, gate, og = proj_xbc[0], proj_dt[0], proj_gate[0], out_grad[0]
    length, channels = x.shape
    heads = dt.shape[1]
    inner = heads * HEAD_DIM
    ranks = lax.axis_size("ctx")
    shards = lax.axis_size("fsdp")
    per_group = heads // GROUPS
    width = per_group * HEAD_DIM
    reps = ranks // GROUPS
    wide = inner // ranks
    own_heads = heads // ranks
    c_loc, g_loc, h_loc = channels // shards, inner // shards, heads // shards
    spare = c_loc - g_loc - 3 * h_loc
    groups = GROUPS
    blocks = channels // width

    ahead = [(i, i + 1) for i in range(ranks - 1)]
    behind = [(i + 1, i) for i in range(ranks - 1)]
    halo = lax.ppermute(x[length - HALO :, :], "ctx", ahead)

    def pack_row(gain, decay, step, skip):
        return jnp.concatenate([gain, decay, step, skip, jnp.zeros(gain.shape[:-1] + (spare,), F32)], axis=-1)

    packed = jnp.concatenate(
        [conv_weight, conv_bias[None], pack_row(norm_gain, decay_log, step_bias, skip_gain)[None],
         jnp.zeros((8 - KERNEL - 2, c_loc), F32)], axis=0)
    full = lax.all_gather(packed, "fsdp", axis=1, tiled=True)
    extra = full[KERNEL + 1].reshape(shards, c_loc)
    gain = extra[:, :g_loc].reshape(1, inner)
    decay = extra[:, g_loc : g_loc + h_loc].reshape(1, heads)
    step_b = extra[:, g_loc + h_loc : g_loc + 2 * h_loc].reshape(1, heads)
    skip = extra[:, g_loc + 2 * h_loc : g_loc + 3 * h_loc].reshape(1, heads)
    skip_x = jnp.repeat(skip, HEAD_DIM, axis=1)

    rate = jnp.exp(-jnp.exp(decay[0]) * jnp.sum(jax.nn.softplus(dt.astype(F32) + step_b), axis=0))
    rates = lax.all_to_all(rate.reshape(ranks, own_heads), "ctx", 0, 0, tiled=True)
    rates_x = jnp.repeat(rates, HEAD_DIM, axis=1)

    def col(j):
        return jnp.where(j < 2, groups + j, j - 2)

    def grp(j):
        return jnp.maximum(j - 2, 0)

    full_head = pl.BlockSpec((length, heads), lambda j: (0, 0))
    row_head = pl.BlockSpec((1, heads), lambda j: (0, 0))
    state_shape = jax.ShapeDtypeStruct((ranks, STATE, wide), BF16)
    mixed, vp, ut, ec, ei, et = pl.pallas_call(
        lambda *refs: front_kernel(per_group, *refs),
        out_shape=(
            jax.ShapeDtypeStruct((length, channels), BF16),
            jax.ShapeDtypeStruct((length, inner), BF16),
            state_shape,
            jax.ShapeDtypeStruct((length, heads), F32),
            jax.ShapeDtypeStruct((length, heads), F32),
            jax.ShapeDtypeStruct((1, inner), F32),
        ),
        grid=(blocks,),
        in_specs=[
            pl.BlockSpec((length, width), lambda j: (0, col(j))),
            pl.BlockSpec((HALO, width), lambda j: (0, col(j))),
            pl.BlockSpec((8, width), lambda j: (0, col(j))),
            full_head, row_head, row_head,
        ],
        out_specs=(
            pl.BlockSpec((length, width), lambda j: (0, col(j))),
            pl.BlockSpec((length, width), lambda j: (0, grp(j))),
            pl.BlockSpec((reps, STATE, wide), lambda j: (grp(j), 0, 0)),
            full_head, full_head,
            pl.BlockSpec((1, width), lambda j: (0, grp(j))),
        ),
        scratch_shapes=[pltpu.VMEM((PAD + length, width), F32), pltpu.VMEM((GROUPS, length, STATE), BF16)],
        compiler_params=PARAMS,
        name="front",
    )(x, halo, full, dt, step_b, decay)

    def swap(states):
        return lax.all_to_all(states, "ctx", 0, 0, tiled=True)

    starts = swap(scan_states(swap(ut), rates_x, False))

    wide_spec = pl.BlockSpec((length, width), lambda g: (0, g))
    line_spec = pl.BlockSpec((1, width), lambda g: (0, g))
    k_at = inner // STATE
    q_at = k_at + GROUPS
    state_spec = pl.BlockSpec((reps, STATE, wide), lambda g: (g, 0, 0))
    dy, dyp, grad_gate, gt, rows, a1 = pl.pallas_call(
        lambda *refs: middle_kernel(per_group, *refs),
        out_shape=(
            jax.ShapeDtypeStruct((length, inner), BF16),
            jax.ShapeDtypeStruct((length, inner), BF16),
            jax.ShapeDtypeStruct((length, inner), BF16),
            state_shape,
            jax.ShapeDtypeStruct((8, inner), F32),
            jax.ShapeDtypeStruct((length, heads), F32),
        ),
        grid=(GROUPS,),
        in_specs=[
            wide_spec,
            pl.BlockSpec((length, STATE), lambda g: (0, k_at + g)),
            pl.BlockSpec((length, STATE), lambda g: (0, q_at + g)),
            wide_spec, state_spec, full_head, wide_spec, wide_spec, line_spec, line_spec,
        ],
        out_specs=(wide_spec, wide_spec, wide_spec, state_spec, pl.BlockSpec((8, width), lambda g: (0, g)), full_head),
        compiler_params=PARAMS,
        name="middle",
    )(mixed, mixed, mixed, vp, starts, ec, gate, og, gain, skip_x)

    ends = swap(scan_states(swap(gt), rates_x, True))

    def cap(j):
        return jnp.minimum(j, GROUPS - 1)

    wide_cap = pl.BlockSpec((length, width), lambda j: (0, cap(j)))
    line_cap = pl.BlockSpec((1, width), lambda j: (0, cap(j)))
    state_cap = pl.BlockSpec((reps, STATE, wide), lambda j: (cap(j), 0, 0))
    eight = pl.BlockSpec((8, width), lambda j: (0, j))
    wide_all = pl.BlockSpec((length, width), lambda j: (0, j))
    gx, edge, wr, grad_dt, hs = pl.pallas_call(
        lambda *refs: back_kernel(per_group, *refs),
        out_shape=(
            jax.ShapeDtypeStruct((length, channels), BF16),
            jax.ShapeDtypeStruct((8, channels), F32),
            jax.ShapeDtypeStruct((8, channels), F32),
            jax.ShapeDtypeStruct((length, heads), F32),
            jax.ShapeDtypeStruct((8, heads), F32),
        ),
        grid=(blocks,),
        in_specs=[
            wide_cap,
            pl.BlockSpec((length, STATE), lambda j: (0, k_at + cap(j))),
            pl.BlockSpec((length, STATE), lambda j: (0, q_at + cap(j))),
            wide_cap, state_cap, state_cap, wide_cap, wide_cap,
            wide_all,
            pl.BlockSpec((HALO, width), lambda j: (0, j)),
            eight, line_cap, line_cap, full_head, full_head, full_head, row_head, row_head,
        ],
        out_specs=(wide_all, eight, eight, full_head, pl.BlockSpec((8, heads), lambda j: (0, 0))),
        scratch_shapes=[
            pltpu.VMEM((PAD + length, width), F32),
            pltpu.VMEM((PAD + length, width), F32),
            pltpu.VMEM((length, width), F32),
            pltpu.VMEM((2, length, width), F32),
            pltpu.VMEM((length, heads), F32),
            pltpu.VMEM((8, heads), F32),
        ],
        compiler_params=PARAMS,
        name="back",
    )(mixed, mixed, mixed, vp, starts, ends, dy, dyp, x, halo, full, skip_x, et, ei, a1, dt, step_b, decay)

    next_gp = lax.ppermute(edge[:HALO], "ctx", behind)
    fixed = []
    for i in range(HALO):
        row = edge[HALO + i]
        for k in range(i + 1):
            row = row + full[k] * next_gp[i - k]
        fixed.append(row)
    grad_xbc = lax.dynamic_update_slice(gx, jnp.stack(fixed).astype(BF16), (length - HALO, 0))

    skip_grad = jnp.sum(rows[1].reshape(heads, HEAD_DIM), axis=1)
    extra_row = pack_row(
        rows[0].reshape(shards, g_loc), hs[0].reshape(shards, h_loc), hs[1].reshape(shards, h_loc),
        skip_grad.reshape(shards, h_loc)).reshape(1, channels)
    parts = jnp.concatenate([wr[: KERNEL + 1], extra_row, jnp.zeros((8 - KERNEL - 2, channels), F32)], axis=0)
    split = ranks // 8
    piece = c_loc // split
    parts = parts.reshape(8, shards, split, piece).transpose(0, 2, 1, 3).reshape(ranks * shards, piece)
    summed = jnp.sum(lax.all_to_all(parts, ("ctx", "fsdp"), 0, 0, tiled=True), axis=0)
    summed = summed * (1.0 / math.sqrt(length * ranks * shards))
    mine = lax.all_gather(summed, "ctx", axis=0, tiled=True).reshape(8, c_loc)
    tail = mine[KERNEL + 1]
    return (
        grad_xbc[None],
        grad_dt[None],
        grad_gate[None],
        mine[:KERNEL],
        mine[KERNEL],
        tail[g_loc : g_loc + h_loc],
        tail[g_loc + h_loc : g_loc + 2 * h_loc],
        tail[g_loc + 2 * h_loc : g_loc + 3 * h_loc],
        tail[:g_loc],
    )


def solution(mesh):
    data = P("fsdp", "ctx", None)
    one = P("fsdp")
    return jax.shard_map(
        body,
        mesh=mesh,
        in_specs=(data, data, data, data, P(None, "fsdp"), one, one, one, one, one),
        out_specs=(data, data, data, P(None, "fsdp"), one, one, one, one, one),
        check_vma=False,
    )
```

profile of v0, /device:TPU:0, one launch (start us, length us, event | category | flops | bytes accessed | tf_op | source)
XLA Modules:
  0.0 358.1 jit_solution(8744410399735791759)
XLA Ops:
  0.6 1.0 slice_bitcast_fusion
  1.6 4.8 %collective-permute-start = (bf16[3,10240]{1,0:T(4,128)(2,1)S(1)}, bf16[3,10240]{1,0:T(4,128)(2,1)S(1)}, u32[]{:S(2)}, u32[]{:S(2)}) collective-permute-start(bf16[3,10240]{1,0:T(4,128)(2,1)S(1)} %slice_bitcast_fusion), channel_id=1, source_target_pairs={{0,4},{4,8},{8,12},{12,16},{16,20},{20,24},{24,28},{1,5},{5,9},{9,... | collective-permute-start | bytes 184328 | tf_op jit(solution)/shard_map/ppermute | solution.py:286
  6.5 0.8 concatenate.20
  7.3 0.7 broadcast_in_dim.35
  8.0 0.1 pad.9.clone
  8.1 0.9 maximum_maximum_fusion.1
  8.9 6.1 %all_gather.6.refs_2_.refs_10_ = f32[8,10240]{1,0:T(8,128)S(1)} all-gather(f32[8,2560]{1,0:T(8,128)S(1)} %maximum_maximum_fusion.1), channel_id=1, replica_groups=mesh['ctx'=8,'fsdp'=4] {'fsdp'}, dimensions={1}, use_global_device_ids=true | all-gather | bytes 409600 | tf_op jit(solution)/shard_map/all_gather | solution.py:294
  15.0 0.1 slice_reduce_fusion
  15.2 0.1 fusion.5
  15.2 0.1 add.38
  15.3 0.8 fusion
  16.2 0.1 reduce_sum.30
  16.2 0.1 neg.19
  16.3 0.6 multiply_exponential_fusion
  16.9 4.9 %all-to-all-start.1 = ((f32[8,1,16]{2,1,0:T(1,128)}), f32[8,1,16]{2,1,0:T(1,128)S(1)}, u32[]{:S(2)}, u32[]{:S(2)}) async-start(f32[8,1,16]{2,1,0:T(1,128)} %bitcast.3), calls=%async_computation.1 | async-start | bytes 8192 | tf_op jit(solution)/shard_map/all_to_all | solution.py:303
  21.8 0.1 reshape.145.refs_4_.refs_16_
  21.9 0.1 reshape.146.refs_5_.refs_17_
  22.0 0.8 copy-done.9
  22.7 15.0 %front.1 = (bf16[128,10240]{1,0:T(8,128)(2,1)}, bf16[128,8192]{1,0:T(8,128)(2,1)S(1)}, bf16[8,128,1024]{2,1,0:T(8,128)(2,1)S(1)}, f32[128,128]{1,0:T(8,128)S(1)}...) custom-call(bf16[128,10240]{1,0:T(8,128)(2,1)} %bitcast.34, bf16[3,10240]{1,0:T(4,128)(2,1)S(1)} %collective-permute-done.refs_1_.refs_9_, ...), custom_call_target="tpu_custom_call" | custom-call | tf_op jit(solution)/shard_map/front/pallas_call | solution.py:315
  37.7 1.3 copy-done.4
  39.1 1.3 copy-done.8
  40.4 6.0 %all-to-all-start = ((bf16[8,128,1024]{2,1,0:T(8,128)(2,1)}), bf16[8,128,1024]{2,1,0:T(8,128)(2,1)S(1)}, u32[]{:S(2)}, u32[]{:S(2)}) async-start(bf16[8,128,1024]{2,1,0:T(8,128)(2,1)} %copy-done.8), calls=%async_computation | async-start | bytes 4194304 | tf_op jit(solution)/shard_map/all_to_all | solution.py:345
  46.4 0.1 broadcast_in_dim.39
  46.5 0.1 reshape.147.refs_1_
  46.5 48.0 %all-to-all-done.refs_0_ = bf16[8,128,1024]{2,1,0:T(8,128)(2,1)S(1)} async-done(((bf16[8,128,1024]{2,1,0:T(8,128)(2,1)}), bf16[8,128,1024]{2,1,0:T(8,128)(2,1)S(1)}, u32[]{:S(2)}, u32[]{:S(2)}) %all-to-all-start) | async-done | bytes 2097184 | tf_op jit(solution)/shard_map/all_to_all | solution.py:345
  94.6 0.8 scan_front.1
  95.4 1.3 copy-done.3
  96.7 3.6 %all-to-all-start.2 = ((bf16[8,128,1024]{2,1,0:T(8,128)(2,1)}), bf16[8,128,1024]{2,1,0:T(8,128)(2,1)S(1)}, u32[]{:S(2)}, u32[]{:S(2)}) async-start(bf16[8,128,1024]{2,1,0:T(8,128)(2,1)} %copy-done.3), calls=%async_computation.2 | async-start | bytes 4194304 | tf_op jit(solution)/shard_map/all_to_all | solution.py:345
  100.3 0.1 reshape.149
  100.4 0.1 broadcast_in_dim.40
  100.5 0.1 broadcast_in_dim.41.refs_9_.refs_11_
  100.7 48.1 %all-to-all-done.2.refs_4_ = bf16[8,128,1024]{2,1,0:T(8,128)(2,1)S(1)} async-done(((bf16[8,128,1024]{2,1,0:T(8,128)(2,1)}), bf16[8,128,1024]{2,1,0:T(8,128)(2,1)S(1)}, u32[]{:S(2)}, u32[]{:S(2)}) %all-to-all-start.2) | async-done | bytes 2097184 | tf_op jit(solution)/shard_map/all_to_all | solution.py:345
  148.8 1.3 copy-done
  150.1 15.2 %middle.1 = (bf16[128,8192]{1,0:T(8,128)(2,1)S(1)}, bf16[128,8192]{1,0:T(8,128)(2,1)S(1)}, bf16[128,8192]{1,0:T(8,128)(2,1)}, bf16[8,128,1024]{2,1,0:T(8,128)(2,...) custom-call(bf16[128,10240]{1,0:T(8,128)(2,1)} %get-tuple-element.26.refs_0_.refs_1_.refs_2_, ...), custom_call_target="tpu_custom_call" | custom-call | tf_op jit(solution)/shard_map/middle/pallas_call | solution.py:354
  165.3 1.4 copy-done.6
  166.6 1.4 copy-done.7
  168.0 52.0 %all_to_all.39.refs_0_ = bf16[8,128,1024]{2,1,0:T(8,128)(2,1)S(1)} all-to-all(bf16[8,128,1024]{2,1,0:T(8,128)(2,1)} %get-tuple-element.30), channel_id=1, replica_groups=mesh['ctx'=8,'fsdp'=4] {'ctx'}, dimensions={0} | all-to-all | bytes 4194304 | tf_op jit(solution)/shard_map/all_to_all | solution.py:345
  220.0 0.8 scan_back.1
  220.9 1.4 copy-done.2
  222.2 4.5 %all-to-all-start.4 = ((bf16[8,128,1024]{2,1,0:T(8,128)(2,1)}), bf16[8,128,1024]{2,1,0:T(8,128)(2,1)}, u32[]{:S(2)}, u32[]{:S(2)}) async-start(bf16[8,128,1024]{2,1,0:T(8,128)(2,1)} %copy-done.2), calls=%async_computation.4 | async-start | bytes 4194304 | tf_op jit(solution)/shard_map/all_to_all | solution.py:345
  226.7 0.2 slice_reduce_fusion.1
  226.9 0.1 reshape_squeeze.19
  227.0 0.1 reduce_sum.31
  227.1 0.1 reshape.150
  227.2 46.8 %all-to-all-done.4.refs_5_ = bf16[8,128,1024]{2,1,0:T(8,128)(2,1)} async-done(((bf16[8,128,1024]{2,1,0:T(8,128)(2,1)}), bf16[8,128,1024]{2,1,0:T(8,128)(2,1)}, u32[]{:S(2)}, u32[]{:S(2)}) %all-to-all-start.4) | async-done | bytes 2097184 | tf_op jit(solution)/shard_map/all_to_all | solution.py:345
  274.0 1.6 copy-done.5
  275.6 29.6 %back.1 = (bf16[128,10240]{1,0:T(8,128)(2,1)}, f32[8,10240]{1,0:T(8,128)S(1)}, f32[8,10240]{1,0:T(8,128)S(1)}, f32[128,128]{1,0:T(8,128)}, f32[8,128]{1,0:T(8,128)S(1)}) custom-call(bf16[128,10240]{1,0:T(8,128)(2,1)} %get-tuple-element.26.refs_0_.refs_1_.refs_2_, bf16[128,10240]{1,0:T(8,128)(2,1)} %get-tuple-element.26.refs_0_.refs_1_.refs_2_, ...), custom_call_target="tpu_custom_call" | custom-call | tf_op jit(solution)/shard_map/back/pallas_call | solution.py:386
  305.2 0.1 reshape_squeeze.17
  305.3 0.1 reshape_squeeze.18
  305.4 0.1 concatenate.22
  305.6 1.3 collective-permute-start.1
  306.9 0.1 maximum_maximum_fusion
  307.0 1.1 all_to_all.32
  308.1 4.8 %all-to-all-start.5 = ((f32[32,1,2560]{2,1,0:T(1,128)}), f32[32,1,2560]{2,1,0:T(1,128)S(1)}, u32[]{:S(2)}, u32[]{:S(2)}) async-start(f32[32,1,2560]{2,1,0:T(1,128)} %all_to_all.32), calls=%async_computation.5 | async-start | bytes 655360 | tf_op jit(solution)/shard_map/all_to_all | solution.py:435
  312.9 0.3 convert_bitcast_fusion.2
  313.2 0.1 pad_maximum_fusion
  313.4 2.1 dynamic_update_slice.4
  315.5 9.4 %all-to-all-done.5 = f32[32,1,2560]{2,1,0:T(1,128)S(1)} async-done(((f32[32,1,2560]{2,1,0:T(1,128)}), f32[32,1,2560]{2,1,0:T(1,128)S(1)}, u32[]{:S(2)}, u32[]{:S(2)}) %all-to-all-start.5) | async-done | bytes 327712 | tf_op jit(solution)/shard_map/all_to_all | solution.py:435
  324.9 0.2 reduce_sum.32
  325.1 30.5 %all-gather = f32[8,1,2560]{2,1,0:T(1,128)S(1)} all-gather(f32[1,1,2560]{2,1,0:T(1,128)S(1)} %reshape.152), channel_id=1, replica_groups=mesh['ctx'=8,'fsdp'=4] {'ctx'}, dimensions={0}, use_global_device_ids=true | all-gather | bytes 92160 | tf_op jit(solution)/shard_map/all_gather | solution.py:437
  355.6 0.6 slice_reduce_fusion.3
  356.3 0.6 slice.156
  356.9 0.6 fusion.4
  357.5 0.6 copy.25
  (30 shorter events, 0.2 us)
Async XLA Ops:
  1.6 20.4 %collective-permute-start = (bf16[3,10240]{1,0:T(4,128)(2,1)S(1)}, bf16[3,10240]{1,0:T(4,128)(2,1)S(1)}, u32[]{:S(2)}, u32[]{:S(2)}) collective-permute-start(bf16[3,10240]{1,0:T(4,128)(2,1)S(1)} %slice_bitcast_fusion), channel_id=1, source_target_pairs={{0,4},{4,8},{8,12},{12,16},{16,20},{20,24},{24,28},{1,5},{5,9},{9,... | collective-permute-start | bytes 184328 | tf_op jit(solution)/shard_map/ppermute | solution.py:286
  16.9 23.5 %all-to-all-start.1 = ((f32[8,1,16]{2,1,0:T(1,128)}), f32[8,1,16]{2,1,0:T(1,128)S(1)}, u32[]{:S(2)}, u32[]{:S(2)}) async-start(f32[8,1,16]{2,1,0:T(1,128)} %bitcast.3), calls=%async_computation.1 | async-start | bytes 8192 | tf_op jit(solution)/shard_map/all_to_all | solution.py:303
  22.0 0.8 copy-start.9
  37.7 1.3 copy-start.4
  39.1 1.3 copy-start.8
  40.4 54.2 %all-to-all-start = ((bf16[8,128,1024]{2,1,0:T(8,128)(2,1)}), bf16[8,128,1024]{2,1,0:T(8,128)(2,1)S(1)}, u32[]{:S(2)}, u32[]{:S(2)}) async-start(bf16[8,128,1024]{2,1,0:T(8,128)(2,1)} %copy-done.8), calls=%async_computation | async-start | bytes 4194304 | tf_op jit(solution)/shard_map/all_to_all | solution.py:345
  95.4 1.3 copy-start.3
  96.7 52.1 %all-to-all-start.2 = ((bf16[8,128,1024]{2,1,0:T(8,128)(2,1)}), bf16[8,128,1024]{2,1,0:T(8,128)(2,1)S(1)}, u32[]{:S(2)}, u32[]{:S(2)}) async-start(bf16[8,128,1024]{2,1,0:T(8,128)(2,1)} %copy-done.3), calls=%async_computation.2 | async-start | bytes 4194304 | tf_op jit(solution)/shard_map/all_to_all | solution.py:345
  148.7 1.3 copy-start
  165.3 1.4 copy-start.6
  166.6 1.4 copy-start.7
  220.8 1.4 copy-start.2
  222.2 51.8 %copy-start.1 = (bf16[8,128,1024]{2,1,0:T(8,128)(2,1)S(1)}, bf16[8,128,1024]{2,1,0:T(8,128)(2,1)}, u32[]{:S(2)}) copy-start(bf16[8,128,1024]{2,1,0:T(8,128)(2,1)} %copy-done) | copy-start | bytes 6291460
  222.2 51.8 %copy-start.10 = (bf16[1,128,128]{2,1,0:T(8,128)(2,1)S(1)}, bf16[1,128,128]{2,1,0:T(8,128)(2,1)}, u32[]{:S(2)}) copy-start(bf16[1,128,128]{2,1,0:T(8,128)(2,1)} %param.11) | copy-start | bytes 98308
  222.2 51.8 %all-to-all-start.4 = ((bf16[8,128,1024]{2,1,0:T(8,128)(2,1)}), bf16[8,128,1024]{2,1,0:T(8,128)(2,1)}, u32[]{:S(2)}, u32[]{:S(2)}) async-start(bf16[8,128,1024]{2,1,0:T(8,128)(2,1)} %copy-done.2), calls=%async_computation.4 | async-start | bytes 4194304 | tf_op jit(solution)/shard_map/all_to_all | solution.py:345
  274.0 1.6 copy-start.5
  305.6 7.3 %collective-permute-start.1 = (f32[3,10240]{1,0:T(4,128)S(1)}, f32[3,10240]{1,0:T(4,128)S(1)}, u32[]{:S(2)}, u32[]{:S(2)}) collective-permute-start(f32[3,10240]{1,0:T(4,128)S(1)} %slice.118), channel_id=1, source_target_pairs={{4,0},{8,4},{12,8},{16,12},{20,16},{24,20},{28,24},{5,1},{9,5},{13... | collective-permute-start | bytes 368648 | tf_op jit(solution)/shard_map/ppermute | solution.py:418
  308.1 16.8 %all-to-all-start.5 = ((f32[32,1,2560]{2,1,0:T(1,128)}), f32[32,1,2560]{2,1,0:T(1,128)S(1)}, u32[]{:S(2)}, u32[]{:S(2)}) async-start(f32[32,1,2560]{2,1,0:T(1,128)} %all_to_all.32), calls=%async_computation.5 | async-start | bytes 655360 | tf_op jit(solution)/shard_map/all_to_all | solution.py:435
where the time goes:
time: 359 us; the launch traced here: 358 us
  waiting for transfers between devices  152 us (42%)
  blocking collectives  88.7 us (25%)
  Pallas kernels  61.4 us (17%)
  starting transfers between devices  30 us (8%)
  local copies, waits for them, and re-layouts  21.7 us (6%)
    all_to_all x3, waiting for transfers between devices, swap(): return lax.all_to_all(states, 'ctx', 0, 0, tiled=True)  143 us
    all_to_all x1, blocking collectives, swap(): return lax.all_to_all(states, 'ctx', 0, 0, tiled=True)  52 us
    all_gather x1, blocking collectives, body(): mine = lax.all_gather(summed, 'ctx', axis=0, tiled=True).reshape(8, c_loc)  30.5 us
    pallas_call x1, Pallas kernels, body(): pl.pallas_call(lambda *refs: back_kernel(per_group, *refs), out_shape=(ja...  29.6 us
    pallas_call x1, Pallas kernels, body(): pl.pallas_call(lambda *refs: middle_kernel(per_group, *refs), out_shape=(...  15.2 us
    pallas_call x1, Pallas kernels, body(): pl.pallas_call(lambda *refs: front_kernel(per_group, *refs), out_shape=(j...  15 us
    all_to_all x3, starting transfers between devices, swap(): return lax.all_to_all(states, 'ctx', 0, 0, tiled=True)  14.1 us
    unnamed x27, local copies, waits for them, and re-layouts  12.5 us
  transfers between devices with their start and end apart: 7, of which 4 were waited for; matrix products, arithmetic and copies ran while one was open for 2% of the time, Pallas kernels for 4%

commit v1 on v0

--- a/solution.py
+++ b/solution.py
@@ -14,6 +14,7 @@
 EPSILON = 1e-05
 HALO = KERNEL - 1
 PAD = 8
+CHUNKS = 4
 F32 = jnp.float32
 BF16 = jnp.bfloat16
 HIGHEST = lax.Precision.HIGHEST
@@ -79,8 +80,20 @@
     return pre
 
 
-def front_kernel(per_group, x_ref, halo_ref, w_ref, dt_ref, sb_ref, dl_ref,
-                 mixed_ref, vp_ref, ut_ref, ec_ref, ei_ref, et_ref, xs, ks):
+def split_halves(state, mine, own_ref, send_ref):
+    half = state.shape[0] // 2
+    low, high = state[:half].astype(BF16), state[half:].astype(BF16)
+    own_ref[0] = jnp.where(mine == 0, low, high)
+    send_ref[0] = jnp.where(mine == 0, high, low)
+
+
+def join_halves(own_ref, other_ref, mine):
+    own, other = own_ref[0], other_ref[0]
+    return jnp.concatenate([jnp.where(mine == 0, own, other), jnp.where(mine == 0, other, own)], axis=0)
+
+
+def front_kernel(per_group, side_ref, x_ref, halo_ref, w_ref, dt_ref, sb_ref, dl_ref,
+                 mixed_ref, vp_ref, own_ref, send_ref, ec_ref, ei_ref, et_ref, xs, ks):
     j = pl.program_id(0)
     length = x_ref.shape[0]
 
@@ -111,25 +124,17 @@
         et = spread_heads(ec_ref[length - 8 : length, :], g, per_group)[7:8, :]
         et_ref[...] = et
         ut = mm(ks[g].astype(F32).T.astype(BF16), vp) * et
-        reps, _, part = ut_ref.shape
-        for r in range(reps):
-            ut_ref[r] = ut[:, r * part : (r + 1) * part].astype(BF16)
-
-
-def join_parts(ref):
-    if ref.shape[0] == 1:
-        return ref[0]
-    return jnp.concatenate([ref[r] for r in range(ref.shape[0])], axis=1)
-
-
-def middle_kernel(per_group, v_ref, k_ref, q_ref, vp_ref, st_ref, ec_ref, gate_ref, og_ref, gain_ref, skip_ref,
-                  dy_ref, dyp_ref, gg_ref, gt_ref, rows_ref, a1_ref):
+        split_halves(ut, side_ref[0], own_ref, send_ref)
+
+
+def middle_kernel(per_group, side_ref, v_ref, k_ref, q_ref, vp_ref, so_ref, st_ref, ec_ref, gate_ref, og_ref, gain_ref, skip_ref,
+                  dy_ref, dyp_ref, gg_ref, own_ref, send_ref, rows_ref, a1_ref):
     g = pl.program_id(0)
     length, width = v_ref.shape
     heads = ec_ref.shape[1]
     q = q_ref[...]
     z = jnp.where(lower_mask(length), mm_nt(q, k_ref[...]), 0.0).astype(BF16)
-    yn = mm(jnp.concatenate([z, q], axis=1), jnp.concatenate([vp_ref[...], join_parts(st_ref)], axis=0))
+    yn = mm(jnp.concatenate([z, q], axis=1), jnp.concatenate([vp_ref[...], join_halves(so_ref, st_ref, side_ref[0])], axis=0))
     ecx = spread_heads(ec_ref[...], g, per_group)
     v = v_ref[...].astype(F32)
     y = (ecx * yn + skip_ref[...] * v).astype(BF16).astype(F32)
@@ -149,9 +154,7 @@
     dyp = (ecx * dy).astype(BF16)
     dyp_ref[...] = dyp
     gt = mm(q.astype(F32).T.astype(BF16), dyp)
-    reps, _, part = gt_ref.shape
-    for r in range(reps):
-        gt_ref[r] = gt[:, r * part : (r + 1) * part].astype(BF16)
+    split_halves(gt, side_ref[1], own_ref, send_ref)
     rows_ref[...] = jnp.zeros(rows_ref.shape, F32)
     rows_ref[0:1, :] = jnp.sum(og * gated * scale, axis=0, keepdims=True)
     rows_ref[1:2, :] = jnp.sum(dy * v, axis=0, keepdims=True)
@@ -163,7 +166,7 @@
     a1_ref[...] += sum_heads(dyp.astype(F32) * yn, g, per_group, heads)
 
 
-def back_kernel(per_group, v_ref, k_ref, q_ref, vp_ref, st_ref, en_ref, dy_ref, dyp_ref, x_ref, halo_ref, w_ref,
+def back_kernel(per_group, side_ref, v_ref, k_ref, q_ref, vp_ref, so_ref, st_ref, eo_ref, en_ref, dy_ref, dyp_ref, x_ref, halo_ref, w_ref,
                 skip_ref, et_ref, ei_ref, a1_ref, dt_ref, sb_ref, dl_ref,
                 gx_ref, edge_ref, wr_ref, gdt_ref, hs_ref, xs, gs, gm, dkq, a2, last):
     j = pl.program_id(0)
@@ -182,8 +185,8 @@
         q = q_ref[...]
         vp = vp_ref[...]
         dyp = dyp_ref[...]
-        st = join_parts(st_ref)
-        en = (et_ref[...] * join_parts(en_ref).astype(F32)).astype(BF16)
+        st = join_halves(so_ref, st_ref, side_ref[0])
+        en = (et_ref[...] * join_halves(eo_ref, en_ref, side_ref[1]).astype(F32)).astype(BF16)
         low = lower_mask(length)
         zt = jnp.where(upper_mask(length), mm_nt(k, q), 0.0).astype(BF16)
         dvp = mm(jnp.concatenate([zt, k], axis=1), jnp.concatenate([dyp, en], axis=0))
@@ -235,33 +238,94 @@
         hs_ref[1:2, :] = jnp.sum(gdt, axis=0, keepdims=True)
 
 
-def scan_kernel(backward, u_ref, d_ref, o_ref):
-    count = u_ref.shape[0]
-    acc = jnp.zeros(u_ref.shape[1:], F32)
-    order = range(count - 1, -1, -1) if backward else range(count)
-    for i in order:
-        o_ref[i] = acc.astype(BF16)
-        acc = d_ref[i : i + 1, :] * acc + u_ref[i].astype(F32)
-
-
 PARAMS = pltpu.CompilerParams(vmem_limit_bytes=48 * 1024 * 1024)
 
 
-def scan_states(states, decay, backward):
-    count, rows, wide = states.shape
-    tile = 32
+def grid_call(kernel, name, steps, in_specs, out_specs, out_shape, scratch=()):
     return pl.pallas_call(
-        lambda *refs: scan_kernel(backward, *refs),
-        out_shape=jax.ShapeDtypeStruct(states.shape, BF16),
-        grid=(rows // tile,),
-        in_specs=[
-            pl.BlockSpec((count, tile, wide), lambda i: (0, i, 0)),
-            pl.BlockSpec((count, wide), lambda i: (0, 0)),
-        ],
-        out_specs=pl.BlockSpec((count, tile, wide), lambda i: (0, i, 0)),
+        kernel,
+        out_shape=out_shape,
+        grid_spec=pltpu.PrefetchScalarGridSpec(
+            num_scalar_prefetch=1, grid=(steps,), in_specs=in_specs, out_specs=out_specs, scratch_shapes=scratch),
         compiler_params=PARAMS,
-        name="scan_back" if backward else "scan_front",
-    )(states, decay)
+        name=name,
+    )
+
+
+def hop_kernel(has_carry, at_ref, own_ref, got_ref, mine_ref, pair_ref, *refs):
+    if has_carry:
+        carry_ref, next_ref, give_ref, keep_ref = refs
+        carry = carry_ref[...].astype(F32)
+    else:
+        next_ref, give_ref, keep_ref = refs
+        carry = jnp.zeros(got_ref.shape, F32)
+    first = at_ref[1] == 0
+    own, got = own_ref[0].astype(F32), got_ref[...].astype(F32)
+    mine, pair = mine_ref[...], pair_ref[...]
+    inner = jnp.where(first, mine, pair) * carry + jnp.where(first, own, got)
+    next_ref[...] = (jnp.where(first, pair, mine) * inner + jnp.where(first, got, own)).astype(BF16)
+    give_ref[...] = jnp.where(first, inner, carry).astype(BF16)
+    keep_ref[...] = jnp.where(first, carry, inner).astype(BF16)
+
+
+def in_hbm(value):
+    return pltpu.with_memory_space_constraint(value, pltpu.HBM)
+
+
+def chain_states(own, send, rate, pair_rate, flip):
+    count, rows, lanes = own.shape
+    ranks = lax.axis_size("ctx")
+    depth = ranks // 2
+    rank = lax.axis_index("ctx")
+    rank = ranks - 1 - rank if flip else rank
+    side, place = rank % 2, rank // 2
+    steps = count + depth - 1
+    tile = lanes // 2
+
+    def physical(r):
+        return ranks - 1 - r if flip else r
+
+    def live(s):
+        return [z for z in range(depth) if 0 <= s - z < count]
+
+    def swap(value, s):
+        pairs = [(physical(2 * z + p), physical(2 * z + 1 - p)) for z in live(s) for p in range(2)]
+        return lax.ppermute(value, "ctx", pairs)
+
+    def up(value, s):
+        pairs = [(physical(2 * z + p), physical(2 * z + 2 + p)) for z in live(s) if z + 1 < depth for p in range(2)]
+        return lax.ppermute(value, "ctx", pairs) if pairs else None
+
+    got = [
+        swap(lax.dynamic_index_in_dim(send, jnp.clip(s - place, 0, count - 1), 0, keepdims=False), s)
+        for s in range(steps)
+    ]
+    per = lanes // tile
+    flat = pl.BlockSpec((rows, tile), lambda i, at: (0, i))
+    line = pl.BlockSpec((1, tile), lambda i, at: (0, at[0] * per + i))
+    read = pl.BlockSpec((1, rows, tile), lambda i, at: (at[0], 0, i))
+    chunk_shape = jax.ShapeDtypeStruct((rows, lanes), BF16)
+    keeps, backs = [], []
+    carry = None
+    for s in range(steps):
+        has_carry = s > 0
+        at = jnp.stack([jnp.clip(s - place, 0, count - 1), side]).astype(jnp.int32)
+        after, give, keep = pl.pallas_call(
+            lambda *refs, has_carry=has_carry: hop_kernel(has_carry, *refs),
+            out_shape=(chunk_shape,) * 3,
+            grid_spec=pltpu.PrefetchScalarGridSpec(
+                num_scalar_prefetch=1,
+                grid=(per,),
+                in_specs=[read, flat, line, line] + [flat] * has_carry,
+                out_specs=[flat] * 3,
+            ),
+            compiler_params=PARAMS,
+            name="hop",
+        )(at, in_hbm(own), in_hbm(got[s]), rate, pair_rate, *([in_hbm(carry)] if has_carry else []))
+        keeps.append(keep)
+        carry = up(after, s)
+        backs.append(swap(give, s))
+    return jnp.stack(keeps), jnp.stack(backs)
 
 
 def body(proj_xbc, proj_dt, proj_gate, out_grad, conv_weight, conv_bias, decay_log, step_bias, skip_gain, norm_gain):
@@ -273,9 +337,11 @@
     shards = lax.axis_size("fsdp")
     per_group = heads // GROUPS
     width = per_group * HEAD_DIM
-    reps = ranks // GROUPS
-    wide = inner // ranks
-    own_heads = heads // ranks
+    side = lax.axis_index("ctx") % 2
+    place = lax.axis_index("ctx") // 2
+    sides = jnp.stack([side, 1 - side, place, ranks // 2 - 1 - place]).astype(jnp.int32)
+    part = inner // CHUNKS
+    per = part // width
     c_loc, g_loc, h_loc = channels // shards, inner // shards, heads // shards
     spare = c_loc - g_loc - 3 * h_loc
     groups = GROUPS
@@ -299,92 +365,86 @@
     skip = extra[:, g_loc + 2 * h_loc : g_loc + 3 * h_loc].reshape(1, heads)
     skip_x = jnp.repeat(skip, HEAD_DIM, axis=1)
 
-    rate = jnp.exp(-jnp.exp(decay[0]) * jnp.sum(jax.nn.softplus(dt.astype(F32) + step_b), axis=0))
-    rates = lax.all_to_all(rate.reshape(ranks, own_heads), "ctx", 0, 0, tiled=True)
-    rates_x = jnp.repeat(rates, HEAD_DIM, axis=1)
-
     def col(j):
         return jnp.where(j < 2, groups + j, j - 2)
 
     def grp(j):
         return jnp.maximum(j - 2, 0)
 
-    full_head = pl.BlockSpec((length, heads), lambda j: (0, 0))
-    row_head = pl.BlockSpec((1, heads), lambda j: (0, 0))
-    state_shape = jax.ShapeDtypeStruct((ranks, STATE, wide), BF16)
-    mixed, vp, ut, ec, ei, et = pl.pallas_call(
-        lambda *refs: front_kernel(per_group, *refs),
+    full_head = pl.BlockSpec((length, heads), lambda j, at: (0, 0))
+    row_head = pl.BlockSpec((1, heads), lambda j, at: (0, 0))
+    state_shape = jax.ShapeDtypeStruct((CHUNKS, STATE // 2, part), BF16)
+    mixed, vp, own, send, ec, ei, et = grid_call(
+        lambda *refs: front_kernel(per_group, *refs), "front", blocks,
         out_shape=(
             jax.ShapeDtypeStruct((length, channels), BF16),
             jax.ShapeDtypeStruct((length, inner), BF16),
+            state_shape,
             state_shape,
             jax.ShapeDtypeStruct((length, heads), F32),
             jax.ShapeDtypeStruct((length, heads), F32),
             jax.ShapeDtypeStruct((1, inner), F32),
         ),
-        grid=(blocks,),
         in_specs=[
-            pl.BlockSpec((length, width), lambda j: (0, col(j))),
-            pl.BlockSpec((HALO, width), lambda j: (0, col(j))),
-            pl.BlockSpec((8, width), lambda j: (0, col(j))),
+            pl.BlockSpec((length, width), lambda j, at: (0, col(j))),
+            pl.BlockSpec((HALO, width), lambda j, at: (0, col(j))),
+            pl.BlockSpec((8, width), lambda j, at: (0, col(j))),
             full_head, row_head, row_head,
         ],
         out_specs=(
-            pl.BlockSpec((length, width), lambda j: (0, col(j))),
-            pl.BlockSpec((length, width), lambda j: (0, grp(j))),
-            pl.BlockSpec((reps, STATE, wide), lambda j: (grp(j), 0, 0)),
+            pl.BlockSpec((length, width), lambda j, at: (0, col(j))),
+            pl.BlockSpec((length, width), lambda j, at: (0, grp(j))),
+            pl.BlockSpec((1, STATE // 2, width), lambda j, at: (grp(j) // per, 0, lax.rem(grp(j), per))),
+            pl.BlockSpec((1, STATE // 2, width), lambda j, at: (grp(j) // per, 0, lax.rem(grp(j), per))),
             full_head, full_head,
-            pl.BlockSpec((1, width), lambda j: (0, grp(j))),
+            pl.BlockSpec((1, width), lambda j, at: (0, grp(j))),
         ),
-        scratch_shapes=[pltpu.VMEM((PAD + length, width), F32), pltpu.VMEM((GROUPS, length, STATE), BF16)],
-        compiler_params=PARAMS,
-        name="front",
-    )(x, halo, full, dt, step_b, decay)
-
-    def swap(states):
-        return lax.all_to_all(states, "ctx", 0, 0, tiled=True)
-
-    starts = swap(scan_states(swap(ut), rates_x, False))
-
-    wide_spec = pl.BlockSpec((length, width), lambda g: (0, g))
-    line_spec = pl.BlockSpec((1, width), lambda g: (0, g))
+        scratch=[pltpu.VMEM((PAD + length, width), F32), pltpu.VMEM((GROUPS, length, STATE), BF16)],
+    )(sides, x, halo, full, dt, step_b, decay)
+
+    pair_et = lax.ppermute(et, "ctx", [(i, i ^ 1) for i in range(ranks)])
+    starts = chain_states(own, send, et, pair_et, False)
+
+    wide_spec = pl.BlockSpec((length, width), lambda g, at: (0, g))
+    line_spec = pl.BlockSpec((1, width), lambda g, at: (0, g))
     k_at = inner // STATE
     q_at = k_at + GROUPS
-    state_spec = pl.BlockSpec((reps, STATE, wide), lambda g: (g, 0, 0))
-    dy, dyp, grad_gate, gt, rows, a1 = pl.pallas_call(
-        lambda *refs: middle_kernel(per_group, *refs),
+    half = (1, STATE // 2, width)
+    state_spec = pl.BlockSpec(half, lambda g, at: (at[2] + g // per, 0, lax.rem(g, per)))
+    grad_spec = pl.BlockSpec(half, lambda g, at: (g // per, 0, lax.rem(g, per)))
+    dy, dyp, grad_gate, own, send, sums, a1 = grid_call(
+        lambda *refs: middle_kernel(per_group, *refs), "middle", GROUPS,
         out_shape=(
             jax.ShapeDtypeStruct((length, inner), BF16),
             jax.ShapeDtypeStruct((length, inner), BF16),
             jax.ShapeDtypeStruct((length, inner), BF16),
             state_shape,
+            state_shape,
             jax.ShapeDtypeStruct((8, inner), F32),
             jax.ShapeDtypeStruct((length, heads), F32),
         ),
-        grid=(GROUPS,),
         in_specs=[
             wide_spec,
-            pl.BlockSpec((length, STATE), lambda g: (0, k_at + g)),
-            pl.BlockSpec((length, STATE), lambda g: (0, q_at + g)),
-            wide_spec, state_spec, full_head, wide_spec, wide_spec, line_spec, line_spec,
+            pl.BlockSpec((length, STATE), lambda g, at: (0, k_at + g)),
+            pl.BlockSpec((length, STATE), lambda g, at: (0, q_at + g)),
+            wide_spec, state_spec, state_spec, full_head, wide_spec, wide_spec, line_spec, line_spec,
         ],
-        out_specs=(wide_spec, wide_spec, wide_spec, state_spec, pl.BlockSpec((8, width), lambda g: (0, g)), full_head),
-        compiler_params=PARAMS,
-        name="middle",
-    )(mixed, mixed, mixed, vp, starts, ec, gate, og, gain, skip_x)
-
-    ends = swap(scan_states(swap(gt), rates_x, True))
+        out_specs=(wide_spec, wide_spec, wide_spec, grad_spec, grad_spec, pl.BlockSpec((8, width), lambda g, at: (0, g)), full_head),
+    )(sides, mixed, mixed, mixed, vp, *starts, ec, gate, og, gain, skip_x)
+
+    ends = chain_states(own, send, et, pair_et, True)
 
     def cap(j):
         return jnp.minimum(j, GROUPS - 1)
 
-    wide_cap = pl.BlockSpec((length, width), lambda j: (0, cap(j)))
-    line_cap = pl.BlockSpec((1, width), lambda j: (0, cap(j)))
-    state_cap = pl.BlockSpec((reps, STATE, wide), lambda j: (cap(j), 0, 0))
-    eight = pl.BlockSpec((8, width), lambda j: (0, j))
-    wide_all = pl.BlockSpec((length, width), lambda j: (0, j))
-    gx, edge, wr, grad_dt, hs = pl.pallas_call(
-        lambda *refs: back_kernel(per_group, *refs),
+    wide_cap = pl.BlockSpec((length, width), lambda j, at: (0, cap(j)))
+    line_cap = pl.BlockSpec((1, width), lambda j, at: (0, cap(j)))
+    start_cap = pl.BlockSpec(half, lambda j, at: (at[2] + cap(j) // per, 0, lax.rem(cap(j), per)))
+    end_cap = pl.BlockSpec(half, lambda j, at: (at[3] + cap(j) // per, 0, lax.rem(cap(j), per)))
+    eight = pl.BlockSpec((8, width), lambda j, at: (0, j))
+    wide_all = pl.BlockSpec((length, width), lambda j, at: (0, j))
+    gx, edge, wr, grad_dt, hs = grid_call(
+        lambda *refs: back_kernel(per_group, *refs), "back", blocks,
         out_shape=(
             jax.ShapeDtypeStruct((length, channels), BF16),
             jax.ShapeDtypeStruct((8, channels), F32),
@@ -392,18 +452,17 @@
             jax.ShapeDtypeStruct((length, heads), F32),
             jax.ShapeDtypeStruct((8, heads), F32),
         ),
-        grid=(blocks,),
         in_specs=[
             wide_cap,
-            pl.BlockSpec((length, STATE), lambda j: (0, k_at + cap(j))),
-            pl.BlockSpec((length, STATE), lambda j: (0, q_at + cap(j))),
-            wide_cap, state_cap, state_cap, wide_cap, wide_cap,
+            pl.BlockSpec((length, STATE), lambda j, at: (0, k_at + cap(j))),
+            pl.BlockSpec((length, STATE), lambda j, at: (0, q_at + cap(j))),
+            wide_cap, start_cap, start_cap, end_cap, end_cap, wide_cap, wide_cap,
             wide_all,
-            pl.BlockSpec((HALO, width), lambda j: (0, j)),
+            pl.BlockSpec((HALO, width), lambda j, at: (0, j)),
             eight, line_cap, line_cap, full_head, full_head, full_head, row_head, row_head,
         ],
-        out_specs=(wide_all, eight, eight, full_head, pl.BlockSpec((8, heads), lambda j: (0, 0))),
-        scratch_shapes=[
+        out_specs=(wide_all, eight, eight, full_head, pl.BlockSpec((8, heads), lambda j, at: (0, 0))),
+        scratch=[
             pltpu.VMEM((PAD + length, width), F32),
             pltpu.VMEM((PAD + length, width), F32),
             pltpu.VMEM((length, width), F32),
@@ -411,9 +470,7 @@
             pltpu.VMEM((length, heads), F32),
             pltpu.VMEM((8, heads), F32),
         ],
-        compiler_params=PARAMS,
-        name="back",
-    )(mixed, mixed, mixed, vp, starts, ends, dy, dyp, x, halo, full, skip_x, et, ei, a1, dt, step_b, decay)
+    )(sides, mixed, mixed, mixed, vp, *starts, *ends, dy, dyp, x, halo, full, skip_x, et, ei, a1, dt, step_b, decay)
 
     next_gp = lax.ppermute(edge[:HALO], "ctx", behind)
     fixed = []
@@ -424,9 +481,9 @@
         fixed.append(row)
     grad_xbc = lax.dynamic_update_slice(gx, jnp.stack(fixed).astype(BF16), (length - HALO, 0))
 
-    skip_grad = jnp.sum(rows[1].reshape(heads, HEAD_DIM), axis=1)
+    skip_grad = jnp.sum(sums[1].reshape(heads, HEAD_DIM), axis=1)
     extra_row = pack_row(
-        rows[0].reshape(shards, g_loc), hs[0].reshape(shards, h_loc), hs[1].reshape(shards, h_loc),
+        sums[0].reshape(shards, g_loc), hs[0].reshape(shards, h_loc), hs[1].reshape(shards, h_loc),
         skip_grad.reshape(shards, h_loc)).reshape(1, channels)
     parts = jnp.concatenate([wr[: KERNEL + 1], extra_row, jnp.zeros((8 - KERNEL - 2, channels), F32)], axis=0)
     split = ranks // 8
@@ -434,7 +491,8 @@
     parts = parts.reshape(8, shards, split, piece).transpose(0, 2, 1, 3).reshape(ranks * shards, piece)
     summed = jnp.sum(lax.all_to_all(parts, ("ctx", "fsdp"), 0, 0, tiled=True), axis=0)
     summed = summed * (1.0 / math.sqrt(length * ranks * shards))
-    mine = lax.all_gather(summed, "ctx", axis=0, tiled=True).reshape(8, c_loc)
+    copies = jnp.broadcast_to(summed[None], (ranks, piece))
+    mine = lax.all_to_all(copies, "ctx", 0, 0, tiled=True).reshape(8, c_loc)
     tail = mine[KERNEL + 1]
     return (
         grad_xbc[None],

time: 359 us -> 295 us (0.82)
  blocking collectives: 88.7 us -> 6.12 us
  waiting for transfers between devices: 152 us -> 92.1 us
  starting transfers between devices: 30 us -> 81.4 us
  local copies, waits for them, and re-layouts: 21.7 us -> 36.9 us
  other arithmetic: 3.22 us -> 8.29 us
  Pallas kernels: 61.4 us -> 66.4 us
    all_to_all x4 -> x1, waiting for transfers between devices: 143 us -> 4.69 us  [body(): mine = lax.all_to_all(copies, 'ctx', 0, 0, tiled=True).reshape(8, c_loc)]
    ppermute x0 -> x41, waiting for transfers between devices: none -> 75.7 us  [the longest x12 60.5 us: up(): return lax.ppermute(value, 'ctx', pairs) if pairs else None]
    ppermute x0 -> x41, starting transfers between devices: none -> 68.1 us  [the longest x28 49.5 us: swap(): return lax.ppermute(value, 'ctx', pairs)]
    all_to_all x1 -> x0, blocking collectives: 52 us -> none  [swap(): return lax.all_to_all(states, 'ctx', 0, 0, tiled=True)]
    all_gather x1 -> x0, blocking collectives: 30.5 us -> none  [body(): mine = lax.all_gather(summed, 'ctx', axis=0, tiled=True).reshape(8, c_loc)]
    pallas_call x0 -> x12, local copies, waits for them, and re-layouts: none -> 16.8 us  [chain_states(): pl.pallas_call(lambda *refs, has_carry=has_carry: hop_kernel(has_carry, *...]
    all_to_all x4 -> x1, starting transfers between devices: 19 us -> 3.36 us  [body(): mine = lax.all_to_all(copies, 'ctx', 0, 0, tiled=True).reshape(8, c_loc)]
    another operation x0 -> x15, other arithmetic: none -> 6.57 us  [the longest x14 6.5 us: chain_states(): at = jnp.stack([jnp.clip(s - place, 0, count - 1), side]).astype(jnp.int32)]
  transfers between devices with their start and end apart: 7 -> 45, of which waited for: 4 -> 14; matrix products, arithmetic and copies ran while one was open for 2% -> 10% of each run, Pallas kernels for 4% -> 1%
where the time goes in v1:
time: 295 us; the launch traced here: 293 us
  waiting for transfers between devices  92.1 us (31%)
  starting transfers between devices  81.4 us (28%)
  Pallas kernels  66.4 us (23%)
  local copies, waits for them, and re-layouts  36.9 us (13%)
  other arithmetic  8.29 us (3%)
  blocking collectives  6.12 us (2%)
    ppermute x12, waiting for transfers between devices, up(): return lax.ppermute(value, 'ctx', pairs) if pairs else None  60.5 us
    ppermute x28, starting transfers between devices, swap(): return lax.ppermute(value, 'ctx', pairs)  49.5 us
    pallas_call x1, Pallas kernels, body(): grid_call(lambda *refs: back_kernel(per_group, *refs), 'back', blocks, ou...  31.1 us
    ppermute x12, starting transfers between devices, up(): return lax.ppermute(value, 'ctx', pairs) if pairs else None  18.1 us
    pallas_call x12, local copies, waits for them, and re-layouts, chain_states(): pl.pallas_call(lambda *refs, has_carry=has_carry: hop_kernel(has_carry, *...  16.8 us
    pallas_call x1, Pallas kernels, body(): grid_call(lambda *refs: middle_kernel(per_group, *refs), 'middle', GROUPS...  15.9 us
    pallas_call x1, Pallas kernels, body(): grid_call(lambda *refs: front_kernel(per_group, *refs), 'front', blocks,...  15.8 us
    ppermute x28, waiting for transfers between devices, swap(): return lax.ppermute(value, 'ctx', pairs)  15.2 us
  transfers between devices with their start and end apart: 45, of which 14 were waited for; matrix products, arithmetic and copies ran while one was open for 10% of the time, Pallas kernels for 1%

profile of v1, /device:TPU:0, one launch (start us, length us, event | category | flops | bytes accessed | tf_op | source)
XLA Modules:
  0.0 293.1 jit_solution(1552127606993056559)
XLA Ops:
  1.6 4.8 %collective-permute-start = (bf16[3,10240]{1,0:T(4,128)(2,1)S(1)}, bf16[3,10240]{1,0:T(4,128)(2,1)S(1)}, u32[]{:S(2)}, u32[]{:S(2)}) collective-permute-start(bf16[3,10240]{1,0:T(4,128)(2,1)S(1)} %slice_bitcast_fusion), channel_id=1, source_target_pairs={{0,4},{4,8},{8,12},{12,16},{16,20},{20,24},{24,28},{1,5},{5,9},{9,... | collective-permute-start | bytes 184328 | tf_op jit(solution)/shard_map/ppermute | solution.py:352
  8.9 6.1 %all_gather.3.refs_3_.refs_13_ = f32[8,10240]{1,0:T(8,128)S(1)} all-gather(f32[8,2560]{1,0:T(8,128)S(1)} %maximum_maximum_fusion.1), channel_id=1, replica_groups=mesh['ctx'=8,'fsdp'=4] {'fsdp'}, dimensions={1}, use_global_device_ids=true | all-gather | bytes 409600 | tf_op jit(solution)/shard_map/all_gather | solution.py:360
  20.8 15.8 %front.1 = (bf16[128,10240]{1,0:T(8,128)(2,1)}, bf16[128,8192]{1,0:T(8,128)(2,1)S(1)}, bf16[4,64,2048]{2,1,0:T(8,128)(2,1)S(1)}, bf16[4,64,2048]{2,1,0:T(8,128)(...) custom-call(s32[4]{0:T(128)S(1)} %pad_add_fusion.refs_0_, ...), custom_call_target="tpu_custom_call" | custom-call | tf_op jit(solution)/shard_map/front/pallas_call | solution.py:377
  36.6 1.2 dynamic-slice_bitcast_fusion.7
  38.7 3.6 %collective-permute-start.1 = (bf16[64,2048]{1,0:T(8,128)(2,1)S(1)}, bf16[64,2048]{1,0:T(8,128)(2,1)S(1)}, u32[]{:S(2)}, u32[]{:S(2)}) collective-permute-start(bf16[64,2048]{1,0:T(8,128)(2,1)S(1)} %get-tuple-element.218), channel_id=1, source_target_pairs={{0,4},{4,0},{1,5},{5,1},{2,6},{6,2},{3,7},{7,3}} | collective-permute-start | bytes 786440 | tf_op jit(solution)/shard_map/ppermute | solution.py:293
  45.0 3.5 %collective-permute-start.3 = (bf16[64,2048]{1,0:T(8,128)(2,1)S(1)}, bf16[64,2048]{1,0:T(8,128)(2,1)S(1)}, u32[]{:S(2)}, u32[]{:S(2)}) collective-permute-start(bf16[64,2048]{1,0:T(8,128)(2,1)S(1)} %get-tuple-element.217), channel_id=1, source_target_pairs={{0,4},{4,0},{8,12},{12,8},{1,5},{5,1},{9,13},{13,9},{2,6},{6,2},{1... | collective-permute-start | bytes 786440 | tf_op jit(solution)/shard_map/ppermute | solution.py:293
  48.4 2.4 collective-permute-start.5
  50.8 1.6 collective-permute-start.7
  53.2 1.8 hop.14
  55.0 1.4 collective-permute-start.4
  56.5 2.9 collective-permute-start.15
  60.1 1.3 collective-permute-done.4
  61.4 1.2 hop.27
  62.6 4.5 %collective-permute-start.6 = (bf16[64,2048]{1,0:T(8,128)(2,1)S(1)}, bf16[64,2048]{1,0:T(8,128)(2,1)S(1)}, u32[]{:S(2)}, u32[]{:S(2)}) collective-permute-start(bf16[64,2048]{1,0:T(8,128)(2,1)S(1)} %get-tuple-element.148), channel_id=1, source_target_pairs={{0,8},{4,12},{8,16},{12,20},{1,9},{5,13},{9,17},{13,21},{2,10},{6,... | collective-permute-start | bytes 786440 | tf_op jit(solution)/shard_map/ppermute | solution.py:297
  67.1 5.4 %collective-permute-done.15 = bf16[64,2048]{1,0:T(8,128)(2,1)S(1)} collective-permute-done((bf16[64,2048]{1,0:T(8,128)(2,1)S(1)}, bf16[64,2048]{1,0:T(8,128)(2,1)S(1)}, u32[]{:S(2)}, u32[]{:S(2)}) %collective-permute-start.15) | collective-permute-done | bytes 262176 | tf_op jit(solution)/shard_map/ppermute | solution.py:293
  72.5 3.4 %collective-permute-start.16 = (bf16[64,2048]{1,0:T(8,128)(2,1)S(1)}, bf16[64,2048]{1,0:T(8,128)(2,1)S(1)}, u32[]{:S(2)}, u32[]{:S(2)}) collective-permute-start(bf16[64,2048]{1,0:T(8,128)(2,1)S(1)} %get-tuple-element.150), channel_id=1, source_target_pairs={{0,4},{4,0},{8,12},{12,8},{1,5},{5,1},{9,13},{13,9},{2,6},{6,2},{1... | collective-permute-start | bytes 786440 | tf_op jit(solution)/shard_map/ppermute | solution.py:293
  76.7 1.2 hop.26
  77.9 1.3 collective-permute-start.8
  79.2 2.9 %collective-permute-done.16 = bf16[64,2048]{1,0:T(8,128)(2,1)S(1)} collective-permute-done((bf16[64,2048]{1,0:T(8,128)(2,1)S(1)}, bf16[64,2048]{1,0:T(8,128)(2,1)S(1)}, u32[]{:S(2)}, u32[]{:S(2)}) %collective-permute-start.16) | collective-permute-done | bytes 262176 | tf_op jit(solution)/shard_map/ppermute | solution.py:293
  82.1 3.4 %collective-permute-start.17 = (bf16[64,2048]{1,0:T(8,128)(2,1)S(1)}, bf16[64,2048]{1,0:T(8,128)(2,1)S(1)}, u32[]{:S(2)}, u32[]{:S(2)}) collective-permute-start(bf16[64,2048]{1,0:T(8,128)(2,1)S(1)} %get-tuple-element.156), channel_id=1, source_target_pairs={{0,4},{4,0},{8,12},{12,8},{16,20},{20,16},{1,5},{5,1},{9,13},{13,9... | collective-permute-start | bytes 786440 | tf_op jit(solution)/shard_map/ppermute | solution.py:293
  86.3 1.2 hop.25
  87.5 2.5 collective-permute-start.10
  90.9 1.5 collective-permute-start.18
  92.4 1.9 collective-permute-done.10
  94.4 1.2 hop.24
  97.3 1.2 hop.23
  99.9 1.7 hop.22
  102.4 1.2 copy-done.4
  103.6 15.9 %middle.1 = (bf16[128,8192]{1,0:T(8,128)(2,1)}, bf16[128,8192]{1,0:T(8,128)(2,1)}, bf16[128,8192]{1,0:T(8,128)(2,1)}, bf16[4,64,2048]{2,1,0:T(8,128)(2,1)S(1)}, ...) custom-call(s32[4]{0:T(128)S(1)} %copy-done.14, ...), custom_call_target="tpu_custom_call" | custom-call | tf_op jit(solution)/shard_map/middle/pallas_call | solution.py:415
  119.5 1.2 copy-done.6
  120.7 1.2 dynamic-slice_bitcast_fusion
  123.8 1.4 collective-permute-start.25
  125.2 1.5 collective-permute-start.27
  127.9 1.8 hop.15
  131.3 2.4 collective-permute-start.29
  133.7 1.2 hop.21
  136.5 3.5 %collective-permute-start.31 = (bf16[64,2048]{1,0:T(8,128)(2,1)S(1)}, bf16[64,2048]{1,0:T(8,128)(2,1)S(1)}, u32[]{:S(2)}, u32[]{:S(2)}) collective-permute-start(bf16[64,2048]{1,0:T(8,128)(2,1)S(1)} %copy-done.28), channel_id=1, source_target_pairs={{12,8},{8,12},{4,0},{0,4},{13,9},{9,13},{5,1},{1,5},{14,10},{10,14... | collective-permute-start | bytes 786440 | tf_op jit(solution)/shard_map/ppermute | solution.py:293
  140.0 2.0 hop.20
  142.0 1.3 collective-permute-start.28
  144.0 2.4 collective-permute-start.33
  146.4 39.8 %collective-permute-done.28 = bf16[64,2048]{1,0:T(8,128)(2,1)S(1)} collective-permute-done((bf16[64,2048]{1,0:T(8,128)(2,1)S(1)}, bf16[64,2048]{1,0:T(8,128)(2,1)S(1)}, u32[]{:S(2)}, u32[]{:S(2)}) %collective-permute-start.28) | collective-permute-done | bytes 262176 | tf_op jit(solution)/shard_map/ppermute | solution.py:297
  186.3 2.0 hop.19
  188.3 1.5 collective-permute-start.30
  190.6 7.8 %collective-permute-done.30 = bf16[64,2048]{1,0:T(8,128)(2,1)S(1)} collective-permute-done((bf16[64,2048]{1,0:T(8,128)(2,1)S(1)}, bf16[64,2048]{1,0:T(8,128)(2,1)S(1)}, u32[]{:S(2)}, u32[]{:S(2)}) %collective-permute-start.30) | collective-permute-done | bytes 262176 | tf_op jit(solution)/shard_map/ppermute | solution.py:297
  198.4 1.2 hop.18
  199.6 1.3 collective-permute-start.32
  200.9 2.6 collective-permute-start.39
  203.6 5.3 %collective-permute-done.32 = bf16[64,2048]{1,0:T(8,128)(2,1)S(1)} collective-permute-done((bf16[64,2048]{1,0:T(8,128)(2,1)S(1)}, bf16[64,2048]{1,0:T(8,128)(2,1)S(1)}, u32[]{:S(2)}, u32[]{:S(2)}) %collective-permute-start.32) | collective-permute-done | bytes 262176 | tf_op jit(solution)/shard_map/ppermute | solution.py:297
  208.9 1.2 hop.17
  210.1 1.3 collective-permute-start.34
  211.4 2.5 collective-permute-start.40
  214.0 4.3 %collective-permute-done.34 = bf16[64,2048]{1,0:T(8,128)(2,1)S(1)} collective-permute-done((bf16[64,2048]{1,0:T(8,128)(2,1)S(1)}, bf16[64,2048]{1,0:T(8,128)(2,1)S(1)}, u32[]{:S(2)}, u32[]{:S(2)}) %collective-permute-start.34) | collective-permute-done | bytes 262176 | tf_op jit(solution)/shard_map/ppermute | solution.py:297
  218.3 1.7 hop.16
  220.1 2.5 collective-permute-start.41
  222.6 5.7 %collective-permute-done.41 = bf16[64,2048]{1,0:T(8,128)(2,1)S(1)} collective-permute-done((bf16[64,2048]{1,0:T(8,128)(2,1)S(1)}, bf16[64,2048]{1,0:T(8,128)(2,1)S(1)}, u32[]{:S(2)}, u32[]{:S(2)}) %collective-permute-start.41) | collective-permute-done | bytes 262176 | tf_op jit(solution)/shard_map/ppermute | solution.py:293
  228.4 1.2 copy-done.21
  229.6 31.1 %back.1 = (bf16[128,10240]{1,0:T(8,128)(2,1)}, f32[8,10240]{1,0:T(8,128)S(1)}, f32[8,10240]{1,0:T(8,128)S(1)}, f32[128,128]{1,0:T(8,128)}, f32[8,128]{1,0:T(8,128)S(1)}) custom-call(s32[4]{0:T(128)S(1)} %copy-done.15, bf16[128,10240]{1,0:T(8,128)(2,1)} %get-tuple-element.68.refs_1_.refs_2_.refs_3_, ...), custom_call_target="tpu_custom_call" | custom-call | tf_op jit(solution)/shard_map/back/pallas_call | solution.py:446
  260.7 1.3 collective-permute-start.42
  262.5 1.1 all_to_all.13
  263.6 3.8 %all-to-all-start = ((f32[32,1,2560]{2,1,0:T(1,128)}), f32[32,1,2560]{2,1,0:T(1,128)S(1)}, u32[]{:S(2)}, u32[]{:S(2)}) async-start(f32[32,1,2560]{2,1,0:T(1,128)} %all_to_all.13), calls=%async_computation | async-start | bytes 655360 | tf_op jit(solution)/shard_map/all_to_all | solution.py:492
  268.2 11.2 %all-to-all-done = f32[32,1,2560]{2,1,0:T(1,128)S(1)} async-done(((f32[32,1,2560]{2,1,0:T(1,128)}), f32[32,1,2560]{2,1,0:T(1,128)S(1)}, u32[]{:S(2)}, u32[]{:S(2)}) %all-to-all-start) | async-done | bytes 327712 | tf_op jit(solution)/shard_map/all_to_all | solution.py:492
  280.3 3.4 %all-to-all-start.1 = ((f32[8,1,2560]{2,1,0:T(1,128)}), f32[8,1,2560]{2,1,0:T(1,128)S(1)}, u32[]{:S(2)}, u32[]{:S(2)}) async-start(f32[8,1,2560]{2,1,0:T(1,128)} %broadcast_in_dim.49), calls=%async_computation.1 | async-start | bytes 163840 | tf_op jit(solution)/shard_map/all_to_all | solution.py:495
  283.8 2.1 dynamic_update_slice.4
  285.9 4.7 %all-to-all-done.1 = f32[8,1,2560]{2,1,0:T(1,128)S(1)} async-done(((f32[8,1,2560]{2,1,0:T(1,128)}), f32[8,1,2560]{2,1,0:T(1,128)S(1)}, u32[]{:S(2)}, u32[]{:S(2)}) %all-to-all-start.1) | async-done | bytes 81952 | tf_op jit(solution)/shard_map/all_to_all | solution.py:495
  (200 shorter events, 32.7 us)
Async XLA Ops:
  1.6 18.4 %collective-permute-start = (bf16[3,10240]{1,0:T(4,128)(2,1)S(1)}, bf16[3,10240]{1,0:T(4,128)(2,1)S(1)}, u32[]{:S(2)}, u32[]{:S(2)}) collective-permute-start(bf16[3,10240]{1,0:T(4,128)(2,1)S(1)} %slice_bitcast_fusion), channel_id=1, source_target_pairs={{0,4},{4,8},{8,12},{12,16},{16,20},{20,24},{24,28},{1,5},{5,9},{9,... | collective-permute-start | bytes 184328 | tf_op jit(solution)/shard_map/ppermute | solution.py:352
  8.1 28.5 %copy-start.29 = (f32[8]{0:T(128)}, f32[8]{0:T(128)S(1)}, u32[]{:S(2)}) copy-start(f32[8]{0:T(128)S(1)} %pad.37.clone) | copy-start | bytes 100
  15.4 22.5 %copy-start.16 = (f32[1,128]{1,0:T(1,128)}, f32[1,128]{1,0:T(1,128)S(1)}, u32[]{:S(2)}) copy-start(f32[1,128]{1,0:T(1,128)S(1)} %reshape.110.refs_5_.refs_19_) | copy-start | bytes 1540
  15.4 22.4 %copy-start.18 = (f32[1,128]{1,0:T(1,128)}, f32[1,128]{1,0:T(1,128)S(1)}, u32[]{:S(2)}) copy-start(f32[1,128]{1,0:T(1,128)S(1)} %reshape.111.refs_6_.refs_20_) | copy-start | bytes 1540
  20.0 17.8 %copy-start.13 = (s32[4]{0:T(128)}, s32[4]{0:T(128)S(1)}, u32[]{:S(2)}) copy-start(s32[4]{0:T(128)S(1)} %pad_add_fusion.refs_0_) | copy-start | bytes 52
  38.7 22.6 %copy-start.1 = (bf16[4,64,2048]{2,1,0:T(8,128)(2,1)S(1)}, bf16[4,64,2048]{2,1,0:T(8,128)(2,1)}, u32[]{:S(2)}) copy-start(bf16[4,64,2048]{2,1,0:T(8,128)(2,1)} %copy-done) | copy-start | bytes 3145732
  38.7 13.7 %collective-permute-start.1 = (bf16[64,2048]{1,0:T(8,128)(2,1)S(1)}, bf16[64,2048]{1,0:T(8,128)(2,1)S(1)}, u32[]{:S(2)}, u32[]{:S(2)}) collective-permute-start(bf16[64,2048]{1,0:T(8,128)(2,1)S(1)} %get-tuple-element.218), channel_id=1, source_target_pairs={{0,4},{4,0},{1,5},{5,1},{2,6},{6,2},{3,7},{7,3}} | collective-permute-start | bytes 786440 | tf_op jit(solution)/shard_map/ppermute | solution.py:293
  43.5 8.9 %collective-permute-start.2 = (f32[1,8192]{1,0:T(1,128)S(1)}, f32[1,8192]{1,0:T(1,128)S(1)}, u32[]{:S(2)}, u32[]{:S(2)}) collective-permute-start(f32[1,8192]{1,0:T(1,128)S(1)} %get-tuple-element.72.refs_3_.refs_15_), channel_id=1, source_target_pairs={{0,4},{4,0},{8,12},{12,8},{16,20},{20,16},{24,28},{28,24},{1,5},{5... | collective-permute-start | bytes 98312 | tf_op jit(solution)/shard_map/ppermute | solution.py:405
  45.0 14.4 %collective-permute-start.3 = (bf16[64,2048]{1,0:T(8,128)(2,1)S(1)}, bf16[64,2048]{1,0:T(8,128)(2,1)S(1)}, u32[]{:S(2)}, u32[]{:S(2)}) collective-permute-start(bf16[64,2048]{1,0:T(8,128)(2,1)S(1)} %get-tuple-element.217), channel_id=1, source_target_pairs={{0,4},{4,0},{8,12},{12,8},{1,5},{5,1},{9,13},{13,9},{2,6},{6,2},{1... | collective-permute-start | bytes 786440 | tf_op jit(solution)/shard_map/ppermute | solution.py:293
  48.4 27.5 %collective-permute-start.5 = (bf16[64,2048]{1,0:T(8,128)(2,1)}, bf16[64,2048]{1,0:T(8,128)(2,1)S(1)}, u32[]{:S(2)}, u32[]{:S(2)}) collective-permute-start(bf16[64,2048]{1,0:T(8,128)(2,1)} %get-tuple-element.216), channel_id=1, source_target_pairs={{0,4},{4,0},{8,12},{12,8},{16,20},{20,16},{1,5},{5,1},{9,13},{13,9... | collective-permute-start | bytes 786440 | tf_op jit(solution)/shard_map/ppermute | solution.py:293
  50.8 34.8 %collective-permute-start.7 = (bf16[64,2048]{1,0:T(8,128)(2,1)}, bf16[64,2048]{1,0:T(8,128)(2,1)S(1)}, u32[]{:S(2)}, u32[]{:S(2)}) collective-permute-start(bf16[64,2048]{1,0:T(8,128)(2,1)} %get-tuple-element.215), channel_id=1, source_target_pairs={{0,4},{4,0},{8,12},{12,8},{16,20},{20,16},{24,28},{28,24},{1,5},{5... | collective-permute-start | bytes 786440 | tf_op jit(solution)/shard_map/ppermute | solution.py:293
  55.0 21.0 %copy-start.27 = (bf16[64,2048]{1,0:T(8,128)(2,1)S(1)}, bf16[64,2048]{1,0:T(8,128)(2,1)}, u32[]{:S(2)}) copy-start(bf16[64,2048]{1,0:T(8,128)(2,1)} %get-tuple-element.213) | copy-start | bytes 786436
  55.0 21.7 %copy-start.39 = (s32[2]{0:T(128)S(1)}, s32[2]{0:T(128)}, u32[]{:S(2)}) copy-start(s32[2]{0:T(128)} %pad_add_fusion.3) | copy-start | bytes 28
  55.0 6.4 %collective-permute-start.4 = (bf16[64,2048]{1,0:T(8,128)(2,1)S(1)}, bf16[64,2048]{1,0:T(8,128)(2,1)S(1)}, u32[]{:S(2)}, u32[]{:S(2)}) collective-permute-start(bf16[64,2048]{1,0:T(8,128)(2,1)S(1)} %get-tuple-element.74), channel_id=1, source_target_pairs={{0,8},{4,12},{1,9},{5,13},{2,10},{6,14},{3,11},{7,15}} | collective-permute-start | bytes 786440 | tf_op jit(solution)/shard_map/ppermute | solution.py:297
  56.5 16.0 %collective-permute-start.15 = (bf16[64,2048]{1,0:T(8,128)(2,1)S(1)}, bf16[64,2048]{1,0:T(8,128)(2,1)S(1)}, u32[]{:S(2)}, u32[]{:S(2)}) collective-permute-start(bf16[64,2048]{1,0:T(8,128)(2,1)S(1)} %get-tuple-element.86), channel_id=1, source_target_pairs={{0,4},{4,0},{1,5},{5,1},{2,6},{6,2},{3,7},{7,3}} | collective-permute-start | bytes 786440 | tf_op jit(solution)/shard_map/ppermute | solution.py:293
  59.4 33.0 %collective-permute-start.9 = (bf16[64,2048]{1,0:T(8,128)(2,1)}, bf16[64,2048]{1,0:T(8,128)(2,1)S(1)}, u32[]{:S(2)}, u32[]{:S(2)}) collective-permute-start(bf16[64,2048]{1,0:T(8,128)(2,1)} %get-tuple-element.214), channel_id=1, source_target_pairs={{8,12},{12,8},{16,20},{20,16},{24,28},{28,24},{9,13},{13,9},{17,21... | collective-permute-start | bytes 786440 | tf_op jit(solution)/shard_map/ppermute | solution.py:293
  62.6 23.1 %copy-start.25 = (bf16[64,2048]{1,0:T(8,128)(2,1)S(1)}, bf16[64,2048]{1,0:T(8,128)(2,1)}, u32[]{:S(2)}) copy-start(bf16[64,2048]{1,0:T(8,128)(2,1)} %get-tuple-element.212) | copy-start | bytes 786436
  62.6 23.7 %copy-start.38 = (s32[2]{0:T(128)S(1)}, s32[2]{0:T(128)}, u32[]{:S(2)}) copy-start(s32[2]{0:T(128)} %pad_add_fusion.4) | copy-start | bytes 28
  62.6 14.1 %collective-permute-start.6 = (bf16[64,2048]{1,0:T(8,128)(2,1)S(1)}, bf16[64,2048]{1,0:T(8,128)(2,1)S(1)}, u32[]{:S(2)}, u32[]{:S(2)}) collective-permute-start(bf16[64,2048]{1,0:T(8,128)(2,1)S(1)} %get-tuple-element.148), channel_id=1, source_target_pairs={{0,8},{4,12},{8,16},{12,20},{1,9},{5,13},{9,17},{13,21},{2,10},{6,... | collective-permute-start | bytes 786440 | tf_op jit(solution)/shard_map/ppermute | solution.py:297
  72.5 9.6 %collective-permute-start.16 = (bf16[64,2048]{1,0:T(8,128)(2,1)S(1)}, bf16[64,2048]{1,0:T(8,128)(2,1)S(1)}, u32[]{:S(2)}, u32[]{:S(2)}) collective-permute-start(bf16[64,2048]{1,0:T(8,128)(2,1)S(1)} %get-tuple-element.150), channel_id=1, source_target_pairs={{0,4},{4,0},{8,12},{12,8},{1,5},{5,1},{9,13},{13,9},{2,6},{6,2},{1... | collective-permute-start | bytes 786440 | tf_op jit(solution)/shard_map/ppermute | solution.py:293
  76.0 21.3 %collective-permute-start.11 = (bf16[64,2048]{1,0:T(8,128)(2,1)S(1)}, bf16[64,2048]{1,0:T(8,128)(2,1)S(1)}, u32[]{:S(2)}, u32[]{:S(2)}) collective-permute-start(bf16[64,2048]{1,0:T(8,128)(2,1)S(1)} %copy-done.27), channel_id=1, source_target_pairs={{16,20},{20,16},{24,28},{28,24},{17,21},{21,17},{25,29},{29,25},{1... | collective-permute-start | bytes 786440 | tf_op jit(solution)/shard_map/ppermute | solution.py:293
  77.9 16.5 %copy-start.37 = (s32[2]{0:T(128)S(1)}, s32[2]{0:T(128)}, u32[]{:S(2)}) copy-start(s32[2]{0:T(128)} %pad_add_fusion.5) | copy-start | bytes 28
  77.9 8.4 %collective-permute-start.8 = (bf16[64,2048]{1,0:T(8,128)(2,1)S(1)}, bf16[64,2048]{1,0:T(8,128)(2,1)S(1)}, u32[]{:S(2)}, u32[]{:S(2)}) collective-permute-start(bf16[64,2048]{1,0:T(8,128)(2,1)S(1)} %get-tuple-element.154), channel_id=1, source_target_pairs={{0,8},{4,12},{8,16},{12,20},{16,24},{20,28},{1,9},{5,13},{9,17},{1... | collective-permute-start | bytes 786440 | tf_op jit(solution)/shard_map/ppermute | solution.py:297
  82.1 8.7 %collective-permute-start.17 = (bf16[64,2048]{1,0:T(8,128)(2,1)S(1)}, bf16[64,2048]{1,0:T(8,128)(2,1)S(1)}, u32[]{:S(2)}, u32[]{:S(2)}) collective-permute-start(bf16[64,2048]{1,0:T(8,128)(2,1)S(1)} %get-tuple-element.156), channel_id=1, source_target_pairs={{0,4},{4,0},{8,12},{12,8},{16,20},{20,16},{1,5},{5,1},{9,13},{13,9... | collective-permute-start | bytes 786440 | tf_op jit(solution)/shard_map/ppermute | solution.py:293
  85.6 14.3 %collective-permute-start.13 = (bf16[64,2048]{1,0:T(8,128)(2,1)S(1)}, bf16[64,2048]{1,0:T(8,128)(2,1)S(1)}, u32[]{:S(2)}, u32[]{:S(2)}) collective-permute-start(bf16[64,2048]{1,0:T(8,128)(2,1)S(1)} %copy-done.25), channel_id=1, source_target_pairs={{24,28},{28,24},{25,29},{29,25},{26,30},{30,26},{27,31},{31,27}} | collective-permute-start | bytes 786440 | tf_op jit(solution)/shard_map/ppermute | solution.py:293
  87.5 6.8 %collective-permute-start.10 = (bf16[64,2048]{1,0:T(8,128)(2,1)S(1)}, bf16[64,2048]{1,0:T(8,128)(2,1)S(1)}, u32[]{:S(2)}, u32[]{:S(2)}) collective-permute-start(bf16[64,2048]{1,0:T(8,128)(2,1)S(1)} %get-tuple-element.142), channel_id=1, source_target_pairs={{0,8},{4,12},{8,16},{12,20},{16,24},{20,28},{1,9},{5,13},{9,17},{1... | collective-permute-start | bytes 786440 | tf_op jit(solution)/shard_map/ppermute | solution.py:297
  90.9 6.4 %collective-permute-start.18 = (bf16[64,2048]{1,0:T(8,128)(2,1)S(1)}, bf16[64,2048]{1,0:T(8,128)(2,1)S(1)}, u32[]{:S(2)}, u32[]{:S(2)}) collective-permute-start(bf16[64,2048]{1,0:T(8,128)(2,1)S(1)} %get-tuple-element.144), channel_id=1, source_target_pairs={{0,4},{4,0},{8,12},{12,8},{16,20},{20,16},{24,28},{28,24},{1,5},{5... | collective-permute-start | bytes 786440 | tf_op jit(solution)/shard_map/ppermute | solution.py:293
  95.5 1.7 collective-permute-start.12
  96.2 3.6 %collective-permute-start.19 = (bf16[64,2048]{1,0:T(8,128)(2,1)S(1)}, bf16[64,2048]{1,0:T(8,128)(2,1)S(1)}, u32[]{:S(2)}, u32[]{:S(2)}) collective-permute-start(bf16[64,2048]{1,0:T(8,128)(2,1)S(1)} %get-tuple-element.138), channel_id=1, source_target_pairs={{8,12},{12,8},{16,20},{20,16},{24,28},{28,24},{9,13},{13,9},{17,21... | collective-permute-start | bytes 786440 | tf_op jit(solution)/shard_map/ppermute | solution.py:293
  98.5 1.4 collective-permute-start.14
  99.1 3.2 %collective-permute-start.20 = (bf16[64,2048]{1,0:T(8,128)(2,1)S(1)}, bf16[64,2048]{1,0:T(8,128)(2,1)S(1)}, u32[]{:S(2)}, u32[]{:S(2)}) collective-permute-start(bf16[64,2048]{1,0:T(8,128)(2,1)S(1)} %get-tuple-element.168), channel_id=1, source_target_pairs={{16,20},{20,16},{24,28},{28,24},{17,21},{21,17},{25,29},{29,25},{1... | collective-permute-start | bytes 786440 | tf_op jit(solution)/shard_map/ppermute | solution.py:293
  101.6 0.7 collective-permute-start.21
  122.2 5.0 %collective-permute-start.22 = (bf16[64,2048]{1,0:T(8,128)(2,1)S(1)}, bf16[64,2048]{1,0:T(8,128)(2,1)S(1)}, u32[]{:S(2)}, u32[]{:S(2)}) collective-permute-start(bf16[64,2048]{1,0:T(8,128)(2,1)S(1)} %get-tuple-element.211), channel_id=1, source_target_pairs={{28,24},{24,28},{29,25},{25,29},{30,26},{26,30},{31,27},{27,31}} | collective-permute-start | bytes 786440 | tf_op jit(solution)/shard_map/ppermute | solution.py:293
  123.1 8.2 %collective-permute-start.23 = (bf16[64,2048]{1,0:T(8,128)(2,1)S(1)}, bf16[64,2048]{1,0:T(8,128)(2,1)S(1)}, u32[]{:S(2)}, u32[]{:S(2)}) collective-permute-start(bf16[64,2048]{1,0:T(8,128)(2,1)S(1)} %get-tuple-element.210), channel_id=1, source_target_pairs={{28,24},{24,28},{20,16},{16,20},{29,25},{25,29},{21,17},{17,21},{3... | collective-permute-start | bytes 786440 | tf_op jit(solution)/shard_map/ppermute | solution.py:293
  123.8 12.7 %collective-permute-start.25 = (bf16[64,2048]{1,0:T(8,128)(2,1)}, bf16[64,2048]{1,0:T(8,128)(2,1)}, u32[]{:S(2)}, u32[]{:S(2)}) collective-permute-start(bf16[64,2048]{1,0:T(8,128)(2,1)} %get-tuple-element.209), channel_id=1, source_target_pairs={{28,24},{24,28},{20,16},{16,20},{12,8},{8,12},{29,25},{25,29},{21,... | collective-permute-start | bytes 786440 | tf_op jit(solution)/shard_map/ppermute | solution.py:293
  125.2 18.8 %collective-permute-start.27 = (bf16[64,2048]{1,0:T(8,128)(2,1)}, bf16[64,2048]{1,0:T(8,128)(2,1)}, u32[]{:S(2)}, u32[]{:S(2)}) collective-permute-start(bf16[64,2048]{1,0:T(8,128)(2,1)} %get-tuple-element.208), channel_id=1, source_target_pairs={{28,24},{24,28},{20,16},{16,20},{12,8},{8,12},{4,0},{0,4},{29,25},... | collective-permute-start | bytes 786440 | tf_op jit(solution)/shard_map/ppermute | solution.py:293
  129.8 3.9 %collective-permute-start.24 = (bf16[64,2048]{1,0:T(8,128)(2,1)S(1)}, bf16[64,2048]{1,0:T(8,128)(2,1)S(1)}, u32[]{:S(2)}, u32[]{:S(2)}) collective-permute-start(bf16[64,2048]{1,0:T(8,128)(2,1)S(1)} %get-tuple-element.97), channel_id=1, source_target_pairs={{28,20},{24,16},{29,21},{25,17},{30,22},{26,18},{31,23},{27,19}} | collective-permute-start | bytes 786440 | tf_op jit(solution)/shard_map/ppermute | solution.py:297
  130.6 5.2 %collective-permute-start.35 = (bf16[64,2048]{1,0:T(8,128)(2,1)S(1)}, bf16[64,2048]{1,0:T(8,128)(2,1)S(1)}, u32[]{:S(2)}, u32[]{:S(2)}) collective-permute-start(bf16[64,2048]{1,0:T(8,128)(2,1)S(1)} %get-tuple-element.109), channel_id=1, source_target_pairs={{28,24},{24,28},{29,25},{25,29},{30,26},{26,30},{31,27},{27,31}} | collective-permute-start | bytes 786440 | tf_op jit(solution)/shard_map/ppermute | solution.py:293
  131.3 59.3 %collective-permute-start.29 = (bf16[64,2048]{1,0:T(8,128)(2,1)}, bf16[64,2048]{1,0:T(8,128)(2,1)S(1)}, u32[]{:S(2)}, u32[]{:S(2)}) collective-permute-start(bf16[64,2048]{1,0:T(8,128)(2,1)} %get-tuple-element.207), channel_id=1, source_target_pairs={{20,16},{16,20},{12,8},{8,12},{4,0},{0,4},{21,17},{17,21},{13,9},{... | collective-permute-start | bytes 786440 | tf_op jit(solution)/shard_map/ppermute | solution.py:293
  134.9 51.3 %copy-start.32 = (s32[2]{0:T(128)S(1)}, s32[2]{0:T(128)}, u32[]{:S(2)}) copy-start(s32[2]{0:T(128)} %pad_add_fusion.11) | copy-start | bytes 28
  134.9 5.0 %collective-permute-start.26 = (bf16[64,2048]{1,0:T(8,128)(2,1)S(1)}, bf16[64,2048]{1,0:T(8,128)(2,1)S(1)}, u32[]{:S(2)}, u32[]{:S(2)}) collective-permute-start(bf16[64,2048]{1,0:T(8,128)(2,1)S(1)} %get-tuple-element.160), channel_id=1, source_target_pairs={{28,20},{24,16},{20,12},{16,8},{29,21},{25,17},{21,13},{17,9},{30,... | collective-permute-start | bytes 786440 | tf_op jit(solution)/shard_map/ppermute | solution.py:297
  135.8 7.5 %collective-permute-start.36 = (bf16[64,2048]{1,0:T(8,128)(2,1)S(1)}, bf16[64,2048]{1,0:T(8,128)(2,1)S(1)}, u32[]{:S(2)}, u32[]{:S(2)}) collective-permute-start(bf16[64,2048]{1,0:T(8,128)(2,1)S(1)} %get-tuple-element.162), channel_id=1, source_target_pairs={{28,24},{24,28},{20,16},{16,20},{29,25},{25,29},{21,17},{17,21},{3... | collective-permute-start | bytes 786440 | tf_op jit(solution)/shard_map/ppermute | solution.py:293
  136.5 67.1 %collective-permute-start.31 = (bf16[64,2048]{1,0:T(8,128)(2,1)S(1)}, bf16[64,2048]{1,0:T(8,128)(2,1)S(1)}, u32[]{:S(2)}, u32[]{:S(2)}) collective-permute-start(bf16[64,2048]{1,0:T(8,128)(2,1)S(1)} %copy-done.28), channel_id=1, source_target_pairs={{12,8},{8,12},{4,0},{0,4},{13,9},{9,13},{5,1},{1,5},{14,10},{10,14... | collective-permute-start | bytes 786440 | tf_op jit(solution)/shard_map/ppermute | solution.py:293
  142.0 56.4 %copy-start.31 = (s32[2]{0:T(128)S(1)}, s32[2]{0:T(128)}, u32[]{:S(2)}) copy-start(s32[2]{0:T(128)} %pad_add_fusion.12) | copy-start | bytes 28
  142.0 44.2 %collective-permute-start.28 = (bf16[64,2048]{1,0:T(8,128)(2,1)S(1)}, bf16[64,2048]{1,0:T(8,128)(2,1)S(1)}, u32[]{:S(2)}, u32[]{:S(2)}) collective-permute-start(bf16[64,2048]{1,0:T(8,128)(2,1)S(1)} %get-tuple-element.130), channel_id=1, source_target_pairs={{28,20},{24,16},{20,12},{16,8},{12,4},{8,0},{29,21},{25,17},{21,13... | collective-permute-start | bytes 786440 | tf_op jit(solution)/shard_map/ppermute | solution.py:297
  143.3 46.4 %collective-permute-start.37 = (bf16[64,2048]{1,0:T(8,128)(2,1)S(1)}, bf16[64,2048]{1,0:T(8,128)(2,1)S(1)}, u32[]{:S(2)}, u32[]{:S(2)}) collective-permute-start(bf16[64,2048]{1,0:T(8,128)(2,1)S(1)} %get-tuple-element.132), channel_id=1, source_target_pairs={{28,24},{24,28},{20,16},{16,20},{12,8},{8,12},{29,25},{25,29},{21,... | collective-permute-start | bytes 786440 | tf_op jit(solution)/shard_map/ppermute | solution.py:293
  144.0 70.0 %collective-permute-start.33 = (bf16[64,2048]{1,0:T(8,128)(2,1)S(1)}, bf16[64,2048]{1,0:T(8,128)(2,1)S(1)}, u32[]{:S(2)}, u32[]{:S(2)}) collective-permute-start(bf16[64,2048]{1,0:T(8,128)(2,1)S(1)} %copy-done.26), channel_id=1, source_target_pairs={{4,0},{0,4},{5,1},{1,5},{6,2},{2,6},{7,3},{3,7}} | collective-permute-start | bytes 786440 | tf_op jit(solution)/shard_map/ppermute | solution.py:293
  188.3 10.2 %collective-permute-start.30 = (bf16[64,2048]{1,0:T(8,128)(2,1)S(1)}, bf16[64,2048]{1,0:T(8,128)(2,1)S(1)}, u32[]{:S(2)}, u32[]{:S(2)}) collective-permute-start(bf16[64,2048]{1,0:T(8,128)(2,1)S(1)} %get-tuple-element.198), channel_id=1, source_target_pairs={{28,20},{24,16},{20,12},{16,8},{12,4},{8,0},{29,21},{25,17},{21,13... | collective-permute-start | bytes 786440 | tf_op jit(solution)/shard_map/ppermute | solution.py:297
  189.8 13.8 %collective-permute-start.38 = (bf16[64,2048]{1,0:T(8,128)(2,1)S(1)}, bf16[64,2048]{1,0:T(8,128)(2,1)S(1)}, u32[]{:S(2)}, u32[]{:S(2)}) collective-permute-start(bf16[64,2048]{1,0:T(8,128)(2,1)S(1)} %get-tuple-element.200), channel_id=1, source_target_pairs={{28,24},{24,28},{20,16},{16,20},{12,8},{8,12},{4,0},{0,4},{29,25},... | collective-permute-start | bytes 786440 | tf_op jit(solution)/shard_map/ppermute | solution.py:293
  199.6 9.3 %collective-permute-start.32 = (bf16[64,2048]{1,0:T(8,128)(2,1)S(1)}, bf16[64,2048]{1,0:T(8,128)(2,1)S(1)}, u32[]{:S(2)}, u32[]{:S(2)}) collective-permute-start(bf16[64,2048]{1,0:T(8,128)(2,1)S(1)} %get-tuple-element.179), channel_id=1, source_target_pairs={{20,12},{16,8},{12,4},{8,0},{21,13},{17,9},{13,5},{9,1},{22,14},{1... | collective-permute-start | bytes 786440 | tf_op jit(solution)/shard_map/ppermute | solution.py:297
  200.9 13.0 %collective-permute-start.39 = (bf16[64,2048]{1,0:T(8,128)(2,1)S(1)}, bf16[64,2048]{1,0:T(8,128)(2,1)S(1)}, u32[]{:S(2)}, u32[]{:S(2)}) collective-permute-start(bf16[64,2048]{1,0:T(8,128)(2,1)S(1)} %get-tuple-element.181), channel_id=1, source_target_pairs={{20,16},{16,20},{12,8},{8,12},{4,0},{0,4},{21,17},{17,21},{13,9},{... | collective-permute-start | bytes 786440 | tf_op jit(solution)/shard_map/ppermute | solution.py:293
  210.1 8.3 %collective-permute-start.34 = (bf16[64,2048]{1,0:T(8,128)(2,1)S(1)}, bf16[64,2048]{1,0:T(8,128)(2,1)S(1)}, u32[]{:S(2)}, u32[]{:S(2)}) collective-permute-start(bf16[64,2048]{1,0:T(8,128)(2,1)S(1)} %get-tuple-element.185), channel_id=1, source_target_pairs={{12,4},{8,0},{13,5},{9,1},{14,6},{10,2},{15,7},{11,3}} | collective-permute-start | bytes 786440 | tf_op jit(solution)/shard_map/ppermute | solution.py:297
  211.4 11.2 %collective-permute-start.40 = (bf16[64,2048]{1,0:T(8,128)(2,1)S(1)}, bf16[64,2048]{1,0:T(8,128)(2,1)S(1)}, u32[]{:S(2)}, u32[]{:S(2)}) collective-permute-start(bf16[64,2048]{1,0:T(8,128)(2,1)S(1)} %get-tuple-element.187), channel_id=1, source_target_pairs={{12,8},{8,12},{4,0},{0,4},{13,9},{9,13},{5,1},{1,5},{14,10},{10,14... | collective-permute-start | bytes 786440 | tf_op jit(solution)/shard_map/ppermute | solution.py:293
  213.9 15.7 %copy-start.7 = (bf16[7,64,2048]{2,1,0:T(8,128)(2,1)S(1)}, bf16[7,64,2048]{2,1,0:T(8,128)(2,1)}, u32[]{:S(2)}) copy-start(bf16[7,64,2048]{2,1,0:T(8,128)(2,1)} %copy-done.6) | copy-start | bytes 5505028
  213.9 15.6 %copy-start.5 = (bf16[7,64,2048]{2,1,0:T(8,128)(2,1)S(1)}, bf16[7,64,2048]{2,1,0:T(8,128)(2,1)}, u32[]{:S(2)}) copy-start(bf16[7,64,2048]{2,1,0:T(8,128)(2,1)} %copy-done.4) | copy-start | bytes 5505028
  213.9 15.6 %copy-start.10 = (bf16[1,128,128]{2,1,0:T(8,128)(2,1)S(1)}, bf16[1,128,128]{2,1,0:T(8,128)(2,1)}, u32[]{:S(2)}) copy-start(bf16[1,128,128]{2,1,0:T(8,128)(2,1)} %param.11) | copy-start | bytes 98308
  214.0 15.6 %copy-start.12 = (f32[128,128]{1,0:T(8,128)S(1)}, f32[128,128]{1,0:T(8,128)}, u32[]{:S(2)}) copy-start(f32[128,128]{1,0:T(8,128)} %copy-done.11) | copy-start | bytes 196612
  214.0 15.6 %copy-start.15 = (s32[4]{0:T(128)S(1)}, s32[4]{0:T(128)}, u32[]{:S(2)}) copy-start(s32[4]{0:T(128)} %copy-done.13) | copy-start | bytes 52
  214.0 15.6 %copy-start.17 = (f32[1,128]{1,0:T(1,128)S(1)}, f32[1,128]{1,0:T(1,128)}, u32[]{:S(2)}) copy-start(f32[1,128]{1,0:T(1,128)} %copy-done.16) | copy-start | bytes 1540
  220.1 8.3 %collective-permute-start.41 = (bf16[64,2048]{1,0:T(8,128)(2,1)S(1)}, bf16[64,2048]{1,0:T(8,128)(2,1)S(1)}, u32[]{:S(2)}, u32[]{:S(2)}) collective-permute-start(bf16[64,2048]{1,0:T(8,128)(2,1)S(1)} %get-tuple-element.192), channel_id=1, source_target_pairs={{4,0},{0,4},{5,1},{1,5},{6,2},{2,6},{7,3},{3,7}} | collective-permute-start | bytes 786440 | tf_op jit(solution)/shard_map/ppermute | solution.py:293
  229.6 32.8 %copy-start.30 = (f32[8]{0:T(128)S(1)}, f32[8]{0:T(128)}, u32[]{:S(2)}) copy-start(f32[8]{0:T(128)} %copy-done.29) | copy-start | bytes 100
  260.7 7.2 %collective-permute-start.42 = (f32[3,10240]{1,0:T(4,128)S(1)}, f32[3,10240]{1,0:T(4,128)S(1)}, u32[]{:S(2)}, u32[]{:S(2)}) collective-permute-start(f32[3,10240]{1,0:T(4,128)S(1)} %slice.121), channel_id=1, source_target_pairs={{4,0},{8,4},{12,8},{16,12},{20,16},{24,20},{28,24},{5,1},{9,5},{13... | collective-permute-start | bytes 368648 | tf_op jit(solution)/shard_map/ppermute | solution.py:475
  263.6 15.8 %all-to-all-start = ((f32[32,1,2560]{2,1,0:T(1,128)}), f32[32,1,2560]{2,1,0:T(1,128)S(1)}, u32[]{:S(2)}, u32[]{:S(2)}) async-start(f32[32,1,2560]{2,1,0:T(1,128)} %all_to_all.13), calls=%async_computation | async-start | bytes 655360 | tf_op jit(solution)/shard_map/all_to_all | solution.py:492
  280.3 10.3 %all-to-all-start.1 = ((f32[8,1,2560]{2,1,0:T(1,128)}), f32[8,1,2560]{2,1,0:T(1,128)S(1)}, u32[]{:S(2)}, u32[]{:S(2)}) async-start(f32[8,1,2560]{2,1,0:T(1,128)} %broadcast_in_dim.49), calls=%async_computation.1 | async-start | bytes 163840 | tf_op jit(solution)/shard_map/all_to_all | solution.py:495
  (21 other events, 110.5 us)

commit v2 on v1

v2 whole, which is shorter than its diff:
```python
import math

import jax
import jax.numpy as jnp
from jax import lax
from jax.experimental import pallas as pl
from jax.experimental.pallas import tpu as pltpu
from jax.sharding import PartitionSpec as P

HEAD_DIM = 64
STATE = 128
GROUPS = 8
KERNEL = 4
EPSILON = 1e-05
HALO = KERNEL - 1
PAD = 8
CHUNKS = 4
F32 = jnp.float32
BF16 = jnp.bfloat16
HIGHEST = lax.Precision.HIGHEST


def mm(a, b):
    return jnp.dot(a, b, preferred_element_type=F32)


def mm_nt(a, b):
    return lax.dot_general(a, b, (((1,), (1,)), ((), ())), preferred_element_type=F32)


def sigmoid(v):
    return 0.5 * jnp.tanh(0.5 * v) + 0.5


def softplus(v):
    return jnp.maximum(v, 0.0) + jnp.log(1.0 + jnp.exp(-jnp.abs(v)))


def spread_heads(table, group, per_group):
    heads = table.shape[1]
    table = pltpu.roll(table, lax.rem(heads - group * per_group, heads), 1)
    rows = table.shape[0]
    pair = 128 // HEAD_DIM
    lane = lax.broadcasted_iota(jnp.int32, (rows, 128), 1)
    tiles = []
    for i in range(per_group // pair):
        tile = jnp.broadcast_to(table[:, pair * i : pair * i + 1], (rows, 128))
        for p in range(1, pair):
            col = jnp.broadcast_to(table[:, pair * i + p : pair * i + p + 1], (rows, 128))
            tile = jnp.where(lane >= p * HEAD_DIM, col, tile)
        tiles.append(tile)
    return jnp.concatenate(tiles, axis=1)


def sum_heads(values, group, per_group, heads):
    width = values.shape[1]
    row = lax.broadcasted_iota(jnp.int32, (width, heads), 0) // HEAD_DIM + group * per_group
    col = lax.broadcasted_iota(jnp.int32, (width, heads), 1)
    pick = jnp.where(row == col, 1.0, 0.0).astype(BF16)
    high = values.astype(BF16)
    low = (values - high.astype(F32)).astype(BF16)
    return mm(high, pick) + mm(low, pick)


def lower_mask(n):
    return lax.broadcasted_iota(jnp.int32, (n, n), 0) >= lax.broadcasted_iota(jnp.int32, (n, n), 1)


def upper_mask(n):
    return lax.broadcasted_iota(jnp.int32, (n, n), 0) <= lax.broadcasted_iota(jnp.int32, (n, n), 1)


def conv_pre(x_ref, halo_ref, w_ref, xs):
    length = x_ref.shape[0]
    xs[PAD - HALO : PAD, :] = halo_ref[...].astype(F32)
    xs[PAD : PAD + length, :] = x_ref[...].astype(F32)
    pre = jnp.broadcast_to(w_ref[KERNEL : KERNEL + 1, :], (length, x_ref.shape[1]))
    for k in range(KERNEL):
        pre = pre + w_ref[k : k + 1, :] * xs[PAD - HALO + k : PAD - HALO + k + length, :]
    return pre


def split_halves(state, mine, own_ref, send_ref):
    half = state.shape[0] // 2
    low, high = state[:half].astype(BF16), state[half:].astype(BF16)
    shape = own_ref.shape
    own_ref[...] = jnp.where(mine == 0, low, high).reshape(shape)
    send_ref[...] = jnp.where(mine == 0, high, low).reshape(shape)


def keys_kernel(per_group, x_ref, halo_ref, w_ref, dt_ref, sb_ref, dl_ref, kq_ref, ec_ref, ei_ref, et_ref, xs):
    length = x_ref.shape[0]

    @pl.when(pl.program_id(0) == 0)
    def _():
        step = softplus(dt_ref[...].astype(F32) + sb_ref[...])
        ld = -jnp.exp(dl_ref[...]) * step
        tril = jnp.where(lower_mask(length), 1.0, 0.0).astype(F32)
        cum = jnp.dot(tril, ld, precision=HIGHEST, preferred_element_type=F32)
        ec = jnp.exp(cum)
        ec_ref[...] = ec
        ei_ref[...] = jnp.exp(-cum) * step
        width = per_group * HEAD_DIM
        for g in range(GROUPS):
            et_ref[:, g * width : (g + 1) * width] = spread_heads(ec[length - 8 :, :], g, per_group)[7:8, :]

    pre = conv_pre(x_ref, halo_ref, w_ref, xs)
    kq_ref[...] = (pre * sigmoid(pre)).astype(BF16)


def front_kernel(per_group, first, x_ref, halo_ref, w_ref, k_ref, ei_ref, et_ref,
                 side_ref, mixed_ref, vp_ref, own_ref, send_ref, xs):
    g = first + pl.program_id(0)
    pre = conv_pre(x_ref, halo_ref, w_ref, xs)
    mixed = (pre * sigmoid(pre)).astype(BF16)
    mixed_ref[...] = mixed
    vp = (mixed.astype(F32) * spread_heads(ei_ref[...], g, per_group)).astype(BF16)
    vp_ref[...] = vp
    ut = mm(k_ref[...].astype(F32).T.astype(BF16), vp) * et_ref[...]
    split_halves(ut, side_ref[0], own_ref, send_ref)


def choose(refs, pick):
    value = refs[0][...]
    for i in range(1, len(refs)):
        value = jnp.where(pick == i, refs[i][...], value)
    return value


def join_halves(own, other, mine):
    return jnp.concatenate([jnp.where(mine == 0, own, other), jnp.where(mine == 0, other, own)], axis=0)


def middle_kernel(per_group, first, depth, v_ref, k_ref, q_ref, vp_ref, ec_ref, gate_ref, og_ref, gain_ref, skip_ref,
                  side_ref, *refs):
    keeps, backs = refs[:depth], refs[depth : 2 * depth]
    dy_ref, dyp_ref, st_ref, own_ref, send_ref, a1_ref, gg_ref, rows_ref = refs[2 * depth :]
    st = join_halves(choose(keeps, side_ref[2]), choose(backs, side_ref[2]), side_ref[0])
    st_ref[...] = st
    g = first + pl.program_id(0)
    length, width = v_ref.shape
    heads = ec_ref.shape[1]
    q = q_ref[...]
    z = jnp.where(lower_mask(length), mm_nt(q, k_ref[...]), 0.0).astype(BF16)
    yn = mm(jnp.concatenate([z, q], axis=1), jnp.concatenate([vp_ref[...], st], axis=0))
    ecx = spread_heads(ec_ref[...], g, per_group)
    v = v_ref[...].astype(F32)
    y = (ecx * yn + skip_ref[...] * v).astype(BF16).astype(F32)
    gate = gate_ref[...].astype(F32)
    og = og_ref[...].astype(F32)
    sig = sigmoid(gate)
    act = gate * sig
    gated = y * act
    scale = lax.rsqrt(jnp.sum(gated * gated, axis=1, keepdims=True) * (1.0 / width) + EPSILON)
    dgn = og * gain_ref[...]
    inner = jnp.sum(dgn * gated, axis=1, keepdims=True) * (1.0 / width)
    dgated = scale * dgn - gated * (scale * scale * scale * inner)
    dyb = (dgated * act).astype(BF16)
    dy_ref[...] = dyb
    gg_ref[...] = (dgated * y * (sig + act * (1.0 - sig))).astype(BF16)
    dy = dyb.astype(F32)
    dyp = (ecx * dy).astype(BF16)
    dyp_ref[...] = dyp
    gt = mm(q.astype(F32).T.astype(BF16), dyp)
    split_halves(gt, side_ref[1], own_ref, send_ref)
    rows_ref[...] = jnp.zeros(rows_ref.shape, F32)
    rows_ref[0:1, :] = jnp.sum(og * gated * scale, axis=0, keepdims=True)
    rows_ref[1:2, :] = jnp.sum(dy * v, axis=0, keepdims=True)

    @pl.when(pl.program_id(0) == 0)
    def _():
        a1_ref[...] = jnp.zeros(a1_ref.shape, F32)

    a1_ref[...] += sum_heads(dyp.astype(F32) * yn, g, per_group, heads)


def conv_back(grads, x_ref, halo_ref, w_ref, gx_ref, edge_ref, wr_ref, xs, gs):
    length = x_ref.shape[0]
    pre = conv_pre(x_ref, halo_ref, w_ref, xs)
    sig = sigmoid(pre)
    gp = grads * (sig * (1.0 + pre * (1.0 - sig)))
    gs[0:length, :] = gp
    gs[length:, :] = jnp.zeros((gs.shape[0] - length, gs.shape[1]), F32)
    wr_ref[...] = jnp.zeros(wr_ref.shape, F32)
    total = jnp.zeros(gp.shape, F32)
    for k in range(KERNEL):
        lead = HALO - k
        total = total + w_ref[k : k + 1, :] * gs[lead : lead + length, :]
        wr_ref[k : k + 1, :] = jnp.sum(gp * xs[PAD - HALO + k : PAD - HALO + k + length, :], axis=0, keepdims=True)
    wr_ref[KERNEL : KERNEL + 1, :] = jnp.sum(gp, axis=0, keepdims=True)
    gx_ref[...] = total.astype(BF16)
    edge_ref[...] = jnp.zeros(edge_ref.shape, F32)
    edge_ref[0:HALO, :] = gp[0:HALO, :]
    edge_ref[HALO : 2 * HALO, :] = total[length - HALO : length, :]


def back_kernel(per_group, first, depth, k_ref, q_ref, vp_ref, st_ref, dy_ref, dyp_ref, x_ref, halo_ref, w_ref,
                skip_ref, et_ref, ei_ref, side_ref, *refs):
    keeps, backs = refs[:depth], refs[depth : 2 * depth]
    dkq_ref, a2_ref, last_ref, gx_ref, edge_ref, wr_ref, xs, gs = refs[2 * depth :]
    j = first + pl.program_id(0)
    length, width = x_ref.shape
    heads = ei_ref.shape[1]

    @pl.when(pl.program_id(0) == 0)
    def _():
        a2_ref[...] = jnp.zeros(a2_ref.shape, F32)
        last_ref[...] = jnp.zeros(last_ref.shape, F32)

    k = k_ref[...]
    q = q_ref[...]
    vp = vp_ref[...]
    dyp = dyp_ref[...]
    st = st_ref[...]
    en = join_halves(choose(keeps, side_ref[3]), choose(backs, side_ref[3]), side_ref[1])
    en = (et_ref[...] * en.astype(F32)).astype(BF16)
    zt = jnp.where(upper_mask(length), mm_nt(k, q), 0.0).astype(BF16)
    dvp = mm(jnp.concatenate([zt, k], axis=1), jnp.concatenate([dyp, en], axis=0))
    grads = spread_heads(ei_ref[...], j, per_group) * dvp + skip_ref[...] * dy_ref[...].astype(F32)
    a2_ref[...] += sum_heads(vp.astype(F32) * dvp, j, per_group, heads)
    ends = en.astype(F32) * (st.astype(F32) + mm(k.astype(F32).T.astype(BF16), vp))
    ends = jnp.broadcast_to(jnp.sum(ends, axis=0, keepdims=True), (8, width))
    last_ref[...] += sum_heads(ends, j, per_group, heads)
    dz = jnp.where(lower_mask(length), mm_nt(dyp, vp), 0.0)
    dkq_ref[0] = mm(dz.T.astype(BF16), q) + mm_nt(vp, en)
    dkq_ref[1] = mm(dz.astype(BF16), k) + mm_nt(dyp, st)
    conv_back(grads, x_ref, halo_ref, w_ref, gx_ref, edge_ref, wr_ref, xs, gs)


def last_kernel(count, x_ref, halo_ref, w_ref, dt_ref, sb_ref, dl_ref, *refs):
    dkq, a1, a2, last = (refs[i * count : (i + 1) * count] for i in range(4))
    gdt_ref, hs_ref, gx_ref, edge_ref, wr_ref, xs, gs = refs[4 * count :]
    grads = jnp.concatenate([ref[0] for ref in dkq], axis=1)
    conv_back(grads, x_ref, halo_ref, w_ref, gx_ref, edge_ref, wr_ref, xs, gs)

    @pl.when(pl.program_id(0) == 0)
    def _():
        length, heads = dt_ref.shape
        raw = dt_ref[...].astype(F32) + sb_ref[...]
        step = softplus(raw)
        rate = jnp.exp(dl_ref[...])
        row = lax.broadcasted_iota(jnp.int32, (length, heads), 0)
        down = sum(ref[...] for ref in a2)
        end = sum(ref[...] for ref in last)[0:1, :]
        dcum = sum(ref[...] for ref in a1) - down + jnp.where(row == length - 1, end, 0.0)
        triu = jnp.where(upper_mask(length), 1.0, 0.0).astype(F32)
        dld = jnp.dot(triu, dcum, precision=HIGHEST, preferred_element_type=F32)
        gdt = (down / step - rate * dld) * sigmoid(raw)
        gdt_ref[...] = gdt
        hs_ref[...] = jnp.zeros(hs_ref.shape, F32)
        hs_ref[0:1, :] = jnp.sum(-rate * step * dld, axis=0, keepdims=True)
        hs_ref[1:2, :] = jnp.sum(gdt, axis=0, keepdims=True)


PARAMS = pltpu.CompilerParams(vmem_limit_bytes=40 * 1024 * 1024)


def grid_call(kernel, name, steps, in_specs, out_specs, out_shape, scratch=(), into=()):
    given = len(in_specs)
    anywhere = pl.BlockSpec(memory_space=pl.ANY)

    def place(s):
        return s if s.shape[0] == STATE // 2 else pltpu.HBM(s.shape, s.dtype)

    call = pl.pallas_call(
        lambda *refs: kernel(*refs[:given], *refs[given + len(into) :]),
        out_shape=tuple(place(s) for s in out_shape),
        grid=(steps,),
        in_specs=[*in_specs, *[anywhere] * len(into)],
        out_specs=out_specs,
        scratch_shapes=scratch,
        input_output_aliases={given + i: len(out_shape) - len(into) + i for i in range(len(into))},
        compiler_params=PARAMS,
        name=name,
    )

    def run(*values):
        kept = [v if s.memory_space == pltpu.SMEM or v.shape[0] == STATE // 2 else in_hbm(v)
                for v, s in zip(values, in_specs, strict=True)]
        return call(*kept, *[in_hbm(v) for v in into])

    return run


def hop_kernel(has_carry, choices, chunk, side, mine_ref, pair_ref, *refs):
    own, got = choose(refs[:choices], chunk), choose(refs[choices : 2 * choices], chunk)
    refs = refs[2 * choices :]
    if has_carry:
        carry_ref, next_ref, give_ref, keep_ref = refs
        carry = carry_ref[...].astype(F32)
    else:
        next_ref, give_ref, keep_ref = refs
        carry = jnp.zeros(next_ref.shape, F32)
    first = side == 0
    own, got = own.astype(F32), got.astype(F32)
    mine, pair = mine_ref[...], pair_ref[...]
    inner = jnp.where(first, mine, pair) * carry + jnp.where(first, own, got)
    next_ref[...] = (jnp.where(first, pair, mine) * inner + jnp.where(first, got, own)).astype(BF16)
    give_ref[...] = jnp.where(first, inner, carry).astype(BF16)
    keep_ref[...] = jnp.where(first, carry, inner).astype(BF16)


def in_hbm(value):
    return pltpu.with_memory_space_constraint(value, pltpu.HBM)


class Chain:
    def __init__(self, count, rates, sides, flip):
        self.count, self.rates, self.sides, self.flip = count, rates, sides, flip
        self.ranks = lax.axis_size("ctx")
        self.depth = self.ranks // 2
        self.steps = count + self.depth - 1
        self.carry = None

    def physical(self, r):
        return self.ranks - 1 - r if self.flip else r

    def live(self, s):
        return [z for z in range(self.depth) if 0 <= s - z < self.count]

    def swap(self, value, s=None):
        places = range(self.depth) if s is None else self.live(s)
        pairs = [(self.physical(2 * z + p), self.physical(2 * z + 1 - p)) for z in places for p in range(2)]
        return lax.ppermute(value, "ctx", pairs)

    def up(self, value, s):
        live = [z for z in self.live(s) if z + 1 < self.depth]
        pairs = [(self.physical(2 * z + p), self.physical(2 * z + 2 + p)) for z in live for p in range(2)]
        return lax.ppermute(value, "ctx", pairs) if pairs else None

    def step(self, s, owns, gots):
        rows, lanes = gots[0].shape
        owns, gots = owns[: s + 1], gots[: s + 1]
        tile = lanes // 2
        per = lanes // tile
        flat = pl.BlockSpec((rows, tile), lambda i, at: (0, i))
        flip, count = int(self.flip), self.count

        def chunk(at):
            return jnp.clip(s - at[2 + flip], 0, count - 1)

        line = pl.BlockSpec((1, tile), lambda i, at: (0, chunk(at) * per + i))
        carries = [] if self.carry is None else [self.carry]
        operands = [*self.rates, *owns, *gots, *carries]
        after, give, keep = pl.pallas_call(
            lambda at, *refs: hop_kernel(len(carries) > 0, len(owns), chunk(at), at[flip], *refs),
            out_shape=(jax.ShapeDtypeStruct((rows, lanes), BF16),) * 3,
            grid_spec=pltpu.PrefetchScalarGridSpec(
                num_scalar_prefetch=1,
                grid=(per,),
                in_specs=[line, line] + [flat] * (len(operands) - 2),
                out_specs=[flat] * 3,
            ),
            compiler_params=PARAMS,
            name="hop_back" if self.flip else "hop",
        )(self.sides, *operands)
        self.carry = self.up(after, s)
        return keep, self.swap(give, s)

def body(proj_xbc, proj_dt, proj_gate, out_grad, conv_weight, conv_bias, decay_log, step_bias, skip_gain, norm_gain):
    x, dt, gate, og = proj_xbc[0], proj_dt[0], proj_gate[0], out_grad[0]
    length, channels = x.shape
    heads = dt.shape[1]
    inner = heads * HEAD_DIM
    ranks = lax.axis_size("ctx")
    shards = lax.axis_size("fsdp")
    per_group = heads // GROUPS
    width = per_group * HEAD_DIM
    side = lax.axis_index("ctx") % 2
    place = lax.axis_index("ctx") // 2
    sides = jnp.stack([side, 1 - side, place, ranks // 2 - 1 - place]).astype(jnp.int32)
    part = inner // CHUNKS
    per = part // width
    c_loc, g_loc, h_loc = channels // shards, inner // shards, heads // shards
    spare = c_loc - g_loc - 3 * h_loc
    groups = GROUPS
    blocks = channels // width

    ahead = [(i, i + 1) for i in range(ranks - 1)]
    behind = [(i + 1, i) for i in range(ranks - 1)]
    halo = lax.ppermute(x[length - HALO :, :], "ctx", ahead)

    def pack_row(gain, decay, step, skip):
        return jnp.concatenate([gain, decay, step, skip, jnp.zeros(gain.shape[:-1] + (spare,), F32)], axis=-1)

    packed = jnp.concatenate(
        [conv_weight, conv_bias[None], pack_row(norm_gain, decay_log, step_bias, skip_gain)[None],
         jnp.zeros((8 - KERNEL - 2, c_loc), F32)], axis=0)
    full = lax.all_gather(packed, "fsdp", axis=1, tiled=True)
    extra = full[KERNEL + 1].reshape(shards, c_loc)
    gain = extra[:, :g_loc].reshape(1, inner)
    decay = extra[:, g_loc : g_loc + h_loc].reshape(1, heads)
    step_b = extra[:, g_loc + h_loc : g_loc + 2 * h_loc].reshape(1, heads)
    skip = extra[:, g_loc + 2 * h_loc : g_loc + 3 * h_loc].reshape(1, heads)
    skip_x = jnp.repeat(skip, HEAD_DIM, axis=1)

    def spec(shape, where):
        return pl.BlockSpec(shape, where)

    def shape(dims, kind):
        return jax.ShapeDtypeStruct(dims, kind)

    table = spec((length, heads), lambda i: (0, 0))
    row_head = spec((1, heads), lambda i: (0, 0))
    scalars = pl.BlockSpec(memory_space=pltpu.SMEM)
    wide_out = spec((length, width), lambda i: (0, i))
    half_out = spec((STATE // 2, width), lambda i: (0, i))
    window = pltpu.VMEM((PAD + length, width), F32)
    wide_bf, half_bf = shape((length, part), BF16), shape((STATE // 2, part), BF16)
    grad_shapes = (shape((length, channels), BF16), shape((8, channels), F32), shape((8, channels), F32))

    def conv_specs(first):
        return [spec((rows, width), lambda i: (0, first + i)) for rows in (length, HALO, 8)]

    def cols(rows, first):
        return spec((rows, width), lambda i: (0, first + i))

    def head_cols(first):
        return [spec((length, STATE), lambda i: (0, first + i)), spec((length, STATE), lambda i: (0, GROUPS + first + i))]

    kq, ec, ei, et = grid_call(
        lambda *refs: keys_kernel(per_group, *refs), "keys", 2,
        out_shape=(shape((length, 2 * width), BF16), shape((length, heads), F32), shape((length, heads), F32),
                   shape((1, inner), F32)),
        in_specs=conv_specs(GROUPS) + [table, row_head, row_head],
        out_specs=(wide_out, table, table, spec((1, inner), lambda i: (0, 0))),
        scratch=[window],
    )(x, halo, full, dt, step_b, decay)
    rates = (et, lax.ppermute(et, "ctx", [(i, i ^ 1) for i in range(ranks)]))

    def front(c):
        first = c * per
        return grid_call(
            lambda *refs: front_kernel(per_group, first, *refs), "front", per,
            out_shape=(wide_bf, wide_bf, half_bf, half_bf),
            in_specs=conv_specs(first) + head_cols(first)[:1] + [table, cols(1, first), scalars],
            out_specs=(wide_out, wide_out, half_out, half_out),
            scratch=[window],
        )(x, halo, full, kq, ei, et, sides)

    def middle(c):
        first = c * per
        near = starts[c : c + depth]
        return grid_call(
            lambda *refs: middle_kernel(per_group, first, depth, *refs), "middle", per,
            out_shape=(wide_bf, wide_bf, shape((STATE, part), BF16), half_bf, half_bf, shape((length, heads), F32),
                       shape((length, inner), BF16), shape((8, inner), F32)),
            in_specs=[wide_out, *head_cols(first), wide_out, table, cols(length, first), cols(length, first),
                      cols(1, first), cols(1, first), scalars] + [half_out] * (2 * depth),
            out_specs=(wide_out, wide_out, spec((STATE, width), lambda i: (0, i)), half_out, half_out, table,
                       cols(length, first), cols(8, first)),
            into=mids[-1][6:] if mids else (),
        )(fronts[c][0], kq, kq, fronts[c][1], ec, gate, og, gain, skip_x, sides,
          *[n[0] for n in near], *[n[1] for n in near])

    def back(c):
        first = c * per
        near = ends[c : c + depth]
        dy, dyp, st = mids[c][:3]
        return grid_call(
            lambda *refs: back_kernel(per_group, first, depth, *refs), "back", per,
            out_shape=(shape((2, length, per * STATE), F32), shape((length, heads), F32), shape((8, heads), F32),
                       *grad_shapes),
            in_specs=[*head_cols(first), wide_out, spec((STATE, width), lambda i: (0, i)), wide_out, wide_out,
                      *conv_specs(first), cols(1, first), cols(1, first), table, scalars] + [half_out] * (2 * depth),
            out_specs=(spec((2, length, STATE), lambda i: (0, 0, i)), table, spec((8, heads), lambda i: (0, 0)),
                       cols(length, first), cols(8, first), cols(8, first)),
            scratch=[window, window],
            into=backs[-1][3:] if backs else (),
        )(kq, kq, fronts[c][1], st, dy, dyp, x, halo, full, skip_x, et, ei, sides,
          *[n[0] for n in near], *[n[1] for n in near])

    fore, aft = Chain(CHUNKS, rates, sides, False), Chain(CHUNKS, rates, sides, True)
    depth, steps = fore.depth, fore.steps
    fronts, mids, backs, starts, ends, got, got_back = [], [], [], [], [], [], []
    for u in range(CHUNKS + 2 * depth + 1):
        if u < CHUNKS:
            fronts.append(front(u))
            got.append(fore.swap(fronts[u][3]))
        if u < steps:
            starts.append(fore.step(u, [f[2] for f in fronts], got))
        if depth <= u < depth + CHUNKS:
            mids.append(middle(u - depth))
            got_back.append(fore.swap(mids[-1][4]))
        if depth + 1 <= u < depth + 1 + steps:
            ends.append(aft.step(u - depth - 1, [m[3] for m in mids], got_back))
        if u >= 2 * depth + 1:
            backs.append(back(u - 2 * depth - 1))

    grad_dt, hs, gx, edge, wr = grid_call(
        lambda *refs: last_kernel(CHUNKS, *refs), "last", 2,
        out_shape=(shape((length, heads), F32), shape((8, heads), F32), *grad_shapes),
        in_specs=conv_specs(GROUPS) + [table, row_head, row_head]
        + [spec((1, length, per * STATE), lambda i: (i, 0, 0))] * CHUNKS + [table] * (2 * CHUNKS)
        + [spec((8, heads), lambda i: (0, 0))] * CHUNKS,
        out_specs=(table, spec((8, heads), lambda i: (0, 0)), cols(length, GROUPS), cols(8, GROUPS), cols(8, GROUPS)),
        scratch=[window, window],
        into=backs[-1][3:],
    )(x, halo, full, dt, step_b, decay, *[b[0] for b in backs], *[m[5] for m in mids], *[b[1] for b in backs],
      *[b[2] for b in backs])
    grad_gate, sums = mids[-1][6:]

    next_gp = lax.ppermute(edge[:HALO], "ctx", behind)
    fixed = []
    for i in range(HALO):
        row = edge[HALO + i]
        for k in range(i + 1):
            row = row + full[k] * next_gp[i - k]
        fixed.append(row)
    grad_xbc = lax.dynamic_update_slice(gx, jnp.stack(fixed).astype(BF16), (length - HALO, 0))

    skip_grad = jnp.sum(sums[1].reshape(heads, HEAD_DIM), axis=1)
    extra_row = pack_row(
        sums[0].reshape(shards, g_loc), hs[0].reshape(shards, h_loc), hs[1].reshape(shards, h_loc),
        skip_grad.reshape(shards, h_loc)).reshape(1, channels)
    parts = jnp.concatenate([wr[: KERNEL + 1], extra_row, jnp.zeros((8 - KERNEL - 2, channels), F32)], axis=0)
    split = ranks // 8
    piece = c_loc // split
    parts = parts.reshape(8, shards, split, piece).transpose(0, 2, 1, 3).reshape(ranks * shards, piece)
    summed = jnp.sum(lax.all_to_all(parts, ("ctx", "fsdp"), 0, 0, tiled=True), axis=0)
    summed = summed * (1.0 / math.sqrt(length * ranks * shards))
    copies = jnp.broadcast_to(summed[None], (ranks, piece))
    mine = lax.all_to_all(copies, "ctx", 0, 0, tiled=True).reshape(8, c_loc)
    tail = mine[KERNEL + 1]
    return (
        grad_xbc[None],
        grad_dt[None],
        grad_gate[None],
        mine[:KERNEL],
        mine[KERNEL],
        tail[g_loc : g_loc + h_loc],
        tail[g_loc + h_loc : g_loc + 2 * h_loc],
        tail[g_loc + 2 * h_loc : g_loc + 3 * h_loc],
        tail[:g_loc],
    )


def solution(mesh):
    data = P("fsdp", "ctx", None)
    one = P("fsdp")
    return jax.shard_map(
        body,
        mesh=mesh,
        in_specs=(data, data, data, data, P(None, "fsdp"), one, one, one, one, one),
        out_specs=(data, data, data, P(None, "fsdp"), one, one, one, one, one),
        check_vma=False,
    )
```

time: 295 us -> 257 us (0.87)
  waiting for transfers between devices: 92.1 us -> 50.2 us
  Pallas kernels: 66.4 us -> 102 us
  local copies, waits for them, and re-layouts: 36.9 us -> 18.8 us
  starting transfers between devices: 81.4 us -> 72.6 us
  other arithmetic: 8.29 us -> 4.37 us
    pallas_call x5 -> x28, Pallas kernels: 66.4 us -> 102 us  [the longest x14 74.5 us: run(): return call(*kept, *[in_hbm(v) for v in into])]
    ppermute x12, waiting for transfers between devices: 60.5 us -> 26.4 us  [up(): return lax.ppermute(value, 'ctx', pairs) if pairs else None]
    pallas_call x12 -> x0, local copies, waits for them, and re-layouts: 16.8 us -> none  [chain_states(): pl.pallas_call(lambda *refs, has_carry=has_carry: hop_kernel(has_carry, *...]
    ppermute x28 -> x22, starting transfers between devices: 49.5 us -> 37.8 us  [swap(): return lax.ppermute(value, 'ctx', pairs)]
    ppermute x28 -> x22, waiting for transfers between devices: 15.2 us -> 6.7 us  [swap(): return lax.ppermute(value, 'ctx', pairs)]
    another operation x14 -> x0, other arithmetic: 6.5 us -> none  [chain_states(): at = jnp.stack([jnp.clip(s - place, 0, count - 1), side]).astype(jnp.int32)]
    unnamed x98 -> x20, local copies, waits for them, and re-layouts: 8.1 us -> 3.59 us
  transfers between devices with their start and end apart: 45 -> 39, of which waited for: 14 -> 10; matrix products, arithmetic and copies ran while one was open for 10% -> 5% of each run, Pallas kernels for 1% -> 30%
where the time goes in v2:
time: 257 us; the launch traced here: 255 us
  Pallas kernels  102 us (40%)
  starting transfers between devices  72.6 us (28%)
  waiting for transfers between devices  50.2 us (20%)
  local copies, waits for them, and re-layouts  18.8 us (7%)
  blocking collectives  6.12 us (2%)
  other arithmetic  4.37 us (2%)
    pallas_call x14, Pallas kernels, run(): return call(*kept, *[in_hbm(v) for v in into])  74.5 us
    ppermute x22, starting transfers between devices, swap(): return lax.ppermute(value, 'ctx', pairs)  37.8 us
    pallas_call x14, Pallas kernels, step(): pl.pallas_call(lambda at, *refs: hop_kernel(len(carries) > 0, len(owns),...  27.2 us
    ppermute x12, waiting for transfers between devices, up(): return lax.ppermute(value, 'ctx', pairs) if pairs else None  26.4 us
    ppermute x12, starting transfers between devices, up(): return lax.ppermute(value, 'ctx', pairs) if pairs else None  19 us
    all_to_all x1, waiting for transfers between devices, body(): lax.all_to_all(parts, ('ctx', 'fsdp'), 0, 0, tiled=True)  10.1 us
    ppermute x22, waiting for transfers between devices, swap(): return lax.ppermute(value, 'ctx', pairs)  6.7 us
    all_gather x1, blocking collectives, body(): full = lax.all_gather(packed, 'fsdp', axis=1, tiled=True)  6.12 us
  transfers between devices with their start and end apart: 39, of which 10 were waited for; matrix products, arithmetic and copies ran while one was open for 5% of the time, Pallas kernels for 30%

profile of v2, /device:TPU:0, one launch (start us, length us, event | category | flops | bytes accessed | tf_op | source)
XLA Modules:
  0.0 255.0 jit_solution(12574450158734631491)
XLA Ops:
  1.6 4.8 %collective-permute-start = (bf16[3,10240]{1,0:T(4,128)(2,1)S(1)}, bf16[3,10240]{1,0:T(4,128)(2,1)S(1)}, u32[]{:S(2)}, u32[]{:S(2)}) collective-permute-start(bf16[3,10240]{1,0:T(4,128)(2,1)S(1)} %slice_bitcast_fusion), channel_id=1, source_target_pairs={{0,4},{4,8},{8,12},{12,16},{16,20},{20,24},{24,28},{1,5},{5,9},{9,... | collective-permute-start | bytes 184328 | tf_op jit(solution)/shard_map/ppermute | solution.py:381
  8.9 6.1 %all_gather.3.refs_2_.refs_8_ = f32[8,10240]{1,0:T(8,128)S(1)} all-gather(f32[8,2560]{1,0:T(8,128)S(1)} %maximum_maximum_fusion.1), channel_id=1, replica_groups=mesh['ctx'=8,'fsdp'=4] {'fsdp'}, dimensions={1}, use_global_device_ids=true | all-gather | bytes 409600 | tf_op jit(solution)/shard_map/all_gather | solution.py:389
  17.2 3.6 %keys.1 = (bf16[128,2048]{1,0:T(8,128)(2,1)}, f32[128,128]{1,0:T(8,128)}, f32[128,128]{1,0:T(8,128)}, f32[1,8192]{1,0:T(1,128)}) custom-call(bf16[128,10240]{1,0:T(8,128)(2,1)} %bitcast.39, bf16[3,10240]{1,0:T(4,128)(2,1)} %copy-done.5, f32[8,10240]{1,0:T(8,128)} %copy-done.4, bf16[128,128]{1,0:T(8,128)(2,1)} %bitcast.66, f32[1,128]{1,0:T(1,128)} %reshape.110.refs_4_, ...), custom_call_target="tpu_custom_call" | custom-call | tf_op jit(solution)/shard_map/keys/pallas_call | solution.py:280
  20.8 3.8 %front.4 = (bf16[128,2048]{1,0:T(8,128)(2,1)}, bf16[128,2048]{1,0:T(8,128)(2,1)}, bf16[64,2048]{1,0:T(8,128)(2,1)S(1)}, bf16[64,2048]{1,0:T(8,128)(2,1)S(1)}) custom-call(bf16[128,10240]{1,0:T(8,128)(2,1)} %bitcast.40, bf16[3,10240]{1,0:T(4,128)(2,1)} %copy-done.5, f32[8,10240]{1,0:T(8,128)} %copy-done.4, ...), custom_call_target="tpu_custom_call" | custom-call | tf_op jit(solution)/shard_map/front/pallas_call | solution.py:280
  24.6 1.5 collective-permute-start.2
  26.7 3.8 %front.5 = (bf16[128,2048]{1,0:T(8,128)(2,1)}, bf16[128,2048]{1,0:T(8,128)(2,1)}, bf16[64,2048]{1,0:T(8,128)(2,1)S(1)}, bf16[64,2048]{1,0:T(8,128)(2,1)S(1)}) custom-call(bf16[128,10240]{1,0:T(8,128)(2,1)} %bitcast.41, bf16[3,10240]{1,0:T(4,128)(2,1)} %copy-done.5, f32[8,10240]{1,0:T(8,128)} %copy-done.4, ...), custom_call_target="tpu_custom_call" | custom-call | tf_op jit(solution)/shard_map/front/pallas_call | solution.py:280
  30.5 1.5 collective-permute-start.3
  32.0 2.4 collective-permute-done.1.refs_1_
  34.5 1.5 hop.7
  36.0 3.5 %collective-permute-start.4 = (bf16[64,2048]{1,0:T(8,128)(2,1)S(1)}, bf16[64,2048]{1,0:T(8,128)(2,1)S(1)}, u32[]{:S(2)}, u32[]{:S(2)}) collective-permute-start(bf16[64,2048]{1,0:T(8,128)(2,1)S(1)} %get-tuple-element.141), channel_id=1, source_target_pairs={{0,8},{4,12},{1,9},{5,13},{2,10},{6,14},{3,11},{7,15}} | collective-permute-start | bytes 786440 | tf_op jit(solution)/shard_map/ppermute | solution.py:329
  39.5 3.8 %front.6 = (bf16[128,2048]{1,0:T(8,128)(2,1)}, bf16[128,2048]{1,0:T(8,128)(2,1)}, bf16[64,2048]{1,0:T(8,128)(2,1)S(1)}, bf16[64,2048]{1,0:T(8,128)(2,1)S(1)}) custom-call(bf16[128,10240]{1,0:T(8,128)(2,1)} %bitcast.42, bf16[3,10240]{1,0:T(4,128)(2,1)} %copy-done.5, f32[8,10240]{1,0:T(8,128)} %copy-done.4, ...), custom_call_target="tpu_custom_call" | custom-call | tf_op jit(solution)/shard_map/front/pallas_call | solution.py:280
  43.4 1.5 collective-permute-start.5
  44.9 1.6 hop.8
  46.6 3.7 %collective-permute-start.6 = (bf16[64,2048]{1,0:T(8,128)(2,1)S(1)}, bf16[64,2048]{1,0:T(8,128)(2,1)S(1)}, u32[]{:S(2)}, u32[]{:S(2)}) collective-permute-start(bf16[64,2048]{1,0:T(8,128)(2,1)S(1)} %get-tuple-element.145), channel_id=1, source_target_pairs={{0,8},{4,12},{8,16},{12,20},{1,9},{5,13},{9,17},{13,21},{2,10},{6,... | collective-permute-start | bytes 786440 | tf_op jit(solution)/shard_map/ppermute | solution.py:329
  50.2 3.9 %front.7 = (bf16[128,2048]{1,0:T(8,128)(2,1)}, bf16[128,2048]{1,0:T(8,128)(2,1)}, bf16[64,2048]{1,0:T(8,128)(2,1)S(1)}, bf16[64,2048]{1,0:T(8,128)(2,1)}) custom-call(bf16[128,10240]{1,0:T(8,128)(2,1)} %bitcast.43, bf16[3,10240]{1,0:T(4,128)(2,1)} %copy-done.5, f32[8,10240]{1,0:T(8,128)} %copy-done.4, ...), custom_call_target="tpu_custom_call" | custom-call | tf_op jit(solution)/shard_map/front/pallas_call | solution.py:280
  54.1 1.6 collective-permute-start.7
  55.7 2.2 hop.9
  58.6 2.7 %collective-permute-start.8 = (bf16[64,2048]{1,0:T(8,128)(2,1)}, bf16[64,2048]{1,0:T(8,128)(2,1)S(1)}, u32[]{:S(2)}, u32[]{:S(2)}) collective-permute-start(bf16[64,2048]{1,0:T(8,128)(2,1)} %get-tuple-element.149), channel_id=1, source_target_pairs={{0,8},{4,12},{8,16},{12,20},{16,24},{20,28},{1,9},{5,13},{9,17},{1... | collective-permute-start | bytes 786440 | tf_op jit(solution)/shard_map/ppermute | solution.py:329
  63.5 3.4 %collective-permute-start.9 = (bf16[64,2048]{1,0:T(8,128)(2,1)S(1)}, bf16[64,2048]{1,0:T(8,128)(2,1)S(1)}, u32[]{:S(2)}, u32[]{:S(2)}) collective-permute-start(bf16[64,2048]{1,0:T(8,128)(2,1)S(1)} %get-tuple-element.151), channel_id=1, source_target_pairs={{0,4},{4,0},{1,5},{5,1},{2,6},{6,2},{3,7},{7,3}} | collective-permute-start | bytes 786440 | tf_op jit(solution)/shard_map/ppermute | solution.py:324
  66.9 2.4 collective-permute-start.10
  69.3 3.5 %collective-permute-start.11 = (bf16[64,2048]{1,0:T(8,128)(2,1)}, bf16[64,2048]{1,0:T(8,128)(2,1)S(1)}, u32[]{:S(2)}, u32[]{:S(2)}) collective-permute-start(bf16[64,2048]{1,0:T(8,128)(2,1)} %copy-done.3), channel_id=1, source_target_pairs={{0,4},{4,0},{8,12},{12,8},{16,20},{20,16},{1,5},{5,1},{9,13},{13,9... | collective-permute-start | bytes 786440 | tf_op jit(solution)/shard_map/ppermute | solution.py:324
  72.8 1.7 hop.10
  74.5 1.3 collective-permute-start.14
  77.0 2.7 %collective-permute-done.14.refs_10_ = bf16[64,2048]{1,0:T(8,128)(2,1)S(1)} collective-permute-done((bf16[64,2048]{1,0:T(8,128)(2,1)S(1)}, bf16[64,2048]{1,0:T(8,128)(2,1)S(1)}, u32[]{:S(2)}, u32[]{:S(2)}) %collective-permute-start.14) | collective-permute-done | bytes 262176 | tf_op jit(solution)/shard_map/ppermute | solution.py:329
  79.6 1.7 hop.11
  82.7 2.1 collective-permute-done.11.refs_16_.refs_15_.refs_14_
  84.8 2.8 %collective-permute-done.12.refs_17_.refs_16_.refs_15_.refs_14_ = bf16[64,2048]{1,0:T(8,128)(2,1)S(1)} collective-permute-done((bf16[64,2048]{1,0:T(8,128)(2,1)S(1)}, bf16[64,2048]{1,0:T(8,128)(2,1)S(1)}, u32[]{:S(2)}, u32[]{:S(2)}) %collective-permute-start.12) | collective-permute-done | bytes 262176 | tf_op jit(solution)/shard_map/ppermute | solution.py:324
  87.6 5.2 %middle.4 = (bf16[128,2048]{1,0:T(8,128)(2,1)}, bf16[128,2048]{1,0:T(8,128)(2,1)}, bf16[128,2048]{1,0:T(8,128)(2,1)}, bf16[64,2048]{1,0:T(8,128)(2,1)S(1)}, bf16...) custom-call(bf16[128,2048]{1,0:T(8,128)(2,1)} %get-tuple-element.134.refs_0_, ...), custom_call_target="tpu_custom_call" | custom-call | tf_op jit(solution)/shard_map/middle/pallas_call | solution.py:280
  93.9 1.7 hop.12
  97.1 5.3 %middle.5 = (bf16[128,2048]{1,0:T(8,128)(2,1)}, bf16[128,2048]{1,0:T(8,128)(2,1)}, bf16[128,2048]{1,0:T(8,128)(2,1)}, bf16[64,2048]{1,0:T(8,128)(2,1)S(1)}, bf16...) custom-call(bf16[128,2048]{1,0:T(8,128)(2,1)} %get-tuple-element.161, ...), custom_call_target="tpu_custom_call", output_to_operand_aliasing={{6}: (18, {}), {7}: (19, {})} | custom-call | tf_op jit(solution)/shard_map/middle/pallas_call | solution.py:280
  103.5 1.5 hop_back.7
  105.8 2.2 hop.13
  108.7 5.3 %middle.6 = (bf16[128,2048]{1,0:T(8,128)(2,1)}, bf16[128,2048]{1,0:T(8,128)(2,1)}, bf16[128,2048]{1,0:T(8,128)(2,1)}, bf16[64,2048]{1,0:T(8,128)(2,1)S(1)}, bf16...) custom-call(bf16[128,2048]{1,0:T(8,128)(2,1)} %get-tuple-element.172, ...), custom_call_target="tpu_custom_call", output_to_operand_aliasing={{6}: (18, {}), {7}: (19, {})} | custom-call | tf_op jit(solution)/shard_map/middle/pallas_call | solution.py:280
  115.0 1.6 hop_back.8
  117.3 5.3 %middle.7 = (bf16[128,2048]{1,0:T(8,128)(2,1)}, bf16[128,2048]{1,0:T(8,128)(2,1)}, bf16[128,2048]{1,0:T(8,128)(2,1)}, bf16[64,2048]{1,0:T(8,128)(2,1)S(1)}, bf16...) custom-call(bf16[128,2048]{1,0:T(8,128)(2,1)} %get-tuple-element.183, ...), custom_call_target="tpu_custom_call", output_to_operand_aliasing={{6}: (18, {}), {7}: (19, {})} | custom-call | tf_op jit(solution)/shard_map/middle/pallas_call | solution.py:280
  123.7 2.3 hop_back.9
  126.0 1.3 collective-permute-start.25
  127.3 1.8 collective-permute-done.24.refs_9_
  129.0 5.5 %collective-permute-done.25.refs_10_ = bf16[64,2048]{1,0:T(8,128)(2,1)S(1)} collective-permute-done((bf16[64,2048]{1,0:T(8,128)(2,1)S(1)}, bf16[64,2048]{1,0:T(8,128)(2,1)S(1)}, u32[]{:S(2)}, u32[]{:S(2)}) %collective-permute-start.25) | collective-permute-done | bytes 262176 | tf_op jit(solution)/shard_map/ppermute | solution.py:329
  134.6 2.3 hop_back.10
  136.9 1.3 collective-permute-start.30
  138.2 9.3 %collective-permute-done.30.refs_10_ = bf16[64,2048]{1,0:T(8,128)(2,1)S(1)} collective-permute-done((bf16[64,2048]{1,0:T(8,128)(2,1)S(1)}, bf16[64,2048]{1,0:T(8,128)(2,1)S(1)}, u32[]{:S(2)}, u32[]{:S(2)}) %collective-permute-start.30) | collective-permute-done | bytes 262176 | tf_op jit(solution)/shard_map/ppermute | solution.py:329
  147.5 2.3 hop_back.11
  149.8 1.3 collective-permute-start.32
  151.8 8.8 %collective-permute-done.32.refs_10_ = bf16[64,2048]{1,0:T(8,128)(2,1)S(1)} collective-permute-done((bf16[64,2048]{1,0:T(8,128)(2,1)S(1)}, bf16[64,2048]{1,0:T(8,128)(2,1)S(1)}, u32[]{:S(2)}, u32[]{:S(2)}) %collective-permute-start.32) | collective-permute-done | bytes 262176 | tf_op jit(solution)/shard_map/ppermute | solution.py:329
  160.5 2.3 hop_back.12
  162.8 1.3 collective-permute-start.34
  165.5 3.6 %collective-permute-start.29 = (bf16[64,2048]{1,0:T(8,128)(2,1)}, bf16[64,2048]{1,0:T(8,128)(2,1)S(1)}, u32[]{:S(2)}, u32[]{:S(2)}) collective-permute-start(bf16[64,2048]{1,0:T(8,128)(2,1)} %get-tuple-element.197), channel_id=1, source_target_pairs={{28,24},{24,28},{20,16},{16,20},{12,8},{8,12},{4,0},{0,4},{29,25},... | collective-permute-start | bytes 786440 | tf_op jit(solution)/shard_map/ppermute | solution.py:324
  169.1 1.9 collective-permute-start.31
  171.1 5.5 %collective-permute-start.33 = (bf16[64,2048]{1,0:T(8,128)(2,1)}, bf16[64,2048]{1,0:T(8,128)(2,1)S(1)}, u32[]{:S(2)}, u32[]{:S(2)}) collective-permute-start(bf16[64,2048]{1,0:T(8,128)(2,1)} %get-tuple-element.214), channel_id=1, source_target_pairs={{12,8},{8,12},{4,0},{0,4},{13,9},{9,13},{5,1},{1,5},{14,10},{10,14... | collective-permute-start | bytes 786440 | tf_op jit(solution)/shard_map/ppermute | solution.py:324
  176.5 2.3 hop_back.13
  178.8 2.1 collective-permute-start.35
  183.5 7.0 %back.4 = (f32[2,128,256]{2,1,0:T(8,128)}, f32[128,128]{1,0:T(8,128)}, f32[8,128]{1,0:T(8,128)}, bf16[128,10240]{1,0:T(8,128)(2,1)}, f32[8,10240]{1,0:T(8,128)}, /*index=5*/f32[8,10240]{1,0:T(8,128)}) custom-call(bf16[128,2048]{1,0:T(8,128)(2,1)} %get-tuple-element.130.refs_3_.refs_1_.refs_2_.refs_0_, ...), custom_call_target="tpu_custom_call" | custom-call | tf_op jit(solution)/shard_map/back/pallas_call | solution.py:280
  190.5 7.1 %back.5 = (f32[2,128,256]{2,1,0:T(8,128)}, f32[128,128]{1,0:T(8,128)}, f32[8,128]{1,0:T(8,128)}, bf16[128,10240]{1,0:T(8,128)(2,1)}, f32[8,10240]{1,0:T(8,128)}, /*index=5*/f32[8,10240]{1,0:T(8,128)}) custom-call(bf16[128,2048]{1,0:T(8,128)(2,1)} %get-tuple-element.130.refs_3_.refs_1_.refs_2_.refs_0_, ...), custom_call_target="tpu_custom_call", output_to_operand_aliasing={{3}: (21, {}), {4}: (22, {}), {5}: (23, {})} | custom-call | tf_op jit(solution)/shard_map/back/pallas_call | solution.py:280
  197.6 7.1 %back.6 = (f32[2,128,256]{2,1,0:T(8,128)}, f32[128,128]{1,0:T(8,128)}, f32[8,128]{1,0:T(8,128)}, bf16[128,10240]{1,0:T(8,128)(2,1)}, f32[8,10240]{1,0:T(8,128)}, /*index=5*/f32[8,10240]{1,0:T(8,128)}) custom-call(bf16[128,2048]{1,0:T(8,128)(2,1)} %get-tuple-element.130.refs_3_.refs_1_.refs_2_.refs_0_, ...), custom_call_target="tpu_custom_call", output_to_operand_aliasing={{3}: (21, {}), {4}: (22, {}), {5}: (23, {})} | custom-call | tf_op jit(solution)/shard_map/back/pallas_call | solution.py:280
  204.7 7.1 %back.7 = (f32[2,128,256]{2,1,0:T(8,128)}, f32[128,128]{1,0:T(8,128)}, f32[8,128]{1,0:T(8,128)}, bf16[128,10240]{1,0:T(8,128)(2,1)}, f32[8,10240]{1,0:T(8,128)}, /*index=5*/f32[8,10240]{1,0:T(8,128)}) custom-call(bf16[128,2048]{1,0:T(8,128)(2,1)} %get-tuple-element.130.refs_3_.refs_1_.refs_2_.refs_0_, ...), custom_call_target="tpu_custom_call", output_to_operand_aliasing={{3}: (21, {}), {4}: (22, {}), {5}: (23, {})} | custom-call | tf_op jit(solution)/shard_map/back/pallas_call | solution.py:280
  211.8 6.1 %last.1 = (f32[128,128]{1,0:T(8,128)}, f32[8,128]{1,0:T(8,128)}, bf16[128,10240]{1,0:T(8,128)(2,1)}, f32[8,10240]{1,0:T(8,128)}, f32[8,10240]{1,0:T(8,128)}) custom-call(bf16[128,10240]{1,0:T(8,128)(2,1)} %bitcast.48, bf16[3,10240]{1,0:T(4,128)(2,1)} %copy-done.5, ...), custom_call_target="tpu_custom_call", output_to_operand_aliasing={{2}: (22, {}), {3}: (23, {}), {4}: (24, {})} | custom-call | tf_op jit(solution)/shard_map/last/pallas_call | solution.py:280
  220.1 1.3 collective-permute-start.36
  223.6 5.8 %all-to-all-start = ((f32[32,1,2560]{2,1,0:T(1,128)}), f32[32,1,2560]{2,1,0:T(1,128)S(1)}, u32[]{:S(2)}, u32[]{:S(2)}) async-start(f32[32,1,2560]{2,1,0:T(1,128)} %all_to_all.13), calls=%async_computation | async-start | bytes 655360 | tf_op jit(solution)/shard_map/all_to_all | solution.py:520
  229.4 1.9 convert_bitcast_fusion.2
  231.3 10.1 %all-to-all-done = f32[32,1,2560]{2,1,0:T(1,128)S(1)} async-done(((f32[32,1,2560]{2,1,0:T(1,128)}), f32[32,1,2560]{2,1,0:T(1,128)S(1)}, u32[]{:S(2)}, u32[]{:S(2)}) %all-to-all-start) | async-done | bytes 327712 | tf_op jit(solution)/shard_map/all_to_all | solution.py:520
  242.2 3.4 %all-to-all-start.1 = ((f32[8,1,2560]{2,1,0:T(1,128)}), f32[8,1,2560]{2,1,0:T(1,128)S(1)}, u32[]{:S(2)}, u32[]{:S(2)}) async-start(f32[8,1,2560]{2,1,0:T(1,128)} %broadcast_in_dim.49), calls=%async_computation.1 | async-start | bytes 163840 | tf_op jit(solution)/shard_map/all_to_all | solution.py:523
  245.7 2.1 dynamic_update_slice.4
  247.9 4.7 %all-to-all-done.1 = f32[8,1,2560]{2,1,0:T(1,128)S(1)} async-done(((f32[8,1,2560]{2,1,0:T(1,128)}), f32[8,1,2560]{2,1,0:T(1,128)S(1)}, u32[]{:S(2)}, u32[]{:S(2)}) %all-to-all-start.1) | async-done | bytes 81952 | tf_op jit(solution)/shard_map/all_to_all | solution.py:523
  (103 shorter events, 31.5 us)
Async XLA Ops:
  1.6 14.9 %collective-permute-start = (bf16[3,10240]{1,0:T(4,128)(2,1)S(1)}, bf16[3,10240]{1,0:T(4,128)(2,1)S(1)}, u32[]{:S(2)}, u32[]{:S(2)}) collective-permute-start(bf16[3,10240]{1,0:T(4,128)(2,1)S(1)} %slice_bitcast_fusion), channel_id=1, source_target_pairs={{0,4},{4,8},{8,12},{12,16},{16,20},{20,24},{24,28},{1,5},{5,9},{9,... | collective-permute-start | bytes 184328 | tf_op jit(solution)/shard_map/ppermute | solution.py:381
  8.1 7.0 %copy-start.6 = (f32[8]{0:T(128)}, f32[8]{0:T(128)S(1)}, u32[]{:S(2)}) copy-start(f32[8]{0:T(128)S(1)} %pad.13.clone) | copy-start | bytes 100
  15.1 1.5 copy-start.4
  16.5 0.6 copy-start.5
  24.6 9.8 %collective-permute-start.2 = (bf16[64,2048]{1,0:T(8,128)(2,1)S(1)}, bf16[64,2048]{1,0:T(8,128)(2,1)S(1)}, u32[]{:S(2)}, u32[]{:S(2)}) collective-permute-start(bf16[64,2048]{1,0:T(8,128)(2,1)S(1)} %get-tuple-element.137), channel_id=1, source_target_pairs={{0,4},{4,0},{8,12},{12,8},{16,20},{20,16},{24,28},{28,24},{1,5},{5... | collective-permute-start | bytes 786440 | tf_op jit(solution)/shard_map/ppermute | solution.py:324
  26.2 8.3 %collective-permute-start.1 = (f32[1,8192]{1,0:T(1,128)}, f32[1,8192]{1,0:T(1,128)S(1)}, u32[]{:S(2)}, u32[]{:S(2)}) collective-permute-start(f32[1,8192]{1,0:T(1,128)} %get-tuple-element.132.refs_5_.refs_0_.refs_10_), channel_id=1, source_target_pairs={{0,4},{4,0},{8,12},{12,8},{16,20},{20,16},{24,28},{28,24},{1,5},{5... | collective-permute-start | bytes 98312 | tf_op jit(solution)/shard_map/ppermute | solution.py:429
  30.5 14.4 %collective-permute-start.3 = (bf16[64,2048]{1,0:T(8,128)(2,1)S(1)}, bf16[64,2048]{1,0:T(8,128)(2,1)S(1)}, u32[]{:S(2)}, u32[]{:S(2)}) collective-permute-start(bf16[64,2048]{1,0:T(8,128)(2,1)S(1)} %get-tuple-element.140), channel_id=1, source_target_pairs={{0,4},{4,0},{8,12},{12,8},{16,20},{20,16},{24,28},{28,24},{1,5},{5... | collective-permute-start | bytes 786440 | tf_op jit(solution)/shard_map/ppermute | solution.py:324
  36.0 8.9 %collective-permute-start.4 = (bf16[64,2048]{1,0:T(8,128)(2,1)S(1)}, bf16[64,2048]{1,0:T(8,128)(2,1)S(1)}, u32[]{:S(2)}, u32[]{:S(2)}) collective-permute-start(bf16[64,2048]{1,0:T(8,128)(2,1)S(1)} %get-tuple-element.141), channel_id=1, source_target_pairs={{0,8},{4,12},{1,9},{5,13},{2,10},{6,14},{3,11},{7,15}} | collective-permute-start | bytes 786440 | tf_op jit(solution)/shard_map/ppermute | solution.py:329
  43.4 12.4 %collective-permute-start.5 = (bf16[64,2048]{1,0:T(8,128)(2,1)S(1)}, bf16[64,2048]{1,0:T(8,128)(2,1)S(1)}, u32[]{:S(2)}, u32[]{:S(2)}) collective-permute-start(bf16[64,2048]{1,0:T(8,128)(2,1)S(1)} %get-tuple-element.144), channel_id=1, source_target_pairs={{0,4},{4,0},{8,12},{12,8},{16,20},{20,16},{24,28},{28,24},{1,5},{5... | collective-permute-start | bytes 786440 | tf_op jit(solution)/shard_map/ppermute | solution.py:324
  46.6 7.6 %copy-start.2 = (bf16[64,2048]{1,0:T(8,128)(2,1)}, bf16[64,2048]{1,0:T(8,128)(2,1)S(1)}, u32[]{:S(2)}) copy-start(bf16[64,2048]{1,0:T(8,128)(2,1)S(1)} %get-tuple-element.152) | copy-start | bytes 786436
  46.6 9.2 %collective-permute-start.6 = (bf16[64,2048]{1,0:T(8,128)(2,1)S(1)}, bf16[64,2048]{1,0:T(8,128)(2,1)S(1)}, u32[]{:S(2)}, u32[]{:S(2)}) collective-permute-start(bf16[64,2048]{1,0:T(8,128)(2,1)S(1)} %get-tuple-element.145), channel_id=1, source_target_pairs={{0,8},{4,12},{8,16},{12,20},{1,9},{5,13},{9,17},{13,21},{2,10},{6,... | collective-permute-start | bytes 786440 | tf_op jit(solution)/shard_map/ppermute | solution.py:329
  54.1 18.7 %collective-permute-start.7 = (bf16[64,2048]{1,0:T(8,128)(2,1)}, bf16[64,2048]{1,0:T(8,128)(2,1)S(1)}, u32[]{:S(2)}, u32[]{:S(2)}) collective-permute-start(bf16[64,2048]{1,0:T(8,128)(2,1)} %get-tuple-element.148), channel_id=1, source_target_pairs={{0,4},{4,0},{8,12},{12,8},{16,20},{20,16},{24,28},{28,24},{1,5},{5... | collective-permute-start | bytes 786440 | tf_op jit(solution)/shard_map/ppermute | solution.py:324
  57.9 0.7 copy-start.3
  58.6 14.1 %collective-permute-start.8 = (bf16[64,2048]{1,0:T(8,128)(2,1)}, bf16[64,2048]{1,0:T(8,128)(2,1)S(1)}, u32[]{:S(2)}, u32[]{:S(2)}) collective-permute-start(bf16[64,2048]{1,0:T(8,128)(2,1)} %get-tuple-element.149), channel_id=1, source_target_pairs={{0,8},{4,12},{8,16},{12,20},{16,24},{20,28},{1,9},{5,13},{9,17},{1... | collective-permute-start | bytes 786440 | tf_op jit(solution)/shard_map/ppermute | solution.py:329
  63.5 18.6 %collective-permute-start.9 = (bf16[64,2048]{1,0:T(8,128)(2,1)S(1)}, bf16[64,2048]{1,0:T(8,128)(2,1)S(1)}, u32[]{:S(2)}, u32[]{:S(2)}) collective-permute-start(bf16[64,2048]{1,0:T(8,128)(2,1)S(1)} %get-tuple-element.151), channel_id=1, source_target_pairs={{0,4},{4,0},{1,5},{5,1},{2,6},{6,2},{3,7},{7,3}} | collective-permute-start | bytes 786440 | tf_op jit(solution)/shard_map/ppermute | solution.py:324
  66.9 15.8 %collective-permute-start.10 = (bf16[64,2048]{1,0:T(8,128)(2,1)}, bf16[64,2048]{1,0:T(8,128)(2,1)S(1)}, u32[]{:S(2)}, u32[]{:S(2)}) collective-permute-start(bf16[64,2048]{1,0:T(8,128)(2,1)} %copy-done.2), channel_id=1, source_target_pairs={{0,4},{4,0},{8,12},{12,8},{1,5},{5,1},{9,13},{13,9},{2,6},{6,2},{1... | collective-permute-start | bytes 786440 | tf_op jit(solution)/shard_map/ppermute | solution.py:324
  69.3 15.5 %collective-permute-start.11 = (bf16[64,2048]{1,0:T(8,128)(2,1)}, bf16[64,2048]{1,0:T(8,128)(2,1)S(1)}, u32[]{:S(2)}, u32[]{:S(2)}) collective-permute-start(bf16[64,2048]{1,0:T(8,128)(2,1)} %copy-done.3), channel_id=1, source_target_pairs={{0,4},{4,0},{8,12},{12,8},{16,20},{20,16},{1,5},{5,1},{9,13},{13,9... | collective-permute-start | bytes 786440 | tf_op jit(solution)/shard_map/ppermute | solution.py:324
  74.5 5.2 %collective-permute-start.14 = (bf16[64,2048]{1,0:T(8,128)(2,1)S(1)}, bf16[64,2048]{1,0:T(8,128)(2,1)S(1)}, u32[]{:S(2)}, u32[]{:S(2)}) collective-permute-start(bf16[64,2048]{1,0:T(8,128)(2,1)S(1)} %get-tuple-element.163), channel_id=1, source_target_pairs={{0,8},{4,12},{8,16},{12,20},{16,24},{20,28},{1,9},{5,13},{9,17},{1... | collective-permute-start | bytes 786440 | tf_op jit(solution)/shard_map/ppermute | solution.py:329
  75.8 11.8 %collective-permute-start.12 = (bf16[64,2048]{1,0:T(8,128)(2,1)S(1)}, bf16[64,2048]{1,0:T(8,128)(2,1)S(1)}, u32[]{:S(2)}, u32[]{:S(2)}) collective-permute-start(bf16[64,2048]{1,0:T(8,128)(2,1)S(1)} %get-tuple-element.154), channel_id=1, source_target_pairs={{0,4},{4,0},{8,12},{12,8},{16,20},{20,16},{24,28},{28,24},{1,5},{5... | collective-permute-start | bytes 786440 | tf_op jit(solution)/shard_map/ppermute | solution.py:324
  81.3 12.6 %collective-permute-start.18 = (bf16[64,2048]{1,0:T(8,128)(2,1)S(1)}, bf16[64,2048]{1,0:T(8,128)(2,1)S(1)}, u32[]{:S(2)}, u32[]{:S(2)}) collective-permute-start(bf16[64,2048]{1,0:T(8,128)(2,1)S(1)} %get-tuple-element.174), channel_id=1, source_target_pairs={{8,16},{12,20},{16,24},{20,28},{9,17},{13,21},{17,25},{21,29},{10,... | collective-permute-start | bytes 786440 | tf_op jit(solution)/shard_map/ppermute | solution.py:329
  82.0 15.1 %collective-permute-start.15 = (bf16[64,2048]{1,0:T(8,128)(2,1)S(1)}, bf16[64,2048]{1,0:T(8,128)(2,1)S(1)}, u32[]{:S(2)}, u32[]{:S(2)}) collective-permute-start(bf16[64,2048]{1,0:T(8,128)(2,1)S(1)} %get-tuple-element.165), channel_id=1, source_target_pairs={{8,12},{12,8},{16,20},{20,16},{24,28},{28,24},{9,13},{13,9},{17,21... | collective-permute-start | bytes 786440 | tf_op jit(solution)/shard_map/ppermute | solution.py:324
  92.9 10.7 %collective-permute-start.13 = (bf16[64,2048]{1,0:T(8,128)(2,1)S(1)}, bf16[64,2048]{1,0:T(8,128)(2,1)S(1)}, u32[]{:S(2)}, u32[]{:S(2)}) collective-permute-start(bf16[64,2048]{1,0:T(8,128)(2,1)S(1)} %get-tuple-element.159), channel_id=1, source_target_pairs={{0,4},{4,0},{8,12},{12,8},{16,20},{20,16},{24,28},{28,24},{1,5},{5... | collective-permute-start | bytes 786440 | tf_op jit(solution)/shard_map/ppermute | solution.py:324
  95.6 10.2 %collective-permute-start.22 = (bf16[64,2048]{1,0:T(8,128)(2,1)S(1)}, bf16[64,2048]{1,0:T(8,128)(2,1)S(1)}, u32[]{:S(2)}, u32[]{:S(2)}) collective-permute-start(bf16[64,2048]{1,0:T(8,128)(2,1)S(1)} %get-tuple-element.185), channel_id=1, source_target_pairs={{16,24},{20,28},{17,25},{21,29},{18,26},{22,30},{19,27},{23,31}} | collective-permute-start | bytes 786440 | tf_op jit(solution)/shard_map/ppermute | solution.py:329
  96.2 12.4 %collective-permute-start.19 = (bf16[64,2048]{1,0:T(8,128)(2,1)S(1)}, bf16[64,2048]{1,0:T(8,128)(2,1)S(1)}, u32[]{:S(2)}, u32[]{:S(2)}) collective-permute-start(bf16[64,2048]{1,0:T(8,128)(2,1)S(1)} %get-tuple-element.176), channel_id=1, source_target_pairs={{16,20},{20,16},{24,28},{28,24},{17,21},{21,17},{25,29},{29,25},{1... | collective-permute-start | bytes 786440 | tf_op jit(solution)/shard_map/ppermute | solution.py:324
  102.4 12.6 %collective-permute-start.16 = (bf16[64,2048]{1,0:T(8,128)(2,1)S(1)}, bf16[64,2048]{1,0:T(8,128)(2,1)S(1)}, u32[]{:S(2)}, u32[]{:S(2)}) collective-permute-start(bf16[64,2048]{1,0:T(8,128)(2,1)S(1)} %get-tuple-element.169), channel_id=1, source_target_pairs={{0,4},{4,0},{8,12},{12,8},{16,20},{20,16},{24,28},{28,24},{1,5},{5... | collective-permute-start | bytes 786440 | tf_op jit(solution)/shard_map/ppermute | solution.py:324
  105.1 9.9 %collective-permute-start.17 = (bf16[64,2048]{1,0:T(8,128)(2,1)S(1)}, bf16[64,2048]{1,0:T(8,128)(2,1)S(1)}, u32[]{:S(2)}, u32[]{:S(2)}) collective-permute-start(bf16[64,2048]{1,0:T(8,128)(2,1)S(1)} %get-tuple-element.170), channel_id=1, source_target_pairs={{28,20},{24,16},{29,21},{25,17},{30,22},{26,18},{31,23},{27,19}} | collective-permute-start | bytes 786440 | tf_op jit(solution)/shard_map/ppermute | solution.py:329
  108.0 9.3 %collective-permute-start.23 = (bf16[64,2048]{1,0:T(8,128)(2,1)S(1)}, bf16[64,2048]{1,0:T(8,128)(2,1)S(1)}, u32[]{:S(2)}, u32[]{:S(2)}) collective-permute-start(bf16[64,2048]{1,0:T(8,128)(2,1)S(1)} %get-tuple-element.187), channel_id=1, source_target_pairs={{24,28},{28,24},{25,29},{29,25},{26,30},{30,26},{27,31},{31,27}} | collective-permute-start | bytes 786440 | tf_op jit(solution)/shard_map/ppermute | solution.py:324
  113.9 9.8 %collective-permute-start.20 = (bf16[64,2048]{1,0:T(8,128)(2,1)S(1)}, bf16[64,2048]{1,0:T(8,128)(2,1)S(1)}, u32[]{:S(2)}, u32[]{:S(2)}) collective-permute-start(bf16[64,2048]{1,0:T(8,128)(2,1)S(1)} %get-tuple-element.180), channel_id=1, source_target_pairs={{0,4},{4,0},{8,12},{12,8},{16,20},{20,16},{24,28},{28,24},{1,5},{5... | collective-permute-start | bytes 786440 | tf_op jit(solution)/shard_map/ppermute | solution.py:324
  116.6 7.1 %collective-permute-start.21 = (bf16[64,2048]{1,0:T(8,128)(2,1)S(1)}, bf16[64,2048]{1,0:T(8,128)(2,1)S(1)}, u32[]{:S(2)}, u32[]{:S(2)}) collective-permute-start(bf16[64,2048]{1,0:T(8,128)(2,1)S(1)} %get-tuple-element.181), channel_id=1, source_target_pairs={{28,20},{24,16},{20,12},{16,8},{29,21},{25,17},{21,13},{17,9},{30,... | collective-permute-start | bytes 786440 | tf_op jit(solution)/shard_map/ppermute | solution.py:329
  122.6 6.4 %collective-permute-start.24 = (bf16[64,2048]{1,0:T(8,128)(2,1)S(1)}, bf16[64,2048]{1,0:T(8,128)(2,1)S(1)}, u32[]{:S(2)}, u32[]{:S(2)}) collective-permute-start(bf16[64,2048]{1,0:T(8,128)(2,1)S(1)} %get-tuple-element.191), channel_id=1, source_target_pairs={{0,4},{4,0},{8,12},{12,8},{16,20},{20,16},{24,28},{28,24},{1,5},{5... | collective-permute-start | bytes 786440 | tf_op jit(solution)/shard_map/ppermute | solution.py:324
  126.0 8.6 %collective-permute-start.25 = (bf16[64,2048]{1,0:T(8,128)(2,1)S(1)}, bf16[64,2048]{1,0:T(8,128)(2,1)S(1)}, u32[]{:S(2)}, u32[]{:S(2)}) collective-permute-start(bf16[64,2048]{1,0:T(8,128)(2,1)S(1)} %get-tuple-element.192), channel_id=1, source_target_pairs={{28,20},{24,16},{20,12},{16,8},{12,4},{8,0},{29,21},{25,17},{21,13... | collective-permute-start | bytes 786440 | tf_op jit(solution)/shard_map/ppermute | solution.py:329
  136.9 10.6 %collective-permute-start.30 = (bf16[64,2048]{1,0:T(8,128)(2,1)S(1)}, bf16[64,2048]{1,0:T(8,128)(2,1)S(1)}, u32[]{:S(2)}, u32[]{:S(2)}) collective-permute-start(bf16[64,2048]{1,0:T(8,128)(2,1)S(1)} %get-tuple-element.202), channel_id=1, source_target_pairs={{28,20},{24,16},{20,12},{16,8},{12,4},{8,0},{29,21},{25,17},{21,13... | collective-permute-start | bytes 786440 | tf_op jit(solution)/shard_map/ppermute | solution.py:329
  149.8 10.8 %collective-permute-start.32 = (bf16[64,2048]{1,0:T(8,128)(2,1)S(1)}, bf16[64,2048]{1,0:T(8,128)(2,1)S(1)}, u32[]{:S(2)}, u32[]{:S(2)}) collective-permute-start(bf16[64,2048]{1,0:T(8,128)(2,1)S(1)} %get-tuple-element.212), channel_id=1, source_target_pairs={{20,12},{16,8},{12,4},{8,0},{21,13},{17,9},{13,5},{9,1},{22,14},{1... | collective-permute-start | bytes 786440 | tf_op jit(solution)/shard_map/ppermute | solution.py:329
  151.1 18.0 %collective-permute-start.26 = (bf16[64,2048]{1,0:T(8,128)(2,1)S(1)}, bf16[64,2048]{1,0:T(8,128)(2,1)S(1)}, u32[]{:S(2)}, u32[]{:S(2)}) collective-permute-start(bf16[64,2048]{1,0:T(8,128)(2,1)S(1)} %get-tuple-element.194), channel_id=1, source_target_pairs={{28,24},{24,28},{29,25},{25,29},{30,26},{26,30},{31,27},{27,31}} | collective-permute-start | bytes 786440 | tf_op jit(solution)/shard_map/ppermute | solution.py:324
  162.8 8.3 %collective-permute-start.34 = (bf16[64,2048]{1,0:T(8,128)(2,1)S(1)}, bf16[64,2048]{1,0:T(8,128)(2,1)S(1)}, u32[]{:S(2)}, u32[]{:S(2)}) collective-permute-start(bf16[64,2048]{1,0:T(8,128)(2,1)S(1)} %get-tuple-element.222), channel_id=1, source_target_pairs={{12,4},{8,0},{13,5},{9,1},{14,6},{10,2},{15,7},{11,3}} | collective-permute-start | bytes 786440 | tf_op jit(solution)/shard_map/ppermute | solution.py:329
  164.1 14.7 %collective-permute-start.27 = (bf16[64,2048]{1,0:T(8,128)(2,1)S(1)}, bf16[64,2048]{1,0:T(8,128)(2,1)S(1)}, u32[]{:S(2)}, u32[]{:S(2)}) collective-permute-start(bf16[64,2048]{1,0:T(8,128)(2,1)S(1)} %get-tuple-element.195), channel_id=1, source_target_pairs={{28,24},{24,28},{20,16},{16,20},{29,25},{25,29},{21,17},{17,21},{3... | collective-permute-start | bytes 786440 | tf_op jit(solution)/shard_map/ppermute | solution.py:324
  164.8 17.7 %collective-permute-start.28 = (bf16[64,2048]{1,0:T(8,128)(2,1)}, bf16[64,2048]{1,0:T(8,128)(2,1)S(1)}, u32[]{:S(2)}, u32[]{:S(2)}) collective-permute-start(bf16[64,2048]{1,0:T(8,128)(2,1)} %get-tuple-element.196), channel_id=1, source_target_pairs={{28,24},{24,28},{20,16},{16,20},{12,8},{8,12},{29,25},{25,29},{21,... | collective-permute-start | bytes 786440 | tf_op jit(solution)/shard_map/ppermute | solution.py:324
  165.5 17.1 %collective-permute-start.29 = (bf16[64,2048]{1,0:T(8,128)(2,1)}, bf16[64,2048]{1,0:T(8,128)(2,1)S(1)}, u32[]{:S(2)}, u32[]{:S(2)}) collective-permute-start(bf16[64,2048]{1,0:T(8,128)(2,1)} %get-tuple-element.197), channel_id=1, source_target_pairs={{28,24},{24,28},{20,16},{16,20},{12,8},{8,12},{4,0},{0,4},{29,25},... | collective-permute-start | bytes 786440 | tf_op jit(solution)/shard_map/ppermute | solution.py:324
  169.1 9.7 %copy-start = (bf16[64,2048]{1,0:T(8,128)(2,1)}, bf16[64,2048]{1,0:T(8,128)(2,1)S(1)}, u32[]{:S(2)}) copy-start(bf16[64,2048]{1,0:T(8,128)(2,1)S(1)} %collective-permute-done.26.refs_17_) | copy-start | bytes 786436
  169.1 21.4 %collective-permute-start.31 = (bf16[64,2048]{1,0:T(8,128)(2,1)}, bf16[64,2048]{1,0:T(8,128)(2,1)S(1)}, u32[]{:S(2)}, u32[]{:S(2)}) collective-permute-start(bf16[64,2048]{1,0:T(8,128)(2,1)} %get-tuple-element.204), channel_id=1, source_target_pairs={{20,16},{16,20},{12,8},{8,12},{4,0},{0,4},{21,17},{17,21},{13,9},{... | collective-permute-start | bytes 786440 | tf_op jit(solution)/shard_map/ppermute | solution.py:324
  171.1 26.5 %collective-permute-start.33 = (bf16[64,2048]{1,0:T(8,128)(2,1)}, bf16[64,2048]{1,0:T(8,128)(2,1)S(1)}, u32[]{:S(2)}, u32[]{:S(2)}) collective-permute-start(bf16[64,2048]{1,0:T(8,128)(2,1)} %get-tuple-element.214), channel_id=1, source_target_pairs={{12,8},{8,12},{4,0},{0,4},{13,9},{9,13},{5,1},{1,5},{14,10},{10,14... | collective-permute-start | bytes 786440 | tf_op jit(solution)/shard_map/ppermute | solution.py:324
  178.8 25.9 %collective-permute-start.35 = (bf16[64,2048]{1,0:T(8,128)(2,1)}, bf16[64,2048]{1,0:T(8,128)(2,1)S(1)}, u32[]{:S(2)}, u32[]{:S(2)}) collective-permute-start(bf16[64,2048]{1,0:T(8,128)(2,1)} %get-tuple-element.224), channel_id=1, source_target_pairs={{4,0},{0,4},{5,1},{1,5},{6,2},{2,6},{7,3},{3,7}} | collective-permute-start | bytes 786440 | tf_op jit(solution)/shard_map/ppermute | solution.py:324
  182.5 1.0 copy-start.1
  211.8 9.5 %copy-start.7 = (f32[8]{0:T(128)S(1)}, f32[8]{0:T(128)}, u32[]{:S(2)}) copy-start(f32[8]{0:T(128)} %copy-done.6) | copy-start | bytes 100
  220.1 9.3 %collective-permute-start.36 = (f32[3,10240]{1,0:T(4,128)S(1)}, f32[3,10240]{1,0:T(4,128)S(1)}, u32[]{:S(2)}, u32[]{:S(2)}) collective-permute-start(f32[3,10240]{1,0:T(4,128)S(1)} %slice.121), channel_id=1, source_target_pairs={{4,0},{8,4},{12,8},{16,12},{20,16},{24,20},{28,24},{5,1},{9,5},{13... | collective-permute-start | bytes 368648 | tf_op jit(solution)/shard_map/ppermute | solution.py:503
  223.6 17.8 %all-to-all-start = ((f32[32,1,2560]{2,1,0:T(1,128)}), f32[32,1,2560]{2,1,0:T(1,128)S(1)}, u32[]{:S(2)}, u32[]{:S(2)}) async-start(f32[32,1,2560]{2,1,0:T(1,128)} %all_to_all.13), calls=%async_computation | async-start | bytes 655360 | tf_op jit(solution)/shard_map/all_to_all | solution.py:520
  242.2 10.3 %all-to-all-start.1 = ((f32[8,1,2560]{2,1,0:T(1,128)}), f32[8,1,2560]{2,1,0:T(1,128)S(1)}, u32[]{:S(2)}, u32[]{:S(2)}) async-start(f32[8,1,2560]{2,1,0:T(1,128)} %broadcast_in_dim.49), calls=%async_computation.1 | async-start | bytes 163840 | tf_op jit(solution)/shard_map/all_to_all | solution.py:523

commit v3 on v2

--- a/solution.py
+++ b/solution.py
@@ -259,8 +259,11 @@
     given = len(in_specs)
     anywhere = pl.BlockSpec(memory_space=pl.ANY)
 
+    def stays(s):
+        return s.shape[0] == STATE // 2 or s.shape == (8, STATE)
+
     def place(s):
-        return s if s.shape[0] == STATE // 2 else pltpu.HBM(s.shape, s.dtype)
+        return s if stays(s) else pltpu.HBM(s.shape, s.dtype)
 
     call = pl.pallas_call(
         lambda *refs: kernel(*refs[:given], *refs[given + len(into) :]),
@@ -275,7 +278,7 @@
     )
 
     def run(*values):
-        kept = [v if s.memory_space == pltpu.SMEM or v.shape[0] == STATE // 2 else in_hbm(v)
+        kept = [v if s.memory_space == pltpu.SMEM or stays(v) else in_hbm(v)
                 for v, s in zip(values, in_specs, strict=True)]
         return call(*kept, *[in_hbm(v) for v in into])
 
@@ -311,6 +314,7 @@
         self.depth = self.ranks // 2
         self.steps = count + self.depth - 1
         self.carry = None
+        self.starts = []
 
     def physical(self, r):
         return self.ranks - 1 - r if self.flip else r
@@ -328,7 +332,11 @@
         pairs = [(self.physical(2 * z + p), self.physical(2 * z + 2 + p)) for z in live for p in range(2)]
         return lax.ppermute(value, "ctx", pairs) if pairs else None
 
-    def step(self, s, owns, gots):
+    def step(self, s, owns, gots, *first):
+        if self.carry is not None and self.flip:
+            keep, back = self.starts[-1]
+            self.carry, back, *_ = lax.optimization_barrier((self.carry, back, *first))
+            self.starts[-1] = (keep, back)
         rows, lanes = gots[0].shape
         owns, gots = owns[: s + 1], gots[: s + 1]
         tile = lanes // 2
@@ -355,7 +363,7 @@
             name="hop_back" if self.flip else "hop",
         )(self.sides, *operands)
         self.carry = self.up(after, s)
-        return keep, self.swap(give, s)
+        self.starts.append((keep, self.swap(give, s)))
 
 def body(proj_xbc, proj_dt, proj_gate, out_grad, conv_weight, conv_bias, decay_log, step_bias, skip_gain, norm_gain):
     x, dt, gate, og = proj_xbc[0], proj_dt[0], proj_gate[0], out_grad[0]
@@ -440,7 +448,7 @@
 
     def middle(c):
         first = c * per
-        near = starts[c : c + depth]
+        near = fore.starts[c : c + depth]
         return grid_call(
             lambda *refs: middle_kernel(per_group, first, depth, *refs), "middle", per,
             out_shape=(wide_bf, wide_bf, shape((STATE, part), BF16), half_bf, half_bf, shape((length, heads), F32),
@@ -455,7 +463,7 @@
 
     def back(c):
         first = c * per
-        near = ends[c : c + depth]
+        near = aft.starts[c : c + depth]
         dy, dyp, st = mids[c][:3]
         return grid_call(
             lambda *refs: back_kernel(per_group, first, depth, *refs), "back", per,
@@ -472,18 +480,18 @@
 
     fore, aft = Chain(CHUNKS, rates, sides, False), Chain(CHUNKS, rates, sides, True)
     depth, steps = fore.depth, fore.steps
-    fronts, mids, backs, starts, ends, got, got_back = [], [], [], [], [], [], []
+    fronts, mids, backs, got, got_back = [], [], [], [], []
     for u in range(CHUNKS + 2 * depth + 1):
         if u < CHUNKS:
             fronts.append(front(u))
             got.append(fore.swap(fronts[u][3]))
         if u < steps:
-            starts.append(fore.step(u, [f[2] for f in fronts], got))
+            fore.step(u, [f[2] for f in fronts], got)
         if depth <= u < depth + CHUNKS:
             mids.append(middle(u - depth))
             got_back.append(fore.swap(mids[-1][4]))
         if depth + 1 <= u < depth + 1 + steps:
-            ends.append(aft.step(u - depth - 1, [m[3] for m in mids], got_back))
+            aft.step(u - depth - 1, [m[3] for m in mids], got_back, *[b[2] for b in backs[-1:]])
         if u >= 2 * depth + 1:
             backs.append(back(u - 2 * depth - 1))
 

time: 257 us -> 248 us (0.965)
  waiting for transfers between devices: 50.2 us -> 47 us
  starting transfers between devices: 72.6 us -> 69.7 us
    ppermute x12, waiting for transfers between devices: 26.4 us -> 7.2 us  [up(): return lax.ppermute(value, 'ctx', pairs) if pairs else None]
    ppermute x22, waiting for transfers between devices: 6.7 us -> 22.7 us  [swap(): return lax.ppermute(value, 'ctx', pairs)]
  transfers between devices with their start and end apart: 39 -> 39, of which waited for: 10 -> 11; matrix products, arithmetic and copies ran while one was open for 5% -> 5% of each run, Pallas kernels for 30% -> 30%
where the time goes in v3:
time: 248 us; the launch traced here: 246 us
  Pallas kernels  101 us (41%)
  starting transfers between devices  69.7 us (28%)
  waiting for transfers between devices  47 us (19%)
  local copies, waits for them, and re-layouts  16.8 us (7%)
  blocking collectives  6.12 us (2%)
  other arithmetic  4.43 us (2%)
    pallas_call x14, Pallas kernels, run(): return call(*kept, *[in_hbm(v) for v in into])  74.2 us
    ppermute x22, starting transfers between devices, swap(): return lax.ppermute(value, 'ctx', pairs)  35.5 us
    pallas_call x14, Pallas kernels, step(): pl.pallas_call(lambda at, *refs: hop_kernel(len(carries) > 0, len(owns),...  26.9 us
    ppermute x22, waiting for transfers between devices, swap(): return lax.ppermute(value, 'ctx', pairs)  22.7 us
    ppermute x12, starting transfers between devices, up(): return lax.ppermute(value, 'ctx', pairs) if pairs else None  19.9 us
    all_to_all x1, waiting for transfers between devices, body(): lax.all_to_all(parts, ('ctx', 'fsdp'), 0, 0, tiled=True)  10 us
    ppermute x12, waiting for transfers between devices, up(): return lax.ppermute(value, 'ctx', pairs) if pairs else None  7.2 us
    all_gather x1, blocking collectives, body(): full = lax.all_gather(packed, 'fsdp', axis=1, tiled=True)  6.12 us
  transfers between devices with their start and end apart: 39, of which 11 were waited for; matrix products, arithmetic and copies ran while one was open for 5% of the time, Pallas kernels for 30%

profile of v3, /device:TPU:0, one launch (start us, length us, event | category | flops | bytes accessed | tf_op | source)
XLA Modules:
  0.0 246.5 jit_solution(1229932224227938889)
XLA Ops:
  1.6 4.8 %collective-permute-start = (bf16[3,10240]{1,0:T(4,128)(2,1)S(1)}, bf16[3,10240]{1,0:T(4,128)(2,1)S(1)}, u32[]{:S(2)}, u32[]{:S(2)}) collective-permute-start(bf16[3,10240]{1,0:T(4,128)(2,1)S(1)} %slice_bitcast_fusion), channel_id=1, source_target_pairs={{0,4},{4,8},{8,12},{12,16},{16,20},{20,24},{24,28},{1,5},{5,9},{9,... | collective-permute-start | bytes 184328 | tf_op jit(solution)/shard_map/ppermute | solution.py:389
  8.9 6.1 %all_gather.3.refs_2_.refs_8_ = f32[8,10240]{1,0:T(8,128)S(1)} all-gather(f32[8,2560]{1,0:T(8,128)S(1)} %maximum_maximum_fusion.1), channel_id=1, replica_groups=mesh['ctx'=8,'fsdp'=4] {'fsdp'}, dimensions={1}, use_global_device_ids=true | all-gather | bytes 409600 | tf_op jit(solution)/shard_map/all_gather | solution.py:397
  17.2 3.6 %keys.1 = (bf16[128,2048]{1,0:T(8,128)(2,1)}, f32[128,128]{1,0:T(8,128)}, f32[128,128]{1,0:T(8,128)}, f32[1,8192]{1,0:T(1,128)}) custom-call(bf16[128,10240]{1,0:T(8,128)(2,1)} %bitcast.39, bf16[3,10240]{1,0:T(4,128)(2,1)} %copy-done.3, f32[8,10240]{1,0:T(8,128)} %copy-done.2, bf16[128,128]{1,0:T(8,128)(2,1)} %bitcast.66, f32[1,128]{1,0:T(1,128)} %reshape.110.refs_4_, ...), custom_call_target="tpu_custom_call" | custom-call | tf_op jit(solution)/shard_map/keys/pallas_call | solution.py:283
  20.8 3.8 %front.4 = (bf16[128,2048]{1,0:T(8,128)(2,1)}, bf16[128,2048]{1,0:T(8,128)(2,1)}, bf16[64,2048]{1,0:T(8,128)(2,1)S(1)}, bf16[64,2048]{1,0:T(8,128)(2,1)S(1)}) custom-call(bf16[128,10240]{1,0:T(8,128)(2,1)} %bitcast.40, bf16[3,10240]{1,0:T(4,128)(2,1)} %copy-done.3, f32[8,10240]{1,0:T(8,128)} %copy-done.2, ...), custom_call_target="tpu_custom_call" | custom-call | tf_op jit(solution)/shard_map/front/pallas_call | solution.py:283
  24.6 1.6 collective-permute-start.2
  26.7 3.8 %front.5 = (bf16[128,2048]{1,0:T(8,128)(2,1)}, bf16[128,2048]{1,0:T(8,128)(2,1)}, bf16[64,2048]{1,0:T(8,128)(2,1)S(1)}, bf16[64,2048]{1,0:T(8,128)(2,1)S(1)}) custom-call(bf16[128,10240]{1,0:T(8,128)(2,1)} %bitcast.41, bf16[3,10240]{1,0:T(4,128)(2,1)} %copy-done.3, f32[8,10240]{1,0:T(8,128)} %copy-done.2, ...), custom_call_target="tpu_custom_call" | custom-call | tf_op jit(solution)/shard_map/front/pallas_call | solution.py:283
  30.5 1.5 collective-permute-start.3
  32.1 2.4 collective-permute-done.1.refs_1_
  34.5 2.1 hop.7
  37.4 3.5 %collective-permute-start.4 = (bf16[64,2048]{1,0:T(8,128)(2,1)S(1)}, bf16[64,2048]{1,0:T(8,128)(2,1)S(1)}, u32[]{:S(2)}, u32[]{:S(2)}) collective-permute-start(bf16[64,2048]{1,0:T(8,128)(2,1)S(1)} %get-tuple-element.153), channel_id=1, source_target_pairs={{0,8},{4,12},{1,9},{5,13},{2,10},{6,14},{3,11},{7,15}} | collective-permute-start | bytes 786440 | tf_op jit(solution)/shard_map/ppermute | solution.py:333
  40.9 3.8 %front.6 = (bf16[128,2048]{1,0:T(8,128)(2,1)}, bf16[128,2048]{1,0:T(8,128)(2,1)}, bf16[64,2048]{1,0:T(8,128)(2,1)S(1)}, bf16[64,2048]{1,0:T(8,128)(2,1)S(1)}) custom-call(bf16[128,10240]{1,0:T(8,128)(2,1)} %bitcast.42, bf16[3,10240]{1,0:T(4,128)(2,1)} %copy-done.3, f32[8,10240]{1,0:T(8,128)} %copy-done.2, ...), custom_call_target="tpu_custom_call" | custom-call | tf_op jit(solution)/shard_map/front/pallas_call | solution.py:283
  44.7 1.5 collective-permute-start.5
  46.3 2.2 hop.8
  48.5 3.7 %collective-permute-start.6 = (bf16[64,2048]{1,0:T(8,128)(2,1)S(1)}, bf16[64,2048]{1,0:T(8,128)(2,1)S(1)}, u32[]{:S(2)}, u32[]{:S(2)}) collective-permute-start(bf16[64,2048]{1,0:T(8,128)(2,1)S(1)} %get-tuple-element.157), channel_id=1, source_target_pairs={{0,8},{4,12},{8,16},{12,20},{1,9},{5,13},{9,17},{13,21},{2,10},{6,... | collective-permute-start | bytes 786440 | tf_op jit(solution)/shard_map/ppermute | solution.py:333
  52.2 3.8 %front.7 = (bf16[128,2048]{1,0:T(8,128)(2,1)}, bf16[128,2048]{1,0:T(8,128)(2,1)}, bf16[64,2048]{1,0:T(8,128)(2,1)S(1)}, bf16[64,2048]{1,0:T(8,128)(2,1)S(1)}) custom-call(bf16[128,10240]{1,0:T(8,128)(2,1)} %bitcast.43, bf16[3,10240]{1,0:T(4,128)(2,1)} %copy-done.3, f32[8,10240]{1,0:T(8,128)} %copy-done.2, ...), custom_call_target="tpu_custom_call" | custom-call | tf_op jit(solution)/shard_map/front/pallas_call | solution.py:283
  56.0 1.6 collective-permute-start.7
  57.6 2.2 hop.9
  59.9 2.8 %collective-permute-start.8 = (bf16[64,2048]{1,0:T(8,128)(2,1)S(1)}, bf16[64,2048]{1,0:T(8,128)(2,1)S(1)}, u32[]{:S(2)}, u32[]{:S(2)}) collective-permute-start(bf16[64,2048]{1,0:T(8,128)(2,1)S(1)} %get-tuple-element.161), channel_id=1, source_target_pairs={{0,8},{4,12},{8,16},{12,20},{16,24},{20,28},{1,9},{5,13},{9,17},{1... | collective-permute-start | bytes 786440 | tf_op jit(solution)/shard_map/ppermute | solution.py:333
  62.7 3.5 %collective-permute-start.9 = (bf16[64,2048]{1,0:T(8,128)(2,1)}, bf16[64,2048]{1,0:T(8,128)(2,1)}, u32[]{:S(2)}, u32[]{:S(2)}) collective-permute-start(bf16[64,2048]{1,0:T(8,128)(2,1)} %get-tuple-element.163), channel_id=1, source_target_pairs={{0,4},{4,0},{1,5},{5,1},{2,6},{6,2},{3,7},{7,3}} | collective-permute-start | bytes 786440 | tf_op jit(solution)/shard_map/ppermute | solution.py:328
  66.1 2.4 collective-permute-start.10
  68.5 3.5 %collective-permute-start.11 = (bf16[64,2048]{1,0:T(8,128)(2,1)}, bf16[64,2048]{1,0:T(8,128)(2,1)S(1)}, u32[]{:S(2)}, u32[]{:S(2)}) collective-permute-start(bf16[64,2048]{1,0:T(8,128)(2,1)} %get-tuple-element.165), channel_id=1, source_target_pairs={{0,4},{4,0},{8,12},{12,8},{16,20},{20,16},{1,5},{5,1},{9,13},{13,9... | collective-permute-start | bytes 786440 | tf_op jit(solution)/shard_map/ppermute | solution.py:328
  72.0 2.3 hop.10
  74.8 2.0 collective-permute-start.14
  78.4 1.3 collective-permute-done.10.refs_15_.refs_14_
  79.7 4.3 %collective-permute-done.11.refs_16_.refs_15_.refs_14_ = bf16[64,2048]{1,0:T(8,128)(2,1)S(1)} collective-permute-done((bf16[64,2048]{1,0:T(8,128)(2,1)}, bf16[64,2048]{1,0:T(8,128)(2,1)S(1)}, u32[]{:S(2)}, u32[]{:S(2)}) %collective-permute-start.11) | collective-permute-done | bytes 262176 | tf_op jit(solution)/shard_map/ppermute | solution.py:328
  84.0 2.8 %collective-permute-done.12.refs_17_.refs_16_.refs_15_.refs_14_ = bf16[64,2048]{1,0:T(8,128)(2,1)S(1)} collective-permute-done((bf16[64,2048]{1,0:T(8,128)(2,1)}, bf16[64,2048]{1,0:T(8,128)(2,1)S(1)}, u32[]{:S(2)}, u32[]{:S(2)}) %collective-permute-start.12) | collective-permute-done | bytes 262176 | tf_op jit(solution)/shard_map/ppermute | solution.py:328
  87.8 5.3 %middle.4 = (bf16[128,2048]{1,0:T(8,128)(2,1)}, bf16[128,2048]{1,0:T(8,128)(2,1)}, bf16[128,2048]{1,0:T(8,128)(2,1)}, bf16[64,2048]{1,0:T(8,128)(2,1)S(1)}, bf16...) custom-call(bf16[128,2048]{1,0:T(8,128)(2,1)} %get-tuple-element.146.refs_0_, ...), custom_call_target="tpu_custom_call" | custom-call | tf_op jit(solution)/shard_map/middle/pallas_call | solution.py:283
  94.4 2.0 hop.11
  97.7 1.8 collective-permute-done.13.refs_3_.refs_4_.refs_5_.refs_6_
  99.6 1.5 hop_back.7
  102.7 5.3 %middle.5 = (bf16[128,2048]{1,0:T(8,128)(2,1)}, bf16[128,2048]{1,0:T(8,128)(2,1)}, bf16[128,2048]{1,0:T(8,128)(2,1)}, bf16[64,2048]{1,0:T(8,128)(2,1)S(1)}, bf16...) custom-call(bf16[128,2048]{1,0:T(8,128)(2,1)} %get-tuple-element.173, ...), custom_call_target="tpu_custom_call", output_to_operand_aliasing={{6}: (18, {}), {7}: (19, {})} | custom-call | tf_op jit(solution)/shard_map/middle/pallas_call | solution.py:283
  109.2 1.7 hop.12
  112.3 2.1 collective-permute-done.16.refs_5_.refs_6_.refs_7_
  114.4 1.6 hop_back.8
  117.5 5.3 %middle.6 = (bf16[128,2048]{1,0:T(8,128)(2,1)}, bf16[128,2048]{1,0:T(8,128)(2,1)}, bf16[128,2048]{1,0:T(8,128)(2,1)}, bf16[64,2048]{1,0:T(8,128)(2,1)S(1)}, bf16...) custom-call(bf16[128,2048]{1,0:T(8,128)(2,1)} %get-tuple-element.186, ...), custom_call_target="tpu_custom_call", output_to_operand_aliasing={{6}: (18, {}), {7}: (19, {})} | custom-call | tf_op jit(solution)/shard_map/middle/pallas_call | solution.py:283
  124.0 2.2 hop.13
  126.9 2.3 collective-permute-done.21.refs_7_.refs_8_
  129.2 1.6 hop_back.9
  130.8 1.3 collective-permute-start.27
  132.8 5.3 %middle.7 = (bf16[128,2048]{1,0:T(8,128)(2,1)}, bf16[128,2048]{1,0:T(8,128)(2,1)}, bf16[128,2048]{1,0:T(8,128)(2,1)}, bf16[64,2048]{1,0:T(8,128)(2,1)S(1)}, bf16...) custom-call(bf16[128,2048]{1,0:T(8,128)(2,1)} %get-tuple-element.199, ...), custom_call_target="tpu_custom_call", output_to_operand_aliasing={{6}: (18, {}), {7}: (19, {})} | custom-call | tf_op jit(solution)/shard_map/middle/pallas_call | solution.py:283
  139.4 8.0 %collective-permute-done.26.refs_9_ = bf16[64,2048]{1,0:T(8,128)(2,1)S(1)} collective-permute-done((bf16[64,2048]{1,0:T(8,128)(2,1)S(1)}, bf16[64,2048]{1,0:T(8,128)(2,1)S(1)}, u32[]{:S(2)}, u32[]{:S(2)}) %collective-permute-start.26) | collective-permute-done | bytes 262176 | tf_op jit(solution)/shard_map/ppermute | solution.py:328
  147.3 1.7 hop_back.10
  149.0 1.3 collective-permute-start.29
  151.1 7.2 %collective-permute-done.29.refs_10_ = bf16[64,2048]{1,0:T(8,128)(2,1)S(1)} collective-permute-done((bf16[64,2048]{1,0:T(8,128)(2,1)S(1)}, bf16[64,2048]{1,0:T(8,128)(2,1)S(1)}, u32[]{:S(2)}, u32[]{:S(2)}) %collective-permute-start.29) | collective-permute-done | bytes 262176 | tf_op jit(solution)/shard_map/ppermute | solution.py:333
  158.3 1.7 hop_back.11
  160.0 1.3 collective-permute-start.31
  161.3 3.3 %collective-permute-start.32 = (bf16[64,2048]{1,0:T(8,128)(2,1)S(1)}, bf16[64,2048]{1,0:T(8,128)(2,1)S(1)}, u32[]{:S(2)}, u32[]{:S(2)}) collective-permute-start(bf16[64,2048]{1,0:T(8,128)(2,1)S(1)} %get-tuple-element.225), channel_id=1, source_target_pairs={{20,16},{16,20},{12,8},{8,12},{4,0},{0,4},{21,17},{17,21},{13,9},{... | collective-permute-start | bytes 786440 | tf_op jit(solution)/shard_map/ppermute | solution.py:328
  164.6 7.1 %back.4 = (f32[2,128,256]{2,1,0:T(8,128)}, f32[128,128]{1,0:T(8,128)}, f32[8,128]{1,0:T(8,128)S(1)}, bf16[128,10240]{1,0:T(8,128)(2,1)}, f32[8,10240]{1,0:T(8,128)}, /*index=5*/f32[8,10240]{1,0:T(8,128)}) custom-call(bf16[128,2048]{1,0:T(8,128)(2,1)} %get-tuple-element.142.refs_3_.refs_1_.refs_2_.refs_0_, ...), custom_call_target="tpu_custom_call" | custom-call | tf_op jit(solution)/shard_map/back/pallas_call | solution.py:283
  171.7 1.7 hop_back.12
  173.4 1.3 collective-permute-start.33
  174.7 2.7 %collective-permute-start.34 = (bf16[64,2048]{1,0:T(8,128)(2,1)S(1)}, bf16[64,2048]{1,0:T(8,128)(2,1)S(1)}, u32[]{:S(2)}, u32[]{:S(2)}) collective-permute-start(bf16[64,2048]{1,0:T(8,128)(2,1)S(1)} %get-tuple-element.238), channel_id=1, source_target_pairs={{12,8},{8,12},{4,0},{0,4},{13,9},{9,13},{5,1},{1,5},{14,10},{10,14... | collective-permute-start | bytes 786440 | tf_op jit(solution)/shard_map/ppermute | solution.py:328
  177.4 7.1 %back.5 = (f32[2,128,256]{2,1,0:T(8,128)}, f32[128,128]{1,0:T(8,128)}, f32[8,128]{1,0:T(8,128)S(1)}, bf16[128,10240]{1,0:T(8,128)(2,1)}, f32[8,10240]{1,0:T(8,128)}, /*index=5*/f32[8,10240]{1,0:T(8,128)}) custom-call(bf16[128,2048]{1,0:T(8,128)(2,1)} %get-tuple-element.142.refs_3_.refs_1_.refs_2_.refs_0, ...), custom_call_target="tpu_custom_call", output_to_operand_aliasing={{3}: (21, {}), {4}: (22, {}), {5}: (23, {})} | custom-call | tf_op jit(solution)/shard_map/back/pallas_call | solution.py:283
  184.5 2.3 hop_back.13
  186.8 3.3 %collective-permute-start.35 = (bf16[64,2048]{1,0:T(8,128)(2,1)S(1)}, bf16[64,2048]{1,0:T(8,128)(2,1)S(1)}, u32[]{:S(2)}, u32[]{:S(2)}) collective-permute-start(bf16[64,2048]{1,0:T(8,128)(2,1)S(1)} %get-tuple-element.250), channel_id=1, source_target_pairs={{4,0},{0,4},{5,1},{1,5},{6,2},{2,6},{7,3},{3,7}} | collective-permute-start | bytes 786440 | tf_op jit(solution)/shard_map/ppermute | solution.py:328
  191.6 7.1 %back.6 = (f32[2,128,256]{2,1,0:T(8,128)}, f32[128,128]{1,0:T(8,128)}, f32[8,128]{1,0:T(8,128)S(1)}, bf16[128,10240]{1,0:T(8,128)(2,1)}, f32[8,10240]{1,0:T(8,128)}, /*index=5*/f32[8,10240]{1,0:T(8,128)}) custom-call(bf16[128,2048]{1,0:T(8,128)(2,1)} %get-tuple-element.142.refs_3_.refs_1_.refs_2_.refs_0, ...), custom_call_target="tpu_custom_call", output_to_operand_aliasing={{3}: (21, {}), {4}: (22, {}), {5}: (23, {})} | custom-call | tf_op jit(solution)/shard_map/back/pallas_call | solution.py:283
  198.7 7.1 %back.7 = (f32[2,128,256]{2,1,0:T(8,128)}, f32[128,128]{1,0:T(8,128)}, f32[8,128]{1,0:T(8,128)S(1)}, bf16[128,10240]{1,0:T(8,128)(2,1)}, f32[8,10240]{1,0:T(8,128)}, /*index=5*/f32[8,10240]{1,0:T(8,128)}) custom-call(bf16[128,2048]{1,0:T(8,128)(2,1)} %get-tuple-element.142.refs_3_.refs_1_.refs_2_.refs_0, ...), custom_call_target="tpu_custom_call", output_to_operand_aliasing={{3}: (21, {}), {4}: (22, {}), {5}: (23, {})} | custom-call | tf_op jit(solution)/shard_map/back/pallas_call | solution.py:283
  205.8 5.8 %last.1 = (f32[128,128]{1,0:T(8,128)}, f32[8,128]{1,0:T(8,128)S(1)}, bf16[128,10240]{1,0:T(8,128)(2,1)}, f32[8,10240]{1,0:T(8,128)}, f32[8,10240]{1,0:T(8,128)}) custom-call(bf16[128,10240]{1,0:T(8,128)(2,1)} %bitcast.48, bf16[3,10240]{1,0:T(4,128)(2,1)} %copy-done.3, ...), custom_call_target="tpu_custom_call", output_to_operand_aliasing={{2}: (22, {}), {3}: (23, {}), {4}: (24, {})} | custom-call | tf_op jit(solution)/shard_map/last/pallas_call | solution.py:283
  213.0 1.3 collective-permute-start.36
  216.5 4.4 %all-to-all-start = ((f32[32,1,2560]{2,1,0:T(1,128)}), f32[32,1,2560]{2,1,0:T(1,128)S(1)}, u32[]{:S(2)}, u32[]{:S(2)}) async-start(f32[32,1,2560]{2,1,0:T(1,128)} %all_to_all.13), calls=%async_computation | async-start | bytes 655360 | tf_op jit(solution)/shard_map/all_to_all | solution.py:528
  220.8 2.0 convert_bitcast_fusion.2
  222.8 10.0 %all-to-all-done = f32[32,1,2560]{2,1,0:T(1,128)S(1)} async-done(((f32[32,1,2560]{2,1,0:T(1,128)}), f32[32,1,2560]{2,1,0:T(1,128)S(1)}, u32[]{:S(2)}, u32[]{:S(2)}) %all-to-all-start) | async-done | bytes 327712 | tf_op jit(solution)/shard_map/all_to_all | solution.py:528
  233.7 3.4 %all-to-all-start.1 = ((f32[8,1,2560]{2,1,0:T(1,128)}), f32[8,1,2560]{2,1,0:T(1,128)S(1)}, u32[]{:S(2)}, u32[]{:S(2)}) async-start(f32[8,1,2560]{2,1,0:T(1,128)} %broadcast_in_dim.49), calls=%async_computation.1 | async-start | bytes 163840 | tf_op jit(solution)/shard_map/all_to_all | solution.py:531
  237.2 2.1 dynamic_update_slice.4
  239.3 4.7 %all-to-all-done.1 = f32[8,1,2560]{2,1,0:T(1,128)S(1)} async-done(((f32[8,1,2560]{2,1,0:T(1,128)}), f32[8,1,2560]{2,1,0:T(1,128)S(1)}, u32[]{:S(2)}, u32[]{:S(2)}) %all-to-all-start.1) | async-done | bytes 81952 | tf_op jit(solution)/shard_map/all_to_all | solution.py:531
  (99 shorter events, 30.9 us)
Async XLA Ops:
  1.6 14.9 %collective-permute-start = (bf16[3,10240]{1,0:T(4,128)(2,1)S(1)}, bf16[3,10240]{1,0:T(4,128)(2,1)S(1)}, u32[]{:S(2)}, u32[]{:S(2)}) collective-permute-start(bf16[3,10240]{1,0:T(4,128)(2,1)S(1)} %slice_bitcast_fusion), channel_id=1, source_target_pairs={{0,4},{4,8},{8,12},{12,16},{16,20},{20,24},{24,28},{1,5},{5,9},{9,... | collective-permute-start | bytes 184328 | tf_op jit(solution)/shard_map/ppermute | solution.py:389
  15.0 1.5 copy-start.2
  15.2 9.4 %copy-start.4 = (f32[4,2560]{1,0:T(4,128)}, f32[4,2560]{1,0:T(4,128)S(1)}, u32[]{:S(2)}) copy-start(f32[4,2560]{1,0:T(4,128)S(1)} %reshape_squeeze.15) | copy-start | bytes 122884
  16.5 0.6 copy-start.3
  24.6 9.9 %collective-permute-start.2 = (bf16[64,2048]{1,0:T(8,128)(2,1)S(1)}, bf16[64,2048]{1,0:T(8,128)(2,1)S(1)}, u32[]{:S(2)}, u32[]{:S(2)}) collective-permute-start(bf16[64,2048]{1,0:T(8,128)(2,1)S(1)} %get-tuple-element.149), channel_id=1, source_target_pairs={{0,4},{4,0},{8,12},{12,8},{16,20},{20,16},{24,28},{28,24},{1,5},{5... | collective-permute-start | bytes 786440 | tf_op jit(solution)/shard_map/ppermute | solution.py:328
  26.2 8.3 %collective-permute-start.1 = (f32[1,8192]{1,0:T(1,128)}, f32[1,8192]{1,0:T(1,128)S(1)}, u32[]{:S(2)}, u32[]{:S(2)}) collective-permute-start(f32[1,8192]{1,0:T(1,128)} %get-tuple-element.144.refs_5_.refs_0_.refs_10_), channel_id=1, source_target_pairs={{0,4},{4,0},{8,12},{12,8},{16,20},{20,16},{24,28},{28,24},{1,5},{5... | collective-permute-start | bytes 98312 | tf_op jit(solution)/shard_map/ppermute | solution.py:437
  30.5 15.7 %collective-permute-start.3 = (bf16[64,2048]{1,0:T(8,128)(2,1)S(1)}, bf16[64,2048]{1,0:T(8,128)(2,1)S(1)}, u32[]{:S(2)}, u32[]{:S(2)}) collective-permute-start(bf16[64,2048]{1,0:T(8,128)(2,1)S(1)} %get-tuple-element.152), channel_id=1, source_target_pairs={{0,4},{4,0},{8,12},{12,8},{16,20},{20,16},{24,28},{28,24},{1,5},{5... | collective-permute-start | bytes 786440 | tf_op jit(solution)/shard_map/ppermute | solution.py:328
  36.7 0.7 copy-start
  37.4 8.9 %collective-permute-start.4 = (bf16[64,2048]{1,0:T(8,128)(2,1)S(1)}, bf16[64,2048]{1,0:T(8,128)(2,1)S(1)}, u32[]{:S(2)}, u32[]{:S(2)}) collective-permute-start(bf16[64,2048]{1,0:T(8,128)(2,1)S(1)} %get-tuple-element.153), channel_id=1, source_target_pairs={{0,8},{4,12},{1,9},{5,13},{2,10},{6,14},{3,11},{7,15}} | collective-permute-start | bytes 786440 | tf_op jit(solution)/shard_map/ppermute | solution.py:333
  44.7 12.9 %collective-permute-start.5 = (bf16[64,2048]{1,0:T(8,128)(2,1)S(1)}, bf16[64,2048]{1,0:T(8,128)(2,1)S(1)}, u32[]{:S(2)}, u32[]{:S(2)}) collective-permute-start(bf16[64,2048]{1,0:T(8,128)(2,1)S(1)} %get-tuple-element.156), channel_id=1, source_target_pairs={{0,4},{4,0},{8,12},{12,8},{16,20},{20,16},{24,28},{28,24},{1,5},{5... | collective-permute-start | bytes 786440 | tf_op jit(solution)/shard_map/ppermute | solution.py:328
  48.5 9.1 %collective-permute-start.6 = (bf16[64,2048]{1,0:T(8,128)(2,1)S(1)}, bf16[64,2048]{1,0:T(8,128)(2,1)S(1)}, u32[]{:S(2)}, u32[]{:S(2)}) collective-permute-start(bf16[64,2048]{1,0:T(8,128)(2,1)S(1)} %get-tuple-element.157), channel_id=1, source_target_pairs={{0,8},{4,12},{8,16},{12,20},{1,9},{5,13},{9,17},{13,21},{2,10},{6,... | collective-permute-start | bytes 786440 | tf_op jit(solution)/shard_map/ppermute | solution.py:333
  56.0 20.8 %copy-start.5 = (f32[4,2560]{1,0:T(4,128)S(1)}, f32[4,2560]{1,0:T(4,128)}, u32[]{:S(2)}) copy-start(f32[4,2560]{1,0:T(4,128)} %copy-done.4) | copy-start | bytes 122884
  56.0 16.0 %collective-permute-start.7 = (bf16[64,2048]{1,0:T(8,128)(2,1)S(1)}, bf16[64,2048]{1,0:T(8,128)(2,1)S(1)}, u32[]{:S(2)}, u32[]{:S(2)}) collective-permute-start(bf16[64,2048]{1,0:T(8,128)(2,1)S(1)} %get-tuple-element.160), channel_id=1, source_target_pairs={{0,4},{4,0},{8,12},{12,8},{16,20},{20,16},{24,28},{28,24},{1,5},{5... | collective-permute-start | bytes 786440 | tf_op jit(solution)/shard_map/ppermute | solution.py:328
  59.9 12.2 %collective-permute-start.8 = (bf16[64,2048]{1,0:T(8,128)(2,1)S(1)}, bf16[64,2048]{1,0:T(8,128)(2,1)S(1)}, u32[]{:S(2)}, u32[]{:S(2)}) collective-permute-start(bf16[64,2048]{1,0:T(8,128)(2,1)S(1)} %get-tuple-element.161), channel_id=1, source_target_pairs={{0,8},{4,12},{8,16},{12,20},{16,24},{20,28},{1,9},{5,13},{9,17},{1... | collective-permute-start | bytes 786440 | tf_op jit(solution)/shard_map/ppermute | solution.py:333
  62.7 15.7 %collective-permute-start.9 = (bf16[64,2048]{1,0:T(8,128)(2,1)}, bf16[64,2048]{1,0:T(8,128)(2,1)}, u32[]{:S(2)}, u32[]{:S(2)}) collective-permute-start(bf16[64,2048]{1,0:T(8,128)(2,1)} %get-tuple-element.163), channel_id=1, source_target_pairs={{0,4},{4,0},{1,5},{5,1},{2,6},{6,2},{3,7},{7,3}} | collective-permute-start | bytes 786440 | tf_op jit(solution)/shard_map/ppermute | solution.py:328
  66.1 13.6 %collective-permute-start.10 = (bf16[64,2048]{1,0:T(8,128)(2,1)}, bf16[64,2048]{1,0:T(8,128)(2,1)}, u32[]{:S(2)}, u32[]{:S(2)}) collective-permute-start(bf16[64,2048]{1,0:T(8,128)(2,1)} %get-tuple-element.164), channel_id=1, source_target_pairs={{0,4},{4,0},{8,12},{12,8},{1,5},{5,1},{9,13},{13,9},{2,6},{6,2},{1... | collective-permute-start | bytes 786440 | tf_op jit(solution)/shard_map/ppermute | solution.py:328
  68.5 15.5 %collective-permute-start.11 = (bf16[64,2048]{1,0:T(8,128)(2,1)}, bf16[64,2048]{1,0:T(8,128)(2,1)S(1)}, u32[]{:S(2)}, u32[]{:S(2)}) collective-permute-start(bf16[64,2048]{1,0:T(8,128)(2,1)} %get-tuple-element.165), channel_id=1, source_target_pairs={{0,4},{4,0},{8,12},{12,8},{16,20},{20,16},{1,5},{5,1},{9,13},{13,9... | collective-permute-start | bytes 786440 | tf_op jit(solution)/shard_map/ppermute | solution.py:328
  74.3 12.5 %collective-permute-start.12 = (bf16[64,2048]{1,0:T(8,128)(2,1)}, bf16[64,2048]{1,0:T(8,128)(2,1)S(1)}, u32[]{:S(2)}, u32[]{:S(2)}) collective-permute-start(bf16[64,2048]{1,0:T(8,128)(2,1)} %get-tuple-element.166), channel_id=1, source_target_pairs={{0,4},{4,0},{8,12},{12,8},{16,20},{20,16},{24,28},{28,24},{1,5},{5... | collective-permute-start | bytes 786440 | tf_op jit(solution)/shard_map/ppermute | solution.py:328
  74.8 19.5 %collective-permute-start.14 = (bf16[64,2048]{1,0:T(8,128)(2,1)}, bf16[64,2048]{1,0:T(8,128)(2,1)}, u32[]{:S(2)}, u32[]{:S(2)}) collective-permute-start(bf16[64,2048]{1,0:T(8,128)(2,1)} %get-tuple-element.175), channel_id=1, source_target_pairs={{0,8},{4,12},{8,16},{12,20},{16,24},{20,28},{1,9},{5,13},{9,17},{1... | collective-permute-start | bytes 786440 | tf_op jit(solution)/shard_map/ppermute | solution.py:333
  86.8 1.0 copy-start.1
  93.1 6.4 %collective-permute-start.13 = (bf16[64,2048]{1,0:T(8,128)(2,1)S(1)}, bf16[64,2048]{1,0:T(8,128)(2,1)S(1)}, u32[]{:S(2)}, u32[]{:S(2)}) collective-permute-start(bf16[64,2048]{1,0:T(8,128)(2,1)S(1)} %get-tuple-element.171), channel_id=1, source_target_pairs={{0,4},{4,0},{8,12},{12,8},{16,20},{20,16},{24,28},{28,24},{1,5},{5... | collective-permute-start | bytes 786440 | tf_op jit(solution)/shard_map/ppermute | solution.py:328
  96.4 6.3 %collective-permute-start.15 = (bf16[64,2048]{1,0:T(8,128)(2,1)S(1)}, bf16[64,2048]{1,0:T(8,128)(2,1)S(1)}, u32[]{:S(2)}, u32[]{:S(2)}) collective-permute-start(bf16[64,2048]{1,0:T(8,128)(2,1)S(1)} %get-tuple-element.177), channel_id=1, source_target_pairs={{8,12},{12,8},{16,20},{20,16},{24,28},{28,24},{9,13},{13,9},{17,21... | collective-permute-start | bytes 786440 | tf_op jit(solution)/shard_map/ppermute | solution.py:328
  97.1 12.2 %collective-permute-start.19 = (bf16[64,2048]{1,0:T(8,128)(2,1)S(1)}, bf16[64,2048]{1,0:T(8,128)(2,1)S(1)}, u32[]{:S(2)}, u32[]{:S(2)}) collective-permute-start(bf16[64,2048]{1,0:T(8,128)(2,1)S(1)} %get-tuple-element.188), channel_id=1, source_target_pairs={{8,16},{12,20},{16,24},{20,28},{9,17},{13,21},{17,25},{21,29},{10,... | collective-permute-start | bytes 786440 | tf_op jit(solution)/shard_map/ppermute | solution.py:333
  101.1 11.2 %collective-permute-start.17 = (bf16[64,2048]{1,0:T(8,128)(2,1)S(1)}, bf16[64,2048]{1,0:T(8,128)(2,1)S(1)}, u32[]{:S(2)}, u32[]{:S(2)}) collective-permute-start(bf16[64,2048]{1,0:T(8,128)(2,1)S(1)} %get-tuple-element.182), channel_id=1, source_target_pairs={{28,20},{24,16},{29,21},{25,17},{30,22},{26,18},{31,23},{27,19}} | collective-permute-start | bytes 786440 | tf_op jit(solution)/shard_map/ppermute | solution.py:333
  101.8 10.5 %collective-permute-start.18 = (bf16[64,2048]{1,0:T(8,128)(2,1)S(1)}, bf16[64,2048]{1,0:T(8,128)(2,1)S(1)}, u32[]{:S(2)}, u32[]{:S(2)}) collective-permute-start(bf16[64,2048]{1,0:T(8,128)(2,1)S(1)} %get-tuple-element.183), channel_id=1, source_target_pairs={{28,24},{24,28},{29,25},{25,29},{30,26},{26,30},{31,27},{27,31}} | collective-permute-start | bytes 786440 | tf_op jit(solution)/shard_map/ppermute | solution.py:328
  108.0 6.4 %collective-permute-start.16 = (bf16[64,2048]{1,0:T(8,128)(2,1)S(1)}, bf16[64,2048]{1,0:T(8,128)(2,1)S(1)}, u32[]{:S(2)}, u32[]{:S(2)}) collective-permute-start(bf16[64,2048]{1,0:T(8,128)(2,1)S(1)} %get-tuple-element.181), channel_id=1, source_target_pairs={{0,4},{4,0},{8,12},{12,8},{16,20},{20,16},{24,28},{28,24},{1,5},{5... | collective-permute-start | bytes 786440 | tf_op jit(solution)/shard_map/ppermute | solution.py:328
  110.9 6.5 %collective-permute-start.20 = (bf16[64,2048]{1,0:T(8,128)(2,1)S(1)}, bf16[64,2048]{1,0:T(8,128)(2,1)S(1)}, u32[]{:S(2)}, u32[]{:S(2)}) collective-permute-start(bf16[64,2048]{1,0:T(8,128)(2,1)S(1)} %get-tuple-element.190), channel_id=1, source_target_pairs={{16,20},{20,16},{24,28},{28,24},{17,21},{21,17},{25,29},{29,25},{1... | collective-permute-start | bytes 786440 | tf_op jit(solution)/shard_map/ppermute | solution.py:328
  111.6 12.4 %collective-permute-start.24 = (bf16[64,2048]{1,0:T(8,128)(2,1)S(1)}, bf16[64,2048]{1,0:T(8,128)(2,1)S(1)}, u32[]{:S(2)}, u32[]{:S(2)}) collective-permute-start(bf16[64,2048]{1,0:T(8,128)(2,1)S(1)} %get-tuple-element.201), channel_id=1, source_target_pairs={{16,24},{20,28},{17,25},{21,29},{18,26},{22,30},{19,27},{23,31}} | collective-permute-start | bytes 786440 | tf_op jit(solution)/shard_map/ppermute | solution.py:333
  116.1 10.8 %collective-permute-start.22 = (bf16[64,2048]{1,0:T(8,128)(2,1)S(1)}, bf16[64,2048]{1,0:T(8,128)(2,1)S(1)}, u32[]{:S(2)}, u32[]{:S(2)}) collective-permute-start(bf16[64,2048]{1,0:T(8,128)(2,1)S(1)} %get-tuple-element.195), channel_id=1, source_target_pairs={{28,20},{24,16},{20,12},{16,8},{29,21},{25,17},{21,13},{17,9},{30,... | collective-permute-start | bytes 786440 | tf_op jit(solution)/shard_map/ppermute | solution.py:333
  116.8 10.1 %collective-permute-start.23 = (bf16[64,2048]{1,0:T(8,128)(2,1)S(1)}, bf16[64,2048]{1,0:T(8,128)(2,1)S(1)}, u32[]{:S(2)}, u32[]{:S(2)}) collective-permute-start(bf16[64,2048]{1,0:T(8,128)(2,1)S(1)} %get-tuple-element.196), channel_id=1, source_target_pairs={{28,24},{24,28},{20,16},{16,20},{29,25},{25,29},{21,17},{17,21},{3... | collective-permute-start | bytes 786440 | tf_op jit(solution)/shard_map/ppermute | solution.py:328
  122.7 6.4 %collective-permute-start.21 = (bf16[64,2048]{1,0:T(8,128)(2,1)S(1)}, bf16[64,2048]{1,0:T(8,128)(2,1)S(1)}, u32[]{:S(2)}, u32[]{:S(2)}) collective-permute-start(bf16[64,2048]{1,0:T(8,128)(2,1)S(1)} %get-tuple-element.194), channel_id=1, source_target_pairs={{0,4},{4,0},{8,12},{12,8},{16,20},{20,16},{24,28},{28,24},{1,5},{5... | collective-permute-start | bytes 786440 | tf_op jit(solution)/shard_map/ppermute | solution.py:328
  126.2 6.6 %collective-permute-start.25 = (bf16[64,2048]{1,0:T(8,128)(2,1)S(1)}, bf16[64,2048]{1,0:T(8,128)(2,1)S(1)}, u32[]{:S(2)}, u32[]{:S(2)}) collective-permute-start(bf16[64,2048]{1,0:T(8,128)(2,1)S(1)} %get-tuple-element.203), channel_id=1, source_target_pairs={{24,28},{28,24},{25,29},{29,25},{26,30},{30,26},{27,31},{31,27}} | collective-permute-start | bytes 786440 | tf_op jit(solution)/shard_map/ppermute | solution.py:328
  130.8 8.5 %collective-permute-start.27 = (bf16[64,2048]{1,0:T(8,128)(2,1)S(1)}, bf16[64,2048]{1,0:T(8,128)(2,1)S(1)}, u32[]{:S(2)}, u32[]{:S(2)}) collective-permute-start(bf16[64,2048]{1,0:T(8,128)(2,1)S(1)} %get-tuple-element.208), channel_id=1, source_target_pairs={{28,20},{24,16},{20,12},{16,8},{12,4},{8,0},{29,21},{25,17},{21,13... | collective-permute-start | bytes 786440 | tf_op jit(solution)/shard_map/ppermute | solution.py:333
  132.1 7.2 %collective-permute-start.28 = (bf16[64,2048]{1,0:T(8,128)(2,1)S(1)}, bf16[64,2048]{1,0:T(8,128)(2,1)S(1)}, u32[]{:S(2)}, u32[]{:S(2)}) collective-permute-start(bf16[64,2048]{1,0:T(8,128)(2,1)S(1)} %get-tuple-element.209), channel_id=1, source_target_pairs={{28,24},{24,28},{20,16},{16,20},{12,8},{8,12},{29,25},{25,29},{21,... | collective-permute-start | bytes 786440 | tf_op jit(solution)/shard_map/ppermute | solution.py:328
  138.1 9.2 %collective-permute-start.26 = (bf16[64,2048]{1,0:T(8,128)(2,1)S(1)}, bf16[64,2048]{1,0:T(8,128)(2,1)S(1)}, u32[]{:S(2)}, u32[]{:S(2)}) collective-permute-start(bf16[64,2048]{1,0:T(8,128)(2,1)S(1)} %get-tuple-element.207), channel_id=1, source_target_pairs={{0,4},{4,0},{8,12},{12,8},{16,20},{20,16},{24,28},{28,24},{1,5},{5... | collective-permute-start | bytes 786440 | tf_op jit(solution)/shard_map/ppermute | solution.py:328
  149.0 9.3 %collective-permute-start.29 = (bf16[64,2048]{1,0:T(8,128)(2,1)S(1)}, bf16[64,2048]{1,0:T(8,128)(2,1)S(1)}, u32[]{:S(2)}, u32[]{:S(2)}) collective-permute-start(bf16[64,2048]{1,0:T(8,128)(2,1)S(1)} %get-tuple-element.215), channel_id=1, source_target_pairs={{28,20},{24,16},{20,12},{16,8},{12,4},{8,0},{29,21},{25,17},{21,13... | collective-permute-start | bytes 786440 | tf_op jit(solution)/shard_map/ppermute | solution.py:333
  150.3 8.0 %collective-permute-start.30 = (bf16[64,2048]{1,0:T(8,128)(2,1)S(1)}, bf16[64,2048]{1,0:T(8,128)(2,1)S(1)}, u32[]{:S(2)}, u32[]{:S(2)}) collective-permute-start(bf16[64,2048]{1,0:T(8,128)(2,1)S(1)} %get-tuple-element.216), channel_id=1, source_target_pairs={{28,24},{24,28},{20,16},{16,20},{12,8},{8,12},{4,0},{0,4},{29,25},... | collective-permute-start | bytes 786440 | tf_op jit(solution)/shard_map/ppermute | solution.py:328
  160.0 11.7 %collective-permute-start.31 = (bf16[64,2048]{1,0:T(8,128)(2,1)S(1)}, bf16[64,2048]{1,0:T(8,128)(2,1)S(1)}, u32[]{:S(2)}, u32[]{:S(2)}) collective-permute-start(bf16[64,2048]{1,0:T(8,128)(2,1)S(1)} %get-tuple-element.224), channel_id=1, source_target_pairs={{20,12},{16,8},{12,4},{8,0},{21,13},{17,9},{13,5},{9,1},{22,14},{1... | collective-permute-start | bytes 786440 | tf_op jit(solution)/shard_map/ppermute | solution.py:333
  161.3 10.4 %collective-permute-start.32 = (bf16[64,2048]{1,0:T(8,128)(2,1)S(1)}, bf16[64,2048]{1,0:T(8,128)(2,1)S(1)}, u32[]{:S(2)}, u32[]{:S(2)}) collective-permute-start(bf16[64,2048]{1,0:T(8,128)(2,1)S(1)} %get-tuple-element.225), channel_id=1, source_target_pairs={{20,16},{16,20},{12,8},{8,12},{4,0},{0,4},{21,17},{17,21},{13,9},{... | collective-permute-start | bytes 786440 | tf_op jit(solution)/shard_map/ppermute | solution.py:328
  173.4 11.1 %collective-permute-start.33 = (bf16[64,2048]{1,0:T(8,128)(2,1)S(1)}, bf16[64,2048]{1,0:T(8,128)(2,1)S(1)}, u32[]{:S(2)}, u32[]{:S(2)}) collective-permute-start(bf16[64,2048]{1,0:T(8,128)(2,1)S(1)} %get-tuple-element.237), channel_id=1, source_target_pairs={{12,4},{8,0},{13,5},{9,1},{14,6},{10,2},{15,7},{11,3}} | collective-permute-start | bytes 786440 | tf_op jit(solution)/shard_map/ppermute | solution.py:333
  174.7 9.8 %collective-permute-start.34 = (bf16[64,2048]{1,0:T(8,128)(2,1)S(1)}, bf16[64,2048]{1,0:T(8,128)(2,1)S(1)}, u32[]{:S(2)}, u32[]{:S(2)}) collective-permute-start(bf16[64,2048]{1,0:T(8,128)(2,1)S(1)} %get-tuple-element.238), channel_id=1, source_target_pairs={{12,8},{8,12},{4,0},{0,4},{13,9},{9,13},{5,1},{1,5},{14,10},{10,14... | collective-permute-start | bytes 786440 | tf_op jit(solution)/shard_map/ppermute | solution.py:328
  186.8 11.9 %collective-permute-start.35 = (bf16[64,2048]{1,0:T(8,128)(2,1)S(1)}, bf16[64,2048]{1,0:T(8,128)(2,1)S(1)}, u32[]{:S(2)}, u32[]{:S(2)}) collective-permute-start(bf16[64,2048]{1,0:T(8,128)(2,1)S(1)} %get-tuple-element.250), channel_id=1, source_target_pairs={{4,0},{0,4},{5,1},{1,5},{6,2},{2,6},{7,3},{3,7}} | collective-permute-start | bytes 786440 | tf_op jit(solution)/shard_map/ppermute | solution.py:328
  213.0 7.9 %collective-permute-start.36 = (f32[3,10240]{1,0:T(4,128)S(1)}, f32[3,10240]{1,0:T(4,128)S(1)}, u32[]{:S(2)}, u32[]{:S(2)}) collective-permute-start(f32[3,10240]{1,0:T(4,128)S(1)} %slice.121), channel_id=1, source_target_pairs={{4,0},{8,4},{12,8},{16,12},{20,16},{24,20},{28,24},{5,1},{9,5},{13... | collective-permute-start | bytes 368648 | tf_op jit(solution)/shard_map/ppermute | solution.py:511
  216.5 16.4 %all-to-all-start = ((f32[32,1,2560]{2,1,0:T(1,128)}), f32[32,1,2560]{2,1,0:T(1,128)S(1)}, u32[]{:S(2)}, u32[]{:S(2)}) async-start(f32[32,1,2560]{2,1,0:T(1,128)} %all_to_all.13), calls=%async_computation | async-start | bytes 655360 | tf_op jit(solution)/shard_map/all_to_all | solution.py:528
  233.7 10.3 %all-to-all-start.1 = ((f32[8,1,2560]{2,1,0:T(1,128)}), f32[8,1,2560]{2,1,0:T(1,128)S(1)}, u32[]{:S(2)}, u32[]{:S(2)}) async-start(f32[8,1,2560]{2,1,0:T(1,128)} %broadcast_in_dim.49), calls=%async_computation.1 | async-start | bytes 163840 | tf_op jit(solution)/shard_map/all_to_all | solution.py:531

commit v4 on v3

--- a/solution.py
+++ b/solution.py
@@ -174,7 +174,7 @@
     a1_ref[...] += sum_heads(dyp.astype(F32) * yn, g, per_group, heads)
 
 
-def conv_back(grads, x_ref, halo_ref, w_ref, gx_ref, edge_ref, wr_ref, xs, gs):
+def conv_back(grads, x_ref, halo_ref, w_ref, gx_ref, lead_ref, tail_ref, wr_ref, xs, gs):
     length = x_ref.shape[0]
     pre = conv_pre(x_ref, halo_ref, w_ref, xs)
     sig = sigmoid(pre)
@@ -189,15 +189,14 @@
         wr_ref[k : k + 1, :] = jnp.sum(gp * xs[PAD - HALO + k : PAD - HALO + k + length, :], axis=0, keepdims=True)
     wr_ref[KERNEL : KERNEL + 1, :] = jnp.sum(gp, axis=0, keepdims=True)
     gx_ref[...] = total.astype(BF16)
-    edge_ref[...] = jnp.zeros(edge_ref.shape, F32)
-    edge_ref[0:HALO, :] = gp[0:HALO, :]
-    edge_ref[HALO : 2 * HALO, :] = total[length - HALO : length, :]
+    lead_ref[...] = gp[0:HALO, :]
+    tail_ref[...] = total[length - HALO : length, :]
 
 
 def back_kernel(per_group, first, depth, k_ref, q_ref, vp_ref, st_ref, dy_ref, dyp_ref, x_ref, halo_ref, w_ref,
                 skip_ref, et_ref, ei_ref, side_ref, *refs):
     keeps, backs = refs[:depth], refs[depth : 2 * depth]
-    dkq_ref, a2_ref, last_ref, gx_ref, edge_ref, wr_ref, xs, gs = refs[2 * depth :]
+    dkq_ref, a2_ref, last_ref, gx_ref, lead_ref, tail_ref, wr_ref, xs, gs = refs[2 * depth :]
     j = first + pl.program_id(0)
     length, width = x_ref.shape
     heads = ei_ref.shape[1]
@@ -224,14 +223,14 @@
     dz = jnp.where(lower_mask(length), mm_nt(dyp, vp), 0.0)
     dkq_ref[0] = mm(dz.T.astype(BF16), q) + mm_nt(vp, en)
     dkq_ref[1] = mm(dz.astype(BF16), k) + mm_nt(dyp, st)
-    conv_back(grads, x_ref, halo_ref, w_ref, gx_ref, edge_ref, wr_ref, xs, gs)
+    conv_back(grads, x_ref, halo_ref, w_ref, gx_ref, lead_ref, tail_ref, wr_ref, xs, gs)
 
 
 def last_kernel(count, x_ref, halo_ref, w_ref, dt_ref, sb_ref, dl_ref, *refs):
     dkq, a1, a2, last = (refs[i * count : (i + 1) * count] for i in range(4))
-    gdt_ref, hs_ref, gx_ref, edge_ref, wr_ref, xs, gs = refs[4 * count :]
+    gdt_ref, hs_ref, gx_ref, lead_ref, tail_ref, wr_ref, xs, gs = refs[4 * count :]
     grads = jnp.concatenate([ref[0] for ref in dkq], axis=1)
-    conv_back(grads, x_ref, halo_ref, w_ref, gx_ref, edge_ref, wr_ref, xs, gs)
+    conv_back(grads, x_ref, halo_ref, w_ref, gx_ref, lead_ref, tail_ref, wr_ref, xs, gs)
 
     @pl.when(pl.program_id(0) == 0)
     def _():
@@ -339,7 +338,7 @@
             self.starts[-1] = (keep, back)
         rows, lanes = gots[0].shape
         owns, gots = owns[: s + 1], gots[: s + 1]
-        tile = lanes // 2
+        tile = lanes
         per = lanes // tile
         flat = pl.BlockSpec((rows, tile), lambda i, at: (0, i))
         flip, count = int(self.flip), self.count
@@ -415,7 +414,8 @@
     half_out = spec((STATE // 2, width), lambda i: (0, i))
     window = pltpu.VMEM((PAD + length, width), F32)
     wide_bf, half_bf = shape((length, part), BF16), shape((STATE // 2, part), BF16)
-    grad_shapes = (shape((length, channels), BF16), shape((8, channels), F32), shape((8, channels), F32))
+    grad_shapes = (shape((length, channels), BF16), shape((HALO, channels), F32), shape((HALO, channels), F32),
+                   shape((8, channels), F32))
 
     def conv_specs(first):
         return [spec((rows, width), lambda i: (0, first + i)) for rows in (length, HALO, 8)]
@@ -472,7 +472,7 @@
             in_specs=[*head_cols(first), wide_out, spec((STATE, width), lambda i: (0, i)), wide_out, wide_out,
                       *conv_specs(first), cols(1, first), cols(1, first), table, scalars] + [half_out] * (2 * depth),
             out_specs=(spec((2, length, STATE), lambda i: (0, 0, i)), table, spec((8, heads), lambda i: (0, 0)),
-                       cols(length, first), cols(8, first), cols(8, first)),
+                       cols(length, first), cols(HALO, first), cols(HALO, first), cols(8, first)),
             scratch=[window, window],
             into=backs[-1][3:] if backs else (),
         )(kq, kq, fronts[c][1], st, dy, dyp, x, halo, full, skip_x, et, ei, sides,
@@ -495,23 +495,24 @@
         if u >= 2 * depth + 1:
             backs.append(back(u - 2 * depth - 1))
 
-    grad_dt, hs, gx, edge, wr = grid_call(
+    grad_dt, hs, gx, lead, tail, wr = grid_call(
         lambda *refs: last_kernel(CHUNKS, *refs), "last", 2,
         out_shape=(shape((length, heads), F32), shape((8, heads), F32), *grad_shapes),
         in_specs=conv_specs(GROUPS) + [table, row_head, row_head]
         + [spec((1, length, per * STATE), lambda i: (i, 0, 0))] * CHUNKS + [table] * (2 * CHUNKS)
         + [spec((8, heads), lambda i: (0, 0))] * CHUNKS,
-        out_specs=(table, spec((8, heads), lambda i: (0, 0)), cols(length, GROUPS), cols(8, GROUPS), cols(8, GROUPS)),
+        out_specs=(table, spec((8, heads), lambda i: (0, 0)), cols(length, GROUPS), cols(HALO, GROUPS),
+                   cols(HALO, GROUPS), cols(8, GROUPS)),
         scratch=[window, window],
         into=backs[-1][3:],
     )(x, halo, full, dt, step_b, decay, *[b[0] for b in backs], *[m[5] for m in mids], *[b[1] for b in backs],
       *[b[2] for b in backs])
     grad_gate, sums = mids[-1][6:]
 
-    next_gp = lax.ppermute(edge[:HALO], "ctx", behind)
+    next_gp = lax.ppermute(lead, "ctx", behind)
     fixed = []
     for i in range(HALO):
-        row = edge[HALO + i]
+        row = tail[i]
         for k in range(i + 1):
             row = row + full[k] * next_gp[i - k]
         fixed.append(row)
@@ -529,17 +530,17 @@
     summed = summed * (1.0 / math.sqrt(length * ranks * shards))
     copies = jnp.broadcast_to(summed[None], (ranks, piece))
     mine = lax.all_to_all(copies, "ctx", 0, 0, tiled=True).reshape(8, c_loc)
-    tail = mine[KERNEL + 1]
+    ends = mine[KERNEL + 1]
     return (
         grad_xbc[None],
         grad_dt[None],
         grad_gate[None],
         mine[:KERNEL],
         mine[KERNEL],
-        tail[g_loc : g_loc + h_loc],
-        tail[g_loc + h_loc : g_loc + 2 * h_loc],
-        tail[g_loc + 2 * h_loc : g_loc + 3 * h_loc],
-        tail[:g_loc],
+        ends[g_loc : g_loc + h_loc],
+        ends[g_loc + h_loc : g_loc + 2 * h_loc],
+        ends[g_loc + 2 * h_loc : g_loc + 3 * h_loc],
+        ends[:g_loc],
     )
 
 

time: 248 us -> 246 us (level)
  no operation moved by 1% of the time
where the time goes in v4:
time: 246 us; the launch traced here: 244 us
  Pallas kernels  99.7 us (41%)
  starting transfers between devices  69.7 us (28%)
  waiting for transfers between devices  47.7 us (19%)
  local copies, waits for them, and re-layouts  15.8 us (6%)
  blocking collectives  6.12 us (2%)
  other arithmetic  4.18 us (2%)
    pallas_call x14, Pallas kernels, run(): return call(*kept, *[in_hbm(v) for v in into])  74.2 us
    ppermute x22, starting transfers between devices, swap(): return lax.ppermute(value, 'ctx', pairs)  35.5 us
    pallas_call x14, Pallas kernels, step(): pl.pallas_call(lambda at, *refs: hop_kernel(len(carries) > 0, len(owns),...  25.5 us
    ppermute x22, waiting for transfers between devices, swap(): return lax.ppermute(value, 'ctx', pairs)  23 us
    ppermute x12, starting transfers between devices, up(): return lax.ppermute(value, 'ctx', pairs) if pairs else None  19.8 us
    all_to_all x1, waiting for transfers between devices, body(): lax.all_to_all(parts, ('ctx', 'fsdp'), 0, 0, tiled=True)  10.3 us
    ppermute x12, waiting for transfers between devices, up(): return lax.ppermute(value, 'ctx', pairs) if pairs else None  7.35 us
    all_gather x1, blocking collectives, body(): full = lax.all_gather(packed, 'fsdp', axis=1, tiled=True)  6.12 us
  transfers between devices with their start and end apart: 39, of which 11 were waited for; matrix products, arithmetic and copies ran while one was open for 5% of the time, Pallas kernels for 30%

profile of v4, /device:TPU:0, one launch (start us, length us, event | category | flops | bytes accessed | tf_op | source)
XLA Modules:
  0.0 244.5 jit_solution(6206354696112418546)
XLA Ops:
  1.6 4.8 %collective-permute-start = (bf16[3,10240]{1,0:T(4,128)(2,1)S(1)}, bf16[3,10240]{1,0:T(4,128)(2,1)S(1)}, u32[]{:S(2)}, u32[]{:S(2)}) collective-permute-start(bf16[3,10240]{1,0:T(4,128)(2,1)S(1)} %slice_bitcast_fusion), channel_id=1, source_target_pairs={{0,4},{4,8},{8,12},{12,16},{16,20},{20,24},{24,28},{1,5},{5,9},{9,... | collective-permute-start | bytes 184328 | tf_op jit(solution)/shard_map/ppermute | solution.py:388
  8.9 6.1 %all_gather.3.refs_2_.refs_8_ = f32[8,10240]{1,0:T(8,128)S(1)} all-gather(f32[8,2560]{1,0:T(8,128)S(1)} %maximum_maximum_fusion.1), channel_id=1, replica_groups=mesh['ctx'=8,'fsdp'=4] {'fsdp'}, dimensions={1}, use_global_device_ids=true | all-gather | bytes 409600 | tf_op jit(solution)/shard_map/all_gather | solution.py:396
  17.2 3.6 %keys.1 = (bf16[128,2048]{1,0:T(8,128)(2,1)}, f32[128,128]{1,0:T(8,128)}, f32[128,128]{1,0:T(8,128)}, f32[1,8192]{1,0:T(1,128)}) custom-call(bf16[128,10240]{1,0:T(8,128)(2,1)} %bitcast.39, bf16[3,10240]{1,0:T(4,128)(2,1)} %copy-done.3, f32[8,10240]{1,0:T(8,128)} %copy-done.2, bf16[128,128]{1,0:T(8,128)(2,1)} %bitcast.66, f32[1,128]{1,0:T(1,128)} %reshape.110.refs_4_, ...), custom_call_target="tpu_custom_call" | custom-call | tf_op jit(solution)/shard_map/keys/pallas_call | solution.py:282
  20.8 3.8 %front.4 = (bf16[128,2048]{1,0:T(8,128)(2,1)}, bf16[128,2048]{1,0:T(8,128)(2,1)}, bf16[64,2048]{1,0:T(8,128)(2,1)S(1)}, bf16[64,2048]{1,0:T(8,128)(2,1)S(1)}) custom-call(bf16[128,10240]{1,0:T(8,128)(2,1)} %bitcast.40, bf16[3,10240]{1,0:T(4,128)(2,1)} %copy-done.3, f32[8,10240]{1,0:T(8,128)} %copy-done.2, ...), custom_call_target="tpu_custom_call" | custom-call | tf_op jit(solution)/shard_map/front/pallas_call | solution.py:282
  24.6 1.6 collective-permute-start.2
  26.7 3.8 %front.5 = (bf16[128,2048]{1,0:T(8,128)(2,1)}, bf16[128,2048]{1,0:T(8,128)(2,1)}, bf16[64,2048]{1,0:T(8,128)(2,1)S(1)}, bf16[64,2048]{1,0:T(8,128)(2,1)S(1)}) custom-call(bf16[128,10240]{1,0:T(8,128)(2,1)} %bitcast.41, bf16[3,10240]{1,0:T(4,128)(2,1)} %copy-done.3, f32[8,10240]{1,0:T(8,128)} %copy-done.2, ...), custom_call_target="tpu_custom_call" | custom-call | tf_op jit(solution)/shard_map/front/pallas_call | solution.py:282
  30.5 1.5 collective-permute-start.3
  32.0 2.4 collective-permute-done.1.refs_1_
  34.5 2.1 hop.7
  37.3 3.5 %collective-permute-start.4 = (bf16[64,2048]{1,0:T(8,128)(2,1)S(1)}, bf16[64,2048]{1,0:T(8,128)(2,1)S(1)}, u32[]{:S(2)}, u32[]{:S(2)}) collective-permute-start(bf16[64,2048]{1,0:T(8,128)(2,1)S(1)} %get-tuple-element.158), channel_id=1, source_target_pairs={{0,8},{4,12},{1,9},{5,13},{2,10},{6,14},{3,11},{7,15}} | collective-permute-start | bytes 786440 | tf_op jit(solution)/shard_map/ppermute | solution.py:332
  40.8 3.9 %front.6 = (bf16[128,2048]{1,0:T(8,128)(2,1)}, bf16[128,2048]{1,0:T(8,128)(2,1)}, bf16[64,2048]{1,0:T(8,128)(2,1)S(1)}, bf16[64,2048]{1,0:T(8,128)(2,1)S(1)}) custom-call(bf16[128,10240]{1,0:T(8,128)(2,1)} %bitcast.42, bf16[3,10240]{1,0:T(4,128)(2,1)} %copy-done.3, f32[8,10240]{1,0:T(8,128)} %copy-done.2, ...), custom_call_target="tpu_custom_call" | custom-call | tf_op jit(solution)/shard_map/front/pallas_call | solution.py:282
  44.6 1.5 collective-permute-start.5
  46.2 2.1 hop.8
  48.3 3.6 %collective-permute-start.6 = (bf16[64,2048]{1,0:T(8,128)(2,1)S(1)}, bf16[64,2048]{1,0:T(8,128)(2,1)S(1)}, u32[]{:S(2)}, u32[]{:S(2)}) collective-permute-start(bf16[64,2048]{1,0:T(8,128)(2,1)S(1)} %get-tuple-element.162), channel_id=1, source_target_pairs={{0,8},{4,12},{8,16},{12,20},{1,9},{5,13},{9,17},{13,21},{2,10},{6,... | collective-permute-start | bytes 786440 | tf_op jit(solution)/shard_map/ppermute | solution.py:332
  52.0 3.8 %front.7 = (bf16[128,2048]{1,0:T(8,128)(2,1)}, bf16[128,2048]{1,0:T(8,128)(2,1)}, bf16[64,2048]{1,0:T(8,128)(2,1)S(1)}, bf16[64,2048]{1,0:T(8,128)(2,1)S(1)}) custom-call(bf16[128,10240]{1,0:T(8,128)(2,1)} %bitcast.43, bf16[3,10240]{1,0:T(4,128)(2,1)} %copy-done.3, f32[8,10240]{1,0:T(8,128)} %copy-done.2, ...), custom_call_target="tpu_custom_call" | custom-call | tf_op jit(solution)/shard_map/front/pallas_call | solution.py:282
  55.8 1.6 collective-permute-start.7
  57.4 2.1 hop.9
  59.5 2.8 %collective-permute-start.8 = (bf16[64,2048]{1,0:T(8,128)(2,1)S(1)}, bf16[64,2048]{1,0:T(8,128)(2,1)S(1)}, u32[]{:S(2)}, u32[]{:S(2)}) collective-permute-start(bf16[64,2048]{1,0:T(8,128)(2,1)S(1)} %get-tuple-element.166), channel_id=1, source_target_pairs={{0,8},{4,12},{8,16},{12,20},{16,24},{20,28},{1,9},{5,13},{9,17},{1... | collective-permute-start | bytes 786440 | tf_op jit(solution)/shard_map/ppermute | solution.py:332
  62.3 3.5 %collective-permute-start.9 = (bf16[64,2048]{1,0:T(8,128)(2,1)}, bf16[64,2048]{1,0:T(8,128)(2,1)}, u32[]{:S(2)}, u32[]{:S(2)}) collective-permute-start(bf16[64,2048]{1,0:T(8,128)(2,1)} %get-tuple-element.168), channel_id=1, source_target_pairs={{0,4},{4,0},{1,5},{5,1},{2,6},{6,2},{3,7},{7,3}} | collective-permute-start | bytes 786440 | tf_op jit(solution)/shard_map/ppermute | solution.py:327
  65.8 2.4 collective-permute-start.10
  68.2 3.5 %collective-permute-start.11 = (bf16[64,2048]{1,0:T(8,128)(2,1)}, bf16[64,2048]{1,0:T(8,128)(2,1)S(1)}, u32[]{:S(2)}, u32[]{:S(2)}) collective-permute-start(bf16[64,2048]{1,0:T(8,128)(2,1)} %get-tuple-element.170), channel_id=1, source_target_pairs={{0,4},{4,0},{8,12},{12,8},{16,20},{20,16},{1,5},{5,1},{9,13},{13,9... | collective-permute-start | bytes 786440 | tf_op jit(solution)/shard_map/ppermute | solution.py:327
  71.7 2.3 hop.10
  74.4 2.0 collective-permute-start.14
  78.0 1.4 collective-permute-done.10.refs_15_.refs_14_
  79.4 4.3 %collective-permute-done.11.refs_16_.refs_15_.refs_14_ = bf16[64,2048]{1,0:T(8,128)(2,1)S(1)} collective-permute-done((bf16[64,2048]{1,0:T(8,128)(2,1)}, bf16[64,2048]{1,0:T(8,128)(2,1)S(1)}, u32[]{:S(2)}, u32[]{:S(2)}) %collective-permute-start.11) | collective-permute-done | bytes 262176 | tf_op jit(solution)/shard_map/ppermute | solution.py:327
  83.7 2.8 %collective-permute-done.12.refs_17_.refs_16_.refs_15_.refs_14_ = bf16[64,2048]{1,0:T(8,128)(2,1)S(1)} collective-permute-done((bf16[64,2048]{1,0:T(8,128)(2,1)}, bf16[64,2048]{1,0:T(8,128)(2,1)S(1)}, u32[]{:S(2)}, u32[]{:S(2)}) %collective-permute-start.12) | collective-permute-done | bytes 262176 | tf_op jit(solution)/shard_map/ppermute | solution.py:327
  87.4 5.3 %middle.4 = (bf16[128,2048]{1,0:T(8,128)(2,1)}, bf16[128,2048]{1,0:T(8,128)(2,1)}, bf16[128,2048]{1,0:T(8,128)(2,1)}, bf16[64,2048]{1,0:T(8,128)(2,1)S(1)}, bf16...) custom-call(bf16[128,2048]{1,0:T(8,128)(2,1)} %get-tuple-element.151.refs_0_, ...), custom_call_target="tpu_custom_call" | custom-call | tf_op jit(solution)/shard_map/middle/pallas_call | solution.py:282
  94.0 1.8 hop.11
  97.2 2.0 collective-permute-done.13.refs_3_.refs_4_.refs_5_.refs_6_
  99.2 1.4 hop_back.7
  102.2 5.3 %middle.5 = (bf16[128,2048]{1,0:T(8,128)(2,1)}, bf16[128,2048]{1,0:T(8,128)(2,1)}, bf16[128,2048]{1,0:T(8,128)(2,1)}, bf16[64,2048]{1,0:T(8,128)(2,1)S(1)}, bf16...) custom-call(bf16[128,2048]{1,0:T(8,128)(2,1)} %get-tuple-element.178, ...), custom_call_target="tpu_custom_call", output_to_operand_aliasing={{6}: (18, {}), {7}: (19, {})} | custom-call | tf_op jit(solution)/shard_map/middle/pallas_call | solution.py:282
  108.8 1.6 hop.12
  111.7 2.2 collective-permute-done.16.refs_5_.refs_6_.refs_7_
  114.0 1.5 hop_back.8
  116.9 5.3 %middle.6 = (bf16[128,2048]{1,0:T(8,128)(2,1)}, bf16[128,2048]{1,0:T(8,128)(2,1)}, bf16[128,2048]{1,0:T(8,128)(2,1)}, bf16[64,2048]{1,0:T(8,128)(2,1)S(1)}, bf16...) custom-call(bf16[128,2048]{1,0:T(8,128)(2,1)} %get-tuple-element.191, ...), custom_call_target="tpu_custom_call", output_to_operand_aliasing={{6}: (18, {}), {7}: (19, {})} | custom-call | tf_op jit(solution)/shard_map/middle/pallas_call | solution.py:282
  123.4 2.2 hop.13
  126.3 2.3 collective-permute-done.21.refs_7_.refs_8_
  128.6 1.5 hop_back.9
  130.1 1.3 collective-permute-start.27
  132.1 5.3 %middle.7 = (bf16[128,2048]{1,0:T(8,128)(2,1)}, bf16[128,2048]{1,0:T(8,128)(2,1)}, bf16[128,2048]{1,0:T(8,128)(2,1)}, bf16[64,2048]{1,0:T(8,128)(2,1)S(1)}, bf16...) custom-call(bf16[128,2048]{1,0:T(8,128)(2,1)} %get-tuple-element.204, ...), custom_call_target="tpu_custom_call", output_to_operand_aliasing={{6}: (18, {}), {7}: (19, {})} | custom-call | tf_op jit(solution)/shard_map/middle/pallas_call | solution.py:282
  138.7 7.8 %collective-permute-done.26.refs_9_ = bf16[64,2048]{1,0:T(8,128)(2,1)S(1)} collective-permute-done((bf16[64,2048]{1,0:T(8,128)(2,1)S(1)}, bf16[64,2048]{1,0:T(8,128)(2,1)S(1)}, u32[]{:S(2)}, u32[]{:S(2)}) %collective-permute-start.26) | collective-permute-done | bytes 262176 | tf_op jit(solution)/shard_map/ppermute | solution.py:327
  146.5 1.6 hop_back.10
  148.1 1.3 collective-permute-start.29
  150.2 7.3 %collective-permute-done.29.refs_10_ = bf16[64,2048]{1,0:T(8,128)(2,1)S(1)} collective-permute-done((bf16[64,2048]{1,0:T(8,128)(2,1)S(1)}, bf16[64,2048]{1,0:T(8,128)(2,1)S(1)}, u32[]{:S(2)}, u32[]{:S(2)}) %collective-permute-start.29) | collective-permute-done | bytes 262176 | tf_op jit(solution)/shard_map/ppermute | solution.py:332
  157.5 1.6 hop_back.11
  159.1 1.3 collective-permute-start.31
  160.4 3.4 %collective-permute-start.32 = (bf16[64,2048]{1,0:T(8,128)(2,1)S(1)}, bf16[64,2048]{1,0:T(8,128)(2,1)S(1)}, u32[]{:S(2)}, u32[]{:S(2)}) collective-permute-start(bf16[64,2048]{1,0:T(8,128)(2,1)S(1)} %get-tuple-element.230), channel_id=1, source_target_pairs={{20,16},{16,20},{12,8},{8,12},{4,0},{0,4},{21,17},{17,21},{13,9},{... | collective-permute-start | bytes 786440 | tf_op jit(solution)/shard_map/ppermute | solution.py:327
  163.7 7.0 %back.4 = (f32[2,128,256]{2,1,0:T(8,128)}, f32[128,128]{1,0:T(8,128)}, f32[8,128]{1,0:T(8,128)S(1)}, bf16[128,10240]{1,0:T(8,128)(2,1)}, f32[3,10240]{1,0:T(4,12...) custom-call(bf16[128,2048]{1,0:T(8,128)(2,1)} %get-tuple-element.147.refs_3_.refs_1_.refs_2_.refs_0_, ...), custom_call_target="tpu_custom_call" | custom-call | tf_op jit(solution)/shard_map/back/pallas_call | solution.py:282
  170.8 1.6 hop_back.12
  172.3 1.3 collective-permute-start.33
  173.6 2.7 %collective-permute-start.34 = (bf16[64,2048]{1,0:T(8,128)(2,1)S(1)}, bf16[64,2048]{1,0:T(8,128)(2,1)S(1)}, u32[]{:S(2)}, u32[]{:S(2)}) collective-permute-start(bf16[64,2048]{1,0:T(8,128)(2,1)S(1)} %get-tuple-element.244), channel_id=1, source_target_pairs={{12,8},{8,12},{4,0},{0,4},{13,9},{9,13},{5,1},{1,5},{14,10},{10,14... | collective-permute-start | bytes 786440 | tf_op jit(solution)/shard_map/ppermute | solution.py:327
  176.3 7.1 %back.5 = (f32[2,128,256]{2,1,0:T(8,128)}, f32[128,128]{1,0:T(8,128)}, f32[8,128]{1,0:T(8,128)S(1)}, bf16[128,10240]{1,0:T(8,128)(2,1)}, f32[3,10240]{1,0:T(4,12...) custom-call(bf16[128,2048]{1,0:T(8,128)(2,1)} %get-tuple-element.147, ...), custom_call_target="tpu_custom_call", output_to_operand_aliasing={{3}: (21, {}), {4}: (22, {}), {5}: (23, {}), {6}: (24, {})} | custom-call | tf_op jit(solution)/shard_map/back/pallas_call | solution.py:282
  183.5 2.2 hop_back.13
  185.7 3.3 %collective-permute-start.35 = (bf16[64,2048]{1,0:T(8,128)(2,1)S(1)}, bf16[64,2048]{1,0:T(8,128)(2,1)S(1)}, u32[]{:S(2)}, u32[]{:S(2)}) collective-permute-start(bf16[64,2048]{1,0:T(8,128)(2,1)S(1)} %get-tuple-element.257), channel_id=1, source_target_pairs={{4,0},{0,4},{5,1},{1,5},{6,2},{2,6},{7,3},{3,7}} | collective-permute-start | bytes 786440 | tf_op jit(solution)/shard_map/ppermute | solution.py:327
  190.5 7.1 %back.6 = (f32[2,128,256]{2,1,0:T(8,128)}, f32[128,128]{1,0:T(8,128)}, f32[8,128]{1,0:T(8,128)S(1)}, bf16[128,10240]{1,0:T(8,128)(2,1)}, f32[3,10240]{1,0:T(4,12...) custom-call(bf16[128,2048]{1,0:T(8,128)(2,1)} %get-tuple-element.147, ...), custom_call_target="tpu_custom_call", output_to_operand_aliasing={{3}: (21, {}), {4}: (22, {}), {5}: (23, {}), {6}: (24, {})} | custom-call | tf_op jit(solution)/shard_map/back/pallas_call | solution.py:282
  197.6 7.1 %back.7 = (f32[2,128,256]{2,1,0:T(8,128)}, f32[128,128]{1,0:T(8,128)}, f32[8,128]{1,0:T(8,128)S(1)}, bf16[128,10240]{1,0:T(8,128)(2,1)}, f32[3,10240]{1,0:T(4,12...) custom-call(bf16[128,2048]{1,0:T(8,128)(2,1)} %get-tuple-element.147, ...), custom_call_target="tpu_custom_call", output_to_operand_aliasing={{3}: (21, {}), {4}: (22, {}), {5}: (23, {}), {6}: (24, {})} | custom-call | tf_op jit(solution)/shard_map/back/pallas_call | solution.py:282
  204.7 5.8 %last.1 = (f32[128,128]{1,0:T(8,128)}, f32[8,128]{1,0:T(8,128)S(1)}, bf16[128,10240]{1,0:T(8,128)(2,1)}, f32[3,10240]{1,0:T(4,128)}, f32[3,10240]{1,0:T(4,128)}, /*index=5*/f32[8,10240]{1,0:T(8,128)}) custom-call(bf16[128,10240]{1,0:T(8,128)(2,1)} %bitcast.48, ...), custom_call_target="tpu_custom_call", output_to_operand_aliasing={{2}: (22, {}), {3}: (23, {}), {4}: (24, {}), {5}: (25, {})} | custom-call | tf_op jit(solution)/shard_map/last/pallas_call | solution.py:282
  210.9 1.3 collective-permute-start.36
  214.4 4.4 %all-to-all-start = ((f32[32,1,2560]{2,1,0:T(1,128)}), f32[32,1,2560]{2,1,0:T(1,128)S(1)}, u32[]{:S(2)}, u32[]{:S(2)}) async-start(f32[32,1,2560]{2,1,0:T(1,128)} %all_to_all.13), calls=%async_computation | async-start | bytes 655360 | tf_op jit(solution)/shard_map/all_to_all | solution.py:529
  218.8 1.7 convert_bitcast_fusion.2
  220.5 10.3 %all-to-all-done = f32[32,1,2560]{2,1,0:T(1,128)S(1)} async-done(((f32[32,1,2560]{2,1,0:T(1,128)}), f32[32,1,2560]{2,1,0:T(1,128)S(1)}, u32[]{:S(2)}, u32[]{:S(2)}) %all-to-all-start) | async-done | bytes 327712 | tf_op jit(solution)/shard_map/all_to_all | solution.py:529
  231.7 3.4 %all-to-all-start.1 = ((f32[8,1,2560]{2,1,0:T(1,128)}), f32[8,1,2560]{2,1,0:T(1,128)S(1)}, u32[]{:S(2)}, u32[]{:S(2)}) async-start(f32[8,1,2560]{2,1,0:T(1,128)} %broadcast_in_dim.49), calls=%async_computation.1 | async-start | bytes 163840 | tf_op jit(solution)/shard_map/all_to_all | solution.py:532
  235.2 2.1 dynamic_update_slice.4
  237.3 4.7 %all-to-all-done.1 = f32[8,1,2560]{2,1,0:T(1,128)S(1)} async-done(((f32[8,1,2560]{2,1,0:T(1,128)}), f32[8,1,2560]{2,1,0:T(1,128)S(1)}, u32[]{:S(2)}, u32[]{:S(2)}) %all-to-all-start.1) | async-done | bytes 81952 | tf_op jit(solution)/shard_map/all_to_all | solution.py:532
  (98 shorter events, 29.9 us)
Async XLA Ops:
  1.6 14.9 %collective-permute-start = (bf16[3,10240]{1,0:T(4,128)(2,1)S(1)}, bf16[3,10240]{1,0:T(4,128)(2,1)S(1)}, u32[]{:S(2)}, u32[]{:S(2)}) collective-permute-start(bf16[3,10240]{1,0:T(4,128)(2,1)S(1)} %slice_bitcast_fusion), channel_id=1, source_target_pairs={{0,4},{4,8},{8,12},{12,16},{16,20},{20,24},{24,28},{1,5},{5,9},{9,... | collective-permute-start | bytes 184328 | tf_op jit(solution)/shard_map/ppermute | solution.py:388
  15.0 1.5 copy-start.2
  15.2 9.4 %copy-start.4 = (f32[4,2560]{1,0:T(4,128)}, f32[4,2560]{1,0:T(4,128)S(1)}, u32[]{:S(2)}) copy-start(f32[4,2560]{1,0:T(4,128)S(1)} %reshape_squeeze.15) | copy-start | bytes 122884
  16.5 0.6 copy-start.3
  24.6 9.9 %collective-permute-start.2 = (bf16[64,2048]{1,0:T(8,128)(2,1)S(1)}, bf16[64,2048]{1,0:T(8,128)(2,1)S(1)}, u32[]{:S(2)}, u32[]{:S(2)}) collective-permute-start(bf16[64,2048]{1,0:T(8,128)(2,1)S(1)} %get-tuple-element.154), channel_id=1, source_target_pairs={{0,4},{4,0},{8,12},{12,8},{16,20},{20,16},{24,28},{28,24},{1,5},{5... | collective-permute-start | bytes 786440 | tf_op jit(solution)/shard_map/ppermute | solution.py:327
  26.2 8.3 %collective-permute-start.1 = (f32[1,8192]{1,0:T(1,128)}, f32[1,8192]{1,0:T(1,128)S(1)}, u32[]{:S(2)}, u32[]{:S(2)}) collective-permute-start(f32[1,8192]{1,0:T(1,128)} %get-tuple-element.149.refs_5_.refs_0_.refs_10_), channel_id=1, source_target_pairs={{0,4},{4,0},{8,12},{12,8},{16,20},{20,16},{24,28},{28,24},{1,5},{5... | collective-permute-start | bytes 98312 | tf_op jit(solution)/shard_map/ppermute | solution.py:437
  30.5 15.7 %collective-permute-start.3 = (bf16[64,2048]{1,0:T(8,128)(2,1)S(1)}, bf16[64,2048]{1,0:T(8,128)(2,1)S(1)}, u32[]{:S(2)}, u32[]{:S(2)}) collective-permute-start(bf16[64,2048]{1,0:T(8,128)(2,1)S(1)} %get-tuple-element.157), channel_id=1, source_target_pairs={{0,4},{4,0},{8,12},{12,8},{16,20},{20,16},{24,28},{28,24},{1,5},{5... | collective-permute-start | bytes 786440 | tf_op jit(solution)/shard_map/ppermute | solution.py:327
  36.6 0.7 copy-start
  37.3 8.9 %collective-permute-start.4 = (bf16[64,2048]{1,0:T(8,128)(2,1)S(1)}, bf16[64,2048]{1,0:T(8,128)(2,1)S(1)}, u32[]{:S(2)}, u32[]{:S(2)}) collective-permute-start(bf16[64,2048]{1,0:T(8,128)(2,1)S(1)} %get-tuple-element.158), channel_id=1, source_target_pairs={{0,8},{4,12},{1,9},{5,13},{2,10},{6,14},{3,11},{7,15}} | collective-permute-start | bytes 786440 | tf_op jit(solution)/shard_map/ppermute | solution.py:332
  44.6 12.8 %collective-permute-start.5 = (bf16[64,2048]{1,0:T(8,128)(2,1)S(1)}, bf16[64,2048]{1,0:T(8,128)(2,1)S(1)}, u32[]{:S(2)}, u32[]{:S(2)}) collective-permute-start(bf16[64,2048]{1,0:T(8,128)(2,1)S(1)} %get-tuple-element.161), channel_id=1, source_target_pairs={{0,4},{4,0},{8,12},{12,8},{16,20},{20,16},{24,28},{28,24},{1,5},{5... | collective-permute-start | bytes 786440 | tf_op jit(solution)/shard_map/ppermute | solution.py:327
  48.3 9.1 %collective-permute-start.6 = (bf16[64,2048]{1,0:T(8,128)(2,1)S(1)}, bf16[64,2048]{1,0:T(8,128)(2,1)S(1)}, u32[]{:S(2)}, u32[]{:S(2)}) collective-permute-start(bf16[64,2048]{1,0:T(8,128)(2,1)S(1)} %get-tuple-element.162), channel_id=1, source_target_pairs={{0,8},{4,12},{8,16},{12,20},{1,9},{5,13},{9,17},{13,21},{2,10},{6,... | collective-permute-start | bytes 786440 | tf_op jit(solution)/shard_map/ppermute | solution.py:332
  55.8 20.7 %copy-start.5 = (f32[4,2560]{1,0:T(4,128)S(1)}, f32[4,2560]{1,0:T(4,128)}, u32[]{:S(2)}) copy-start(f32[4,2560]{1,0:T(4,128)} %copy-done.4) | copy-start | bytes 122884
  55.8 15.9 %collective-permute-start.7 = (bf16[64,2048]{1,0:T(8,128)(2,1)S(1)}, bf16[64,2048]{1,0:T(8,128)(2,1)S(1)}, u32[]{:S(2)}, u32[]{:S(2)}) collective-permute-start(bf16[64,2048]{1,0:T(8,128)(2,1)S(1)} %get-tuple-element.165), channel_id=1, source_target_pairs={{0,4},{4,0},{8,12},{12,8},{16,20},{20,16},{24,28},{28,24},{1,5},{5... | collective-permute-start | bytes 786440 | tf_op jit(solution)/shard_map/ppermute | solution.py:327
  59.5 12.2 %collective-permute-start.8 = (bf16[64,2048]{1,0:T(8,128)(2,1)S(1)}, bf16[64,2048]{1,0:T(8,128)(2,1)S(1)}, u32[]{:S(2)}, u32[]{:S(2)}) collective-permute-start(bf16[64,2048]{1,0:T(8,128)(2,1)S(1)} %get-tuple-element.166), channel_id=1, source_target_pairs={{0,8},{4,12},{8,16},{12,20},{16,24},{20,28},{1,9},{5,13},{9,17},{1... | collective-permute-start | bytes 786440 | tf_op jit(solution)/shard_map/ppermute | solution.py:332
  62.3 15.6 %collective-permute-start.9 = (bf16[64,2048]{1,0:T(8,128)(2,1)}, bf16[64,2048]{1,0:T(8,128)(2,1)}, u32[]{:S(2)}, u32[]{:S(2)}) collective-permute-start(bf16[64,2048]{1,0:T(8,128)(2,1)} %get-tuple-element.168), channel_id=1, source_target_pairs={{0,4},{4,0},{1,5},{5,1},{2,6},{6,2},{3,7},{7,3}} | collective-permute-start | bytes 786440 | tf_op jit(solution)/shard_map/ppermute | solution.py:327
  65.8 13.6 %collective-permute-start.10 = (bf16[64,2048]{1,0:T(8,128)(2,1)}, bf16[64,2048]{1,0:T(8,128)(2,1)}, u32[]{:S(2)}, u32[]{:S(2)}) collective-permute-start(bf16[64,2048]{1,0:T(8,128)(2,1)} %get-tuple-element.169), channel_id=1, source_target_pairs={{0,4},{4,0},{8,12},{12,8},{1,5},{5,1},{9,13},{13,9},{2,6},{6,2},{1... | collective-permute-start | bytes 786440 | tf_op jit(solution)/shard_map/ppermute | solution.py:327
  68.2 15.5 %collective-permute-start.11 = (bf16[64,2048]{1,0:T(8,128)(2,1)}, bf16[64,2048]{1,0:T(8,128)(2,1)S(1)}, u32[]{:S(2)}, u32[]{:S(2)}) collective-permute-start(bf16[64,2048]{1,0:T(8,128)(2,1)} %get-tuple-element.170), channel_id=1, source_target_pairs={{0,4},{4,0},{8,12},{12,8},{16,20},{20,16},{1,5},{5,1},{9,13},{13,9... | collective-permute-start | bytes 786440 | tf_op jit(solution)/shard_map/ppermute | solution.py:327
  73.9 12.5 %collective-permute-start.12 = (bf16[64,2048]{1,0:T(8,128)(2,1)}, bf16[64,2048]{1,0:T(8,128)(2,1)S(1)}, u32[]{:S(2)}, u32[]{:S(2)}) collective-permute-start(bf16[64,2048]{1,0:T(8,128)(2,1)} %get-tuple-element.171), channel_id=1, source_target_pairs={{0,4},{4,0},{8,12},{12,8},{16,20},{20,16},{24,28},{28,24},{1,5},{5... | collective-permute-start | bytes 786440 | tf_op jit(solution)/shard_map/ppermute | solution.py:327
  74.4 19.6 %collective-permute-start.14 = (bf16[64,2048]{1,0:T(8,128)(2,1)}, bf16[64,2048]{1,0:T(8,128)(2,1)}, u32[]{:S(2)}, u32[]{:S(2)}) collective-permute-start(bf16[64,2048]{1,0:T(8,128)(2,1)} %get-tuple-element.180), channel_id=1, source_target_pairs={{0,8},{4,12},{8,16},{12,20},{16,24},{20,28},{1,9},{5,13},{9,17},{1... | collective-permute-start | bytes 786440 | tf_op jit(solution)/shard_map/ppermute | solution.py:332
  86.5 1.0 copy-start.1
  92.8 6.4 %collective-permute-start.13 = (bf16[64,2048]{1,0:T(8,128)(2,1)S(1)}, bf16[64,2048]{1,0:T(8,128)(2,1)S(1)}, u32[]{:S(2)}, u32[]{:S(2)}) collective-permute-start(bf16[64,2048]{1,0:T(8,128)(2,1)S(1)} %get-tuple-element.176), channel_id=1, source_target_pairs={{0,4},{4,0},{8,12},{12,8},{16,20},{20,16},{24,28},{28,24},{1,5},{5... | collective-permute-start | bytes 786440 | tf_op jit(solution)/shard_map/ppermute | solution.py:327
  95.8 6.4 %collective-permute-start.15 = (bf16[64,2048]{1,0:T(8,128)(2,1)S(1)}, bf16[64,2048]{1,0:T(8,128)(2,1)S(1)}, u32[]{:S(2)}, u32[]{:S(2)}) collective-permute-start(bf16[64,2048]{1,0:T(8,128)(2,1)S(1)} %get-tuple-element.182), channel_id=1, source_target_pairs={{8,12},{12,8},{16,20},{20,16},{24,28},{28,24},{9,13},{13,9},{17,21... | collective-permute-start | bytes 786440 | tf_op jit(solution)/shard_map/ppermute | solution.py:327
  96.5 12.3 %collective-permute-start.19 = (bf16[64,2048]{1,0:T(8,128)(2,1)S(1)}, bf16[64,2048]{1,0:T(8,128)(2,1)S(1)}, u32[]{:S(2)}, u32[]{:S(2)}) collective-permute-start(bf16[64,2048]{1,0:T(8,128)(2,1)S(1)} %get-tuple-element.193), channel_id=1, source_target_pairs={{8,16},{12,20},{16,24},{20,28},{9,17},{13,21},{17,25},{21,29},{10,... | collective-permute-start | bytes 786440 | tf_op jit(solution)/shard_map/ppermute | solution.py:332
  100.7 11.1 %collective-permute-start.17 = (bf16[64,2048]{1,0:T(8,128)(2,1)S(1)}, bf16[64,2048]{1,0:T(8,128)(2,1)S(1)}, u32[]{:S(2)}, u32[]{:S(2)}) collective-permute-start(bf16[64,2048]{1,0:T(8,128)(2,1)S(1)} %get-tuple-element.187), channel_id=1, source_target_pairs={{28,20},{24,16},{29,21},{25,17},{30,22},{26,18},{31,23},{27,19}} | collective-permute-start | bytes 786440 | tf_op jit(solution)/shard_map/ppermute | solution.py:332
  101.3 10.4 %collective-permute-start.18 = (bf16[64,2048]{1,0:T(8,128)(2,1)S(1)}, bf16[64,2048]{1,0:T(8,128)(2,1)S(1)}, u32[]{:S(2)}, u32[]{:S(2)}) collective-permute-start(bf16[64,2048]{1,0:T(8,128)(2,1)S(1)} %get-tuple-element.188), channel_id=1, source_target_pairs={{28,24},{24,28},{29,25},{25,29},{30,26},{26,30},{31,27},{27,31}} | collective-permute-start | bytes 786440 | tf_op jit(solution)/shard_map/ppermute | solution.py:327
  107.5 6.4 %collective-permute-start.16 = (bf16[64,2048]{1,0:T(8,128)(2,1)S(1)}, bf16[64,2048]{1,0:T(8,128)(2,1)S(1)}, u32[]{:S(2)}, u32[]{:S(2)}) collective-permute-start(bf16[64,2048]{1,0:T(8,128)(2,1)S(1)} %get-tuple-element.186), channel_id=1, source_target_pairs={{0,4},{4,0},{8,12},{12,8},{16,20},{20,16},{24,28},{28,24},{1,5},{5... | collective-permute-start | bytes 786440 | tf_op jit(solution)/shard_map/ppermute | solution.py:327
  110.3 6.5 %collective-permute-start.20 = (bf16[64,2048]{1,0:T(8,128)(2,1)S(1)}, bf16[64,2048]{1,0:T(8,128)(2,1)S(1)}, u32[]{:S(2)}, u32[]{:S(2)}) collective-permute-start(bf16[64,2048]{1,0:T(8,128)(2,1)S(1)} %get-tuple-element.195), channel_id=1, source_target_pairs={{16,20},{20,16},{24,28},{28,24},{17,21},{21,17},{25,29},{29,25},{1... | collective-permute-start | bytes 786440 | tf_op jit(solution)/shard_map/ppermute | solution.py:327
  111.0 12.4 %collective-permute-start.24 = (bf16[64,2048]{1,0:T(8,128)(2,1)S(1)}, bf16[64,2048]{1,0:T(8,128)(2,1)S(1)}, u32[]{:S(2)}, u32[]{:S(2)}) collective-permute-start(bf16[64,2048]{1,0:T(8,128)(2,1)S(1)} %get-tuple-element.206), channel_id=1, source_target_pairs={{16,24},{20,28},{17,25},{21,29},{18,26},{22,30},{19,27},{23,31}} | collective-permute-start | bytes 786440 | tf_op jit(solution)/shard_map/ppermute | solution.py:332
  115.5 10.8 %collective-permute-start.22 = (bf16[64,2048]{1,0:T(8,128)(2,1)S(1)}, bf16[64,2048]{1,0:T(8,128)(2,1)S(1)}, u32[]{:S(2)}, u32[]{:S(2)}) collective-permute-start(bf16[64,2048]{1,0:T(8,128)(2,1)S(1)} %get-tuple-element.200), channel_id=1, source_target_pairs={{28,20},{24,16},{20,12},{16,8},{29,21},{25,17},{21,13},{17,9},{30,... | collective-permute-start | bytes 786440 | tf_op jit(solution)/shard_map/ppermute | solution.py:332
  116.2 10.1 %collective-permute-start.23 = (bf16[64,2048]{1,0:T(8,128)(2,1)S(1)}, bf16[64,2048]{1,0:T(8,128)(2,1)S(1)}, u32[]{:S(2)}, u32[]{:S(2)}) collective-permute-start(bf16[64,2048]{1,0:T(8,128)(2,1)S(1)} %get-tuple-element.201), channel_id=1, source_target_pairs={{28,24},{24,28},{20,16},{16,20},{29,25},{25,29},{21,17},{17,21},{3... | collective-permute-start | bytes 786440 | tf_op jit(solution)/shard_map/ppermute | solution.py:327
  122.2 6.4 %collective-permute-start.21 = (bf16[64,2048]{1,0:T(8,128)(2,1)S(1)}, bf16[64,2048]{1,0:T(8,128)(2,1)S(1)}, u32[]{:S(2)}, u32[]{:S(2)}) collective-permute-start(bf16[64,2048]{1,0:T(8,128)(2,1)S(1)} %get-tuple-element.199), channel_id=1, source_target_pairs={{0,4},{4,0},{8,12},{12,8},{16,20},{20,16},{24,28},{28,24},{1,5},{5... | collective-permute-start | bytes 786440 | tf_op jit(solution)/shard_map/ppermute | solution.py:327
  125.6 6.5 %collective-permute-start.25 = (bf16[64,2048]{1,0:T(8,128)(2,1)S(1)}, bf16[64,2048]{1,0:T(8,128)(2,1)S(1)}, u32[]{:S(2)}, u32[]{:S(2)}) collective-permute-start(bf16[64,2048]{1,0:T(8,128)(2,1)S(1)} %get-tuple-element.208), channel_id=1, source_target_pairs={{24,28},{28,24},{25,29},{29,25},{26,30},{30,26},{27,31},{31,27}} | collective-permute-start | bytes 786440 | tf_op jit(solution)/shard_map/ppermute | solution.py:327
  130.1 8.5 %collective-permute-start.27 = (bf16[64,2048]{1,0:T(8,128)(2,1)S(1)}, bf16[64,2048]{1,0:T(8,128)(2,1)S(1)}, u32[]{:S(2)}, u32[]{:S(2)}) collective-permute-start(bf16[64,2048]{1,0:T(8,128)(2,1)S(1)} %get-tuple-element.213), channel_id=1, source_target_pairs={{28,20},{24,16},{20,12},{16,8},{12,4},{8,0},{29,21},{25,17},{21,13... | collective-permute-start | bytes 786440 | tf_op jit(solution)/shard_map/ppermute | solution.py:332
  131.4 7.3 %collective-permute-start.28 = (bf16[64,2048]{1,0:T(8,128)(2,1)S(1)}, bf16[64,2048]{1,0:T(8,128)(2,1)S(1)}, u32[]{:S(2)}, u32[]{:S(2)}) collective-permute-start(bf16[64,2048]{1,0:T(8,128)(2,1)S(1)} %get-tuple-element.214), channel_id=1, source_target_pairs={{28,24},{24,28},{20,16},{16,20},{12,8},{8,12},{29,25},{25,29},{21,... | collective-permute-start | bytes 786440 | tf_op jit(solution)/shard_map/ppermute | solution.py:327
  137.4 9.1 %collective-permute-start.26 = (bf16[64,2048]{1,0:T(8,128)(2,1)S(1)}, bf16[64,2048]{1,0:T(8,128)(2,1)S(1)}, u32[]{:S(2)}, u32[]{:S(2)}) collective-permute-start(bf16[64,2048]{1,0:T(8,128)(2,1)S(1)} %get-tuple-element.212), channel_id=1, source_target_pairs={{0,4},{4,0},{8,12},{12,8},{16,20},{20,16},{24,28},{28,24},{1,5},{5... | collective-permute-start | bytes 786440 | tf_op jit(solution)/shard_map/ppermute | solution.py:327
  148.1 9.4 %collective-permute-start.29 = (bf16[64,2048]{1,0:T(8,128)(2,1)S(1)}, bf16[64,2048]{1,0:T(8,128)(2,1)S(1)}, u32[]{:S(2)}, u32[]{:S(2)}) collective-permute-start(bf16[64,2048]{1,0:T(8,128)(2,1)S(1)} %get-tuple-element.220), channel_id=1, source_target_pairs={{28,20},{24,16},{20,12},{16,8},{12,4},{8,0},{29,21},{25,17},{21,13... | collective-permute-start | bytes 786440 | tf_op jit(solution)/shard_map/ppermute | solution.py:332
  149.4 8.1 %collective-permute-start.30 = (bf16[64,2048]{1,0:T(8,128)(2,1)S(1)}, bf16[64,2048]{1,0:T(8,128)(2,1)S(1)}, u32[]{:S(2)}, u32[]{:S(2)}) collective-permute-start(bf16[64,2048]{1,0:T(8,128)(2,1)S(1)} %get-tuple-element.221), channel_id=1, source_target_pairs={{28,24},{24,28},{20,16},{16,20},{12,8},{8,12},{4,0},{0,4},{29,25},... | collective-permute-start | bytes 786440 | tf_op jit(solution)/shard_map/ppermute | solution.py:327
  159.1 11.7 %collective-permute-start.31 = (bf16[64,2048]{1,0:T(8,128)(2,1)S(1)}, bf16[64,2048]{1,0:T(8,128)(2,1)S(1)}, u32[]{:S(2)}, u32[]{:S(2)}) collective-permute-start(bf16[64,2048]{1,0:T(8,128)(2,1)S(1)} %get-tuple-element.229), channel_id=1, source_target_pairs={{20,12},{16,8},{12,4},{8,0},{21,13},{17,9},{13,5},{9,1},{22,14},{1... | collective-permute-start | bytes 786440 | tf_op jit(solution)/shard_map/ppermute | solution.py:332
  160.4 10.4 %collective-permute-start.32 = (bf16[64,2048]{1,0:T(8,128)(2,1)S(1)}, bf16[64,2048]{1,0:T(8,128)(2,1)S(1)}, u32[]{:S(2)}, u32[]{:S(2)}) collective-permute-start(bf16[64,2048]{1,0:T(8,128)(2,1)S(1)} %get-tuple-element.230), channel_id=1, source_target_pairs={{20,16},{16,20},{12,8},{8,12},{4,0},{0,4},{21,17},{17,21},{13,9},{... | collective-permute-start | bytes 786440 | tf_op jit(solution)/shard_map/ppermute | solution.py:327
  172.3 11.1 %collective-permute-start.33 = (bf16[64,2048]{1,0:T(8,128)(2,1)S(1)}, bf16[64,2048]{1,0:T(8,128)(2,1)S(1)}, u32[]{:S(2)}, u32[]{:S(2)}) collective-permute-start(bf16[64,2048]{1,0:T(8,128)(2,1)S(1)} %get-tuple-element.243), channel_id=1, source_target_pairs={{12,4},{8,0},{13,5},{9,1},{14,6},{10,2},{15,7},{11,3}} | collective-permute-start | bytes 786440 | tf_op jit(solution)/shard_map/ppermute | solution.py:332
  173.6 9.8 %collective-permute-start.34 = (bf16[64,2048]{1,0:T(8,128)(2,1)S(1)}, bf16[64,2048]{1,0:T(8,128)(2,1)S(1)}, u32[]{:S(2)}, u32[]{:S(2)}) collective-permute-start(bf16[64,2048]{1,0:T(8,128)(2,1)S(1)} %get-tuple-element.244), channel_id=1, source_target_pairs={{12,8},{8,12},{4,0},{0,4},{13,9},{9,13},{5,1},{1,5},{14,10},{10,14... | collective-permute-start | bytes 786440 | tf_op jit(solution)/shard_map/ppermute | solution.py:327
  185.7 12.0 %collective-permute-start.35 = (bf16[64,2048]{1,0:T(8,128)(2,1)S(1)}, bf16[64,2048]{1,0:T(8,128)(2,1)S(1)}, u32[]{:S(2)}, u32[]{:S(2)}) collective-permute-start(bf16[64,2048]{1,0:T(8,128)(2,1)S(1)} %get-tuple-element.257), channel_id=1, source_target_pairs={{4,0},{0,4},{5,1},{1,5},{6,2},{2,6},{7,3},{3,7}} | collective-permute-start | bytes 786440 | tf_op jit(solution)/shard_map/ppermute | solution.py:327
  210.9 7.9 %collective-permute-start.36 = (f32[3,10240]{1,0:T(4,128)}, f32[3,10240]{1,0:T(4,128)S(1)}, u32[]{:S(2)}, u32[]{:S(2)}) collective-permute-start(f32[3,10240]{1,0:T(4,128)} %get-tuple-element.279), channel_id=1, source_target_pairs={{4,0},{8,4},{12,8},{16,12},{20,16},{24,20},{28,24},{5,1},{9,5},{13... | collective-permute-start | bytes 368648 | tf_op jit(solution)/shard_map/ppermute | solution.py:512
  214.4 16.4 %all-to-all-start = ((f32[32,1,2560]{2,1,0:T(1,128)}), f32[32,1,2560]{2,1,0:T(1,128)S(1)}, u32[]{:S(2)}, u32[]{:S(2)}) async-start(f32[32,1,2560]{2,1,0:T(1,128)} %all_to_all.13), calls=%async_computation | async-start | bytes 655360 | tf_op jit(solution)/shard_map/all_to_all | solution.py:529
  231.7 10.3 %all-to-all-start.1 = ((f32[8,1,2560]{2,1,0:T(1,128)}), f32[8,1,2560]{2,1,0:T(1,128)S(1)}, u32[]{:S(2)}, u32[]{:S(2)}) async-start(f32[8,1,2560]{2,1,0:T(1,128)} %broadcast_in_dim.49), calls=%async_computation.1 | async-start | bytes 163840 | tf_op jit(solution)/shard_map/all_to_all | solution.py:532

commit v5 on v4

--- a/solution.py
+++ b/solution.py
@@ -480,6 +480,7 @@
 
     fore, aft = Chain(CHUNKS, rates, sides, False), Chain(CHUNKS, rates, sides, True)
     depth, steps = fore.depth, fore.steps
+    skip_grad = None
     fronts, mids, backs, got, got_back = [], [], [], [], []
     for u in range(CHUNKS + 2 * depth + 1):
         if u < CHUNKS:
@@ -490,8 +491,10 @@
         if depth <= u < depth + CHUNKS:
             mids.append(middle(u - depth))
             got_back.append(fore.swap(mids[-1][4]))
+        skip_grads = [jnp.sum(mids[-1][7][1].reshape(heads, HEAD_DIM), axis=1)] if u == depth + CHUNKS else []
+        skip_grad = skip_grads[0] if skip_grads else skip_grad
         if depth + 1 <= u < depth + 1 + steps:
-            aft.step(u - depth - 1, [m[3] for m in mids], got_back, *[b[2] for b in backs[-1:]])
+            aft.step(u - depth - 1, [m[3] for m in mids], got_back, *[b[2] for b in backs[-1:]], *skip_grads)
         if u >= 2 * depth + 1:
             backs.append(back(u - 2 * depth - 1))
 
@@ -518,7 +521,6 @@
         fixed.append(row)
     grad_xbc = lax.dynamic_update_slice(gx, jnp.stack(fixed).astype(BF16), (length - HALO, 0))
 
-    skip_grad = jnp.sum(sums[1].reshape(heads, HEAD_DIM), axis=1)
     extra_row = pack_row(
         sums[0].reshape(shards, g_loc), hs[0].reshape(shards, h_loc), hs[1].reshape(shards, h_loc),
         skip_grad.reshape(shards, h_loc)).reshape(1, channels)

time: 246 us -> 258 us (1.049)
  local copies, waits for them, and re-layouts: 15.8 us -> 27.3 us
    unnamed x16 -> x80, local copies, waits for them, and re-layouts: 3.62 us -> 15.1 us
  transfers between devices with their start and end apart: 39 -> 39, of which waited for: 11 -> 11; matrix products, arithmetic and copies ran while one was open for 5% -> 5% of each run, Pallas kernels for 30% -> 29%
where the time goes in v5:
time: 258 us; the launch traced here: 256 us
  Pallas kernels  101 us (39%)
  starting transfers between devices  68.9 us (27%)
  waiting for transfers between devices  47.3 us (18%)
  local copies, waits for them, and re-layouts  27.3 us (11%)
  blocking collectives  6.12 us (2%)
  other arithmetic  4.19 us (2%)
    pallas_call x14, Pallas kernels, run(): return call(*kept, *[in_hbm(v) for v in into])  74.3 us
    ppermute x22, starting transfers between devices, swap(): return lax.ppermute(value, 'ctx', pairs)  34.7 us
    pallas_call x14, Pallas kernels, step(): pl.pallas_call(lambda at, *refs: hop_kernel(len(carries) > 0, len(owns),...  26.3 us
    ppermute x22, waiting for transfers between devices, swap(): return lax.ppermute(value, 'ctx', pairs)  20.9 us
    ppermute x12, starting transfers between devices, up(): return lax.ppermute(value, 'ctx', pairs) if pairs else None  19.7 us
    unnamed x80, local copies, waits for them, and re-layouts  15.1 us
    all_to_all x1, waiting for transfers between devices, body(): lax.all_to_all(parts, ('ctx', 'fsdp'), 0, 0, tiled=True)  10.2 us
    ppermute x12, waiting for transfers between devices, up(): return lax.ppermute(value, 'ctx', pairs) if pairs else None  9.09 us
  transfers between devices with their start and end apart: 39, of which 11 were waited for; matrix products, arithmetic and copies ran while one was open for 5% of the time, Pallas kernels for 29%

profile of v5, /device:TPU:0, one launch (start us, length us, event | category | flops | bytes accessed | tf_op | source)
XLA Modules:
  0.0 256.0 jit_solution(8151307730548646069)
XLA Ops:
  1.6 4.8 %collective-permute-start = (bf16[3,10240]{1,0:T(4,128)(2,1)S(1)}, bf16[3,10240]{1,0:T(4,128)(2,1)S(1)}, u32[]{:S(2)}, u32[]{:S(2)}) collective-permute-start(bf16[3,10240]{1,0:T(4,128)(2,1)S(1)} %slice_bitcast_fusion), channel_id=1, source_target_pairs={{0,4},{4,8},{8,12},{12,16},{16,20},{20,24},{24,28},{1,5},{5,9},{9,... | collective-permute-start | bytes 184328 | tf_op jit(solution)/shard_map/ppermute | solution.py:388
  8.9 6.1 %all_gather.3.refs_2_.refs_8_ = f32[8,10240]{1,0:T(8,128)S(1)} all-gather(f32[8,2560]{1,0:T(8,128)S(1)} %maximum_maximum_fusion.1), channel_id=1, replica_groups=mesh['ctx'=8,'fsdp'=4] {'fsdp'}, dimensions={1}, use_global_device_ids=true | all-gather | bytes 409600 | tf_op jit(solution)/shard_map/all_gather | solution.py:396
  17.2 3.6 %keys.1 = (bf16[128,2048]{1,0:T(8,128)(2,1)}, f32[128,128]{1,0:T(8,128)}, f32[128,128]{1,0:T(8,128)}, f32[1,8192]{1,0:T(1,128)}) custom-call(bf16[128,10240]{1,0:T(8,128)(2,1)} %bitcast.39, bf16[3,10240]{1,0:T(4,128)(2,1)} %copy-done.35, f32[8,10240]{1,0:T(8,128)} %copy-done.34, bf16[128,128]{1,0:T(8,128)(2,1)} %bitcast.66, f32[1,128]{1,0:T(1,128)} %reshape.110.refs_4_, ...), custom_call_target="tpu_custom_call" | custom-call | tf_op jit(solution)/shard_map/keys/pallas_call | solution.py:282
  20.8 3.8 %front.4 = (bf16[128,2048]{1,0:T(8,128)(2,1)}, bf16[128,2048]{1,0:T(8,128)(2,1)}, bf16[64,2048]{1,0:T(8,128)(2,1)S(1)}, bf16[64,2048]{1,0:T(8,128)(2,1)S(1)}) custom-call(bf16[128,10240]{1,0:T(8,128)(2,1)} %bitcast.40, bf16[3,10240]{1,0:T(4,128)(2,1)} %copy-done.35, f32[8,10240]{1,0:T(8,128)} %copy-done.34, ...), custom_call_target="tpu_custom_call" | custom-call | tf_op jit(solution)/shard_map/front/pallas_call | solution.py:282
  24.7 1.6 collective-permute-start.2
  26.7 3.9 %front.5 = (bf16[128,2048]{1,0:T(8,128)(2,1)}, bf16[128,2048]{1,0:T(8,128)(2,1)}, bf16[64,2048]{1,0:T(8,128)(2,1)S(1)}, bf16[64,2048]{1,0:T(8,128)(2,1)S(1)}) custom-call(bf16[128,10240]{1,0:T(8,128)(2,1)} %bitcast.41, bf16[3,10240]{1,0:T(4,128)(2,1)} %copy-done.35, f32[8,10240]{1,0:T(8,128)} %copy-done.34, ...), custom_call_target="tpu_custom_call" | custom-call | tf_op jit(solution)/shard_map/front/pallas_call | solution.py:282
  30.6 1.5 collective-permute-start.3
  32.2 2.4 collective-permute-done.1.refs_1_
  34.6 2.1 hop.7
  36.6 3.5 %collective-permute-start.4 = (bf16[64,2048]{1,0:T(8,128)(2,1)S(1)}, bf16[64,2048]{1,0:T(8,128)(2,1)S(1)}, u32[]{:S(2)}, u32[]{:S(2)}) collective-permute-start(bf16[64,2048]{1,0:T(8,128)(2,1)S(1)} %get-tuple-element.158), channel_id=1, source_target_pairs={{0,8},{4,12},{1,9},{5,13},{2,10},{6,14},{3,11},{7,15}} | collective-permute-start | bytes 786440 | tf_op jit(solution)/shard_map/ppermute | solution.py:332
  40.1 3.8 %front.6 = (bf16[128,2048]{1,0:T(8,128)(2,1)}, bf16[128,2048]{1,0:T(8,128)(2,1)}, bf16[64,2048]{1,0:T(8,128)(2,1)S(1)}, bf16[64,2048]{1,0:T(8,128)(2,1)S(1)}) custom-call(bf16[128,10240]{1,0:T(8,128)(2,1)} %bitcast.42, bf16[3,10240]{1,0:T(4,128)(2,1)} %copy-done.35, f32[8,10240]{1,0:T(8,128)} %copy-done.34, ...), custom_call_target="tpu_custom_call" | custom-call | tf_op jit(solution)/shard_map/front/pallas_call | solution.py:282
  44.0 1.5 collective-permute-start.5
  45.5 2.1 hop.8
  47.6 3.7 %collective-permute-start.6 = (bf16[64,2048]{1,0:T(8,128)(2,1)S(1)}, bf16[64,2048]{1,0:T(8,128)(2,1)S(1)}, u32[]{:S(2)}, u32[]{:S(2)}) collective-permute-start(bf16[64,2048]{1,0:T(8,128)(2,1)S(1)} %get-tuple-element.162), channel_id=1, source_target_pairs={{0,8},{4,12},{8,16},{12,20},{1,9},{5,13},{9,17},{13,21},{2,10},{6,... | collective-permute-start | bytes 786440 | tf_op jit(solution)/shard_map/ppermute | solution.py:332
  51.3 3.9 %front.7 = (bf16[128,2048]{1,0:T(8,128)(2,1)}, bf16[128,2048]{1,0:T(8,128)(2,1)}, bf16[64,2048]{1,0:T(8,128)(2,1)S(1)}, bf16[64,2048]{1,0:T(8,128)(2,1)S(1)}) custom-call(bf16[128,10240]{1,0:T(8,128)(2,1)} %bitcast.43, bf16[3,10240]{1,0:T(4,128)(2,1)} %copy-done.35, f32[8,10240]{1,0:T(8,128)} %copy-done.34, ...), custom_call_target="tpu_custom_call" | custom-call | tf_op jit(solution)/shard_map/front/pallas_call | solution.py:282
  55.2 1.6 collective-permute-start.7
  56.8 2.1 hop.9
  59.0 2.7 %collective-permute-start.8 = (bf16[64,2048]{1,0:T(8,128)(2,1)S(1)}, bf16[64,2048]{1,0:T(8,128)(2,1)S(1)}, u32[]{:S(2)}, u32[]{:S(2)}) collective-permute-start(bf16[64,2048]{1,0:T(8,128)(2,1)S(1)} %get-tuple-element.166), channel_id=1, source_target_pairs={{0,8},{4,12},{8,16},{12,20},{16,24},{20,28},{1,9},{5,13},{9,17},{1... | collective-permute-start | bytes 786440 | tf_op jit(solution)/shard_map/ppermute | solution.py:332
  61.7 3.5 %collective-permute-start.9 = (bf16[64,2048]{1,0:T(8,128)(2,1)}, bf16[64,2048]{1,0:T(8,128)(2,1)}, u32[]{:S(2)}, u32[]{:S(2)}) collective-permute-start(bf16[64,2048]{1,0:T(8,128)(2,1)} %get-tuple-element.168), channel_id=1, source_target_pairs={{0,4},{4,0},{1,5},{5,1},{2,6},{6,2},{3,7},{7,3}} | collective-permute-start | bytes 786440 | tf_op jit(solution)/shard_map/ppermute | solution.py:327
  65.2 2.4 collective-permute-start.10
  67.5 3.5 %collective-permute-start.11 = (bf16[64,2048]{1,0:T(8,128)(2,1)}, bf16[64,2048]{1,0:T(8,128)(2,1)S(1)}, u32[]{:S(2)}, u32[]{:S(2)}) collective-permute-start(bf16[64,2048]{1,0:T(8,128)(2,1)} %get-tuple-element.170), channel_id=1, source_target_pairs={{0,4},{4,0},{8,12},{12,8},{16,20},{20,16},{1,5},{5,1},{9,13},{13,9... | collective-permute-start | bytes 786440 | tf_op jit(solution)/shard_map/ppermute | solution.py:327
  71.0 2.3 hop.10
  73.8 2.0 collective-permute-start.14
  77.4 1.2 collective-permute-done.10.refs_15_.refs_14_
  79.3 3.7 %collective-permute-done.11.refs_16_.refs_15_.refs_14_ = bf16[64,2048]{1,0:T(8,128)(2,1)S(1)} collective-permute-done((bf16[64,2048]{1,0:T(8,128)(2,1)}, bf16[64,2048]{1,0:T(8,128)(2,1)S(1)}, u32[]{:S(2)}, u32[]{:S(2)}) %collective-permute-start.11) | collective-permute-done | bytes 262176 | tf_op jit(solution)/shard_map/ppermute | solution.py:327
  83.0 2.8 %collective-permute-done.12.refs_17_.refs_16_.refs_15_.refs_14_ = bf16[64,2048]{1,0:T(8,128)(2,1)S(1)} collective-permute-done((bf16[64,2048]{1,0:T(8,128)(2,1)}, bf16[64,2048]{1,0:T(8,128)(2,1)S(1)}, u32[]{:S(2)}, u32[]{:S(2)}) %collective-permute-start.12) | collective-permute-done | bytes 262176 | tf_op jit(solution)/shard_map/ppermute | solution.py:327
  88.8 5.3 %middle.4 = (bf16[128,2048]{1,0:T(8,128)(2,1)}, bf16[128,2048]{1,0:T(8,128)(2,1)}, bf16[128,2048]{1,0:T(8,128)(2,1)}, bf16[64,2048]{1,0:T(8,128)(2,1)S(1)}, bf16...) custom-call(bf16[128,2048]{1,0:T(8,128)(2,1)} %get-tuple-element.151.refs_0_, ...), custom_call_target="tpu_custom_call" | custom-call | tf_op jit(solution)/shard_map/middle/pallas_call | solution.py:282
  95.4 1.8 hop.11
  98.6 2.0 collective-permute-done.13.refs_3_.refs_4_.refs_5_.refs_6_
  100.6 1.4 hop_back.7
  104.3 5.3 %middle.5 = (bf16[128,2048]{1,0:T(8,128)(2,1)}, bf16[128,2048]{1,0:T(8,128)(2,1)}, bf16[128,2048]{1,0:T(8,128)(2,1)}, bf16[64,2048]{1,0:T(8,128)(2,1)S(1)}, bf16...) custom-call(bf16[128,2048]{1,0:T(8,128)(2,1)} %get-tuple-element.178, ...), custom_call_target="tpu_custom_call", output_to_operand_aliasing={{6}: (18, {}), {7}: (19, {})} | custom-call | tf_op jit(solution)/shard_map/middle/pallas_call | solution.py:282
  110.9 1.6 hop.12
  113.9 2.2 collective-permute-done.16.refs_5_.refs_6_.refs_7_
  116.1 1.5 hop_back.8
  119.7 5.3 %middle.6 = (bf16[128,2048]{1,0:T(8,128)(2,1)}, bf16[128,2048]{1,0:T(8,128)(2,1)}, bf16[128,2048]{1,0:T(8,128)(2,1)}, bf16[64,2048]{1,0:T(8,128)(2,1)S(1)}, bf16...) custom-call(bf16[128,2048]{1,0:T(8,128)(2,1)} %get-tuple-element.191, ...), custom_call_target="tpu_custom_call", output_to_operand_aliasing={{6}: (18, {}), {7}: (19, {})} | custom-call | tf_op jit(solution)/shard_map/middle/pallas_call | solution.py:282
  126.3 2.2 hop.13
  129.2 2.3 collective-permute-done.21.refs_7_.refs_8_
  131.5 2.2 hop_back.9
  133.6 1.3 collective-permute-start.27
  135.6 5.3 %middle.7 = (bf16[128,2048]{1,0:T(8,128)(2,1)}, bf16[128,2048]{1,0:T(8,128)(2,1)}, bf16[128,2048]{1,0:T(8,128)(2,1)}, bf16[64,2048]{1,0:T(8,128)(2,1)S(1)}, bf16...) custom-call(bf16[128,2048]{1,0:T(8,128)(2,1)} %get-tuple-element.204, ...), custom_call_target="tpu_custom_call", output_to_operand_aliasing={{6}: (18, {}), {7}: (19, {})} | custom-call | tf_op jit(solution)/shard_map/middle/pallas_call | solution.py:282
  143.6 6.6 %collective-permute-done.26.refs_9_ = bf16[64,2048]{1,0:T(8,128)(2,1)S(1)} collective-permute-done((bf16[64,2048]{1,0:T(8,128)(2,1)}, bf16[64,2048]{1,0:T(8,128)(2,1)S(1)}, u32[]{:S(2)}, u32[]{:S(2)}) %collective-permute-start.26) | collective-permute-done | bytes 262176 | tf_op jit(solution)/shard_map/ppermute | solution.py:327
  150.2 1.6 hop_back.10
  151.8 1.3 collective-permute-start.29
  153.9 9.1 %collective-permute-done.29.refs_10_ = bf16[64,2048]{1,0:T(8,128)(2,1)S(1)} collective-permute-done((bf16[64,2048]{1,0:T(8,128)(2,1)S(1)}, bf16[64,2048]{1,0:T(8,128)(2,1)S(1)}, u32[]{:S(2)}, u32[]{:S(2)}) %collective-permute-start.29) | collective-permute-done | bytes 262176 | tf_op jit(solution)/shard_map/ppermute | solution.py:332
  163.0 1.6 hop_back.11
  164.5 1.3 collective-permute-start.31
  165.8 2.5 collective-permute-start.32
  172.2 7.0 %back.4 = (f32[2,128,256]{2,1,0:T(8,128)}, f32[128,128]{1,0:T(8,128)}, f32[8,128]{1,0:T(8,128)S(1)}, bf16[128,10240]{1,0:T(8,128)(2,1)}, f32[3,10240]{1,0:T(4,12...) custom-call(bf16[128,2048]{1,0:T(8,128)(2,1)} %get-tuple-element.147.refs_3_.refs_1_.refs_2_.refs_0_, ...), custom_call_target="tpu_custom_call" | custom-call | tf_op jit(solution)/shard_map/back/pallas_call | solution.py:282
  179.2 1.6 hop_back.12
  180.8 1.3 collective-permute-start.33
  182.1 3.5 %collective-permute-start.34 = (bf16[64,2048]{1,0:T(8,128)(2,1)S(1)}, bf16[64,2048]{1,0:T(8,128)(2,1)S(1)}, u32[]{:S(2)}, u32[]{:S(2)}) collective-permute-start(bf16[64,2048]{1,0:T(8,128)(2,1)S(1)} %get-tuple-element.245), channel_id=1, source_target_pairs={{12,8},{8,12},{4,0},{0,4},{13,9},{9,13},{5,1},{1,5},{14,10},{10,14... | collective-permute-start | bytes 786440 | tf_op jit(solution)/shard_map/ppermute | solution.py:327
  185.6 7.1 %back.5 = (f32[2,128,256]{2,1,0:T(8,128)}, f32[128,128]{1,0:T(8,128)}, f32[8,128]{1,0:T(8,128)S(1)}, bf16[128,10240]{1,0:T(8,128)(2,1)}, f32[3,10240]{1,0:T(4,12...) custom-call(bf16[128,2048]{1,0:T(8,128)(2,1)} %get-tuple-element.147, ...), custom_call_target="tpu_custom_call", output_to_operand_aliasing={{3}: (21, {}), {4}: (22, {}), {5}: (23, {}), {6}: (24, {})} | custom-call | tf_op jit(solution)/shard_map/back/pallas_call | solution.py:282
  193.4 2.3 hop_back.13
  196.5 2.5 collective-permute-start.35
  202.0 7.1 %back.6 = (f32[2,128,256]{2,1,0:T(8,128)}, f32[128,128]{1,0:T(8,128)}, f32[8,128]{1,0:T(8,128)S(1)}, bf16[128,10240]{1,0:T(8,128)(2,1)}, f32[3,10240]{1,0:T(4,12...) custom-call(bf16[128,2048]{1,0:T(8,128)(2,1)} %get-tuple-element.147, ...), custom_call_target="tpu_custom_call", output_to_operand_aliasing={{3}: (21, {}), {4}: (22, {}), {5}: (23, {}), {6}: (24, {})} | custom-call | tf_op jit(solution)/shard_map/back/pallas_call | solution.py:282
  209.0 7.1 %back.7 = (f32[2,128,256]{2,1,0:T(8,128)}, f32[128,128]{1,0:T(8,128)}, f32[8,128]{1,0:T(8,128)S(1)}, bf16[128,10240]{1,0:T(8,128)(2,1)}, f32[3,10240]{1,0:T(4,12...) custom-call(bf16[128,2048]{1,0:T(8,128)(2,1)} %get-tuple-element.147, ...), custom_call_target="tpu_custom_call", output_to_operand_aliasing={{3}: (21, {}), {4}: (22, {}), {5}: (23, {}), {6}: (24, {})} | custom-call | tf_op jit(solution)/shard_map/back/pallas_call | solution.py:282
  216.1 5.8 %last.1 = (f32[128,128]{1,0:T(8,128)}, f32[8,128]{1,0:T(8,128)S(1)}, bf16[128,10240]{1,0:T(8,128)(2,1)}, f32[3,10240]{1,0:T(4,128)}, f32[3,10240]{1,0:T(4,128)}, /*index=5*/f32[8,10240]{1,0:T(8,128)}) custom-call(bf16[128,10240]{1,0:T(8,128)(2,1)} %bitcast.48, ...), custom_call_target="tpu_custom_call", output_to_operand_aliasing={{2}: (22, {}), {3}: (23, {}), {4}: (24, {}), {5}: (25, {})} | custom-call | tf_op jit(solution)/shard_map/last/pallas_call | solution.py:282
  222.0 1.3 collective-permute-start.36
  225.8 4.5 %all-to-all-start = ((f32[32,1,2560]{2,1,0:T(1,128)}), f32[32,1,2560]{2,1,0:T(1,128)S(1)}, u32[]{:S(2)}, u32[]{:S(2)}) async-start(f32[32,1,2560]{2,1,0:T(1,128)} %all_to_all.13), calls=%async_computation | async-start | bytes 655360 | tf_op jit(solution)/shard_map/all_to_all | solution.py:531
  230.3 1.7 convert_bitcast_fusion.2
  232.1 10.2 %all-to-all-done = f32[32,1,2560]{2,1,0:T(1,128)S(1)} async-done(((f32[32,1,2560]{2,1,0:T(1,128)}), f32[32,1,2560]{2,1,0:T(1,128)S(1)}, u32[]{:S(2)}, u32[]{:S(2)}) %all-to-all-start) | async-done | bytes 327712 | tf_op jit(solution)/shard_map/all_to_all | solution.py:531
  243.2 3.4 %all-to-all-start.1 = ((f32[8,1,2560]{2,1,0:T(1,128)}), f32[8,1,2560]{2,1,0:T(1,128)S(1)}, u32[]{:S(2)}, u32[]{:S(2)}) async-start(f32[8,1,2560]{2,1,0:T(1,128)} %broadcast_in_dim.49), calls=%async_computation.1 | async-start | bytes 163840 | tf_op jit(solution)/shard_map/all_to_all | solution.py:534
  246.7 2.1 dynamic_update_slice.4
  248.8 4.7 %all-to-all-done.1 = f32[8,1,2560]{2,1,0:T(1,128)S(1)} async-done(((f32[8,1,2560]{2,1,0:T(1,128)}), f32[8,1,2560]{2,1,0:T(1,128)S(1)}, u32[]{:S(2)}, u32[]{:S(2)}) %all-to-all-start.1) | async-done | bytes 81952 | tf_op jit(solution)/shard_map/all_to_all | solution.py:534
  (162 shorter events, 41.4 us)
Async XLA Ops:
  1.6 14.9 %collective-permute-start = (bf16[3,10240]{1,0:T(4,128)(2,1)S(1)}, bf16[3,10240]{1,0:T(4,128)(2,1)S(1)}, u32[]{:S(2)}, u32[]{:S(2)}) collective-permute-start(bf16[3,10240]{1,0:T(4,128)(2,1)S(1)} %slice_bitcast_fusion), channel_id=1, source_target_pairs={{0,4},{4,8},{8,12},{12,16},{16,20},{20,24},{24,28},{1,5},{5,9},{9,... | collective-permute-start | bytes 184328 | tf_op jit(solution)/shard_map/ppermute | solution.py:388
  15.0 1.5 copy-start.34
  15.2 9.5 %copy-start.36 = (f32[4,2560]{1,0:T(4,128)}, f32[4,2560]{1,0:T(4,128)S(1)}, u32[]{:S(2)}) copy-start(f32[4,2560]{1,0:T(4,128)S(1)} %reshape_squeeze.15) | copy-start | bytes 122884
  24.7 9.9 %collective-permute-start.2 = (bf16[64,2048]{1,0:T(8,128)(2,1)S(1)}, bf16[64,2048]{1,0:T(8,128)(2,1)S(1)}, u32[]{:S(2)}, u32[]{:S(2)}) collective-permute-start(bf16[64,2048]{1,0:T(8,128)(2,1)S(1)} %get-tuple-element.154), channel_id=1, source_target_pairs={{0,4},{4,0},{8,12},{12,8},{16,20},{20,16},{24,28},{28,24},{1,5},{5... | collective-permute-start | bytes 786440 | tf_op jit(solution)/shard_map/ppermute | solution.py:327
  26.3 8.3 %collective-permute-start.1 = (f32[1,8192]{1,0:T(1,128)}, f32[1,8192]{1,0:T(1,128)S(1)}, u32[]{:S(2)}, u32[]{:S(2)}) collective-permute-start(f32[1,8192]{1,0:T(1,128)} %get-tuple-element.149.refs_5_.refs_0_.refs_10_), channel_id=1, source_target_pairs={{0,4},{4,0},{8,12},{12,8},{16,20},{20,16},{24,28},{28,24},{1,5},{5... | collective-permute-start | bytes 98312 | tf_op jit(solution)/shard_map/ppermute | solution.py:437
  30.6 14.9 %collective-permute-start.3 = (bf16[64,2048]{1,0:T(8,128)(2,1)S(1)}, bf16[64,2048]{1,0:T(8,128)(2,1)S(1)}, u32[]{:S(2)}, u32[]{:S(2)}) collective-permute-start(bf16[64,2048]{1,0:T(8,128)(2,1)S(1)} %get-tuple-element.157), channel_id=1, source_target_pairs={{0,4},{4,0},{8,12},{12,8},{16,20},{20,16},{24,28},{28,24},{1,5},{5... | collective-permute-start | bytes 786440 | tf_op jit(solution)/shard_map/ppermute | solution.py:327
  36.6 18.6 %copy-start.30 = (bf16[64,2048]{1,0:T(8,128)(2,1)}, bf16[64,2048]{1,0:T(8,128)(2,1)S(1)}, u32[]{:S(2)}) copy-start(bf16[64,2048]{1,0:T(8,128)(2,1)S(1)} %get-tuple-element.155.refs_10_) | copy-start | bytes 786436
  36.6 8.9 %collective-permute-start.4 = (bf16[64,2048]{1,0:T(8,128)(2,1)S(1)}, bf16[64,2048]{1,0:T(8,128)(2,1)S(1)}, u32[]{:S(2)}, u32[]{:S(2)}) collective-permute-start(bf16[64,2048]{1,0:T(8,128)(2,1)S(1)} %get-tuple-element.158), channel_id=1, source_target_pairs={{0,8},{4,12},{1,9},{5,13},{2,10},{6,14},{3,11},{7,15}} | collective-permute-start | bytes 786440 | tf_op jit(solution)/shard_map/ppermute | solution.py:332
  44.0 12.9 %collective-permute-start.5 = (bf16[64,2048]{1,0:T(8,128)(2,1)S(1)}, bf16[64,2048]{1,0:T(8,128)(2,1)S(1)}, u32[]{:S(2)}, u32[]{:S(2)}) collective-permute-start(bf16[64,2048]{1,0:T(8,128)(2,1)S(1)} %get-tuple-element.161), channel_id=1, source_target_pairs={{0,4},{4,0},{8,12},{12,8},{16,20},{20,16},{24,28},{28,24},{1,5},{5... | collective-permute-start | bytes 786440 | tf_op jit(solution)/shard_map/ppermute | solution.py:327
  47.6 7.5 %copy-start.16 = (bf16[64,2048]{1,0:T(8,128)(2,1)}, bf16[64,2048]{1,0:T(8,128)(2,1)S(1)}, u32[]{:S(2)}) copy-start(bf16[64,2048]{1,0:T(8,128)(2,1)S(1)} %get-tuple-element.159.refs_11_.refs_10_) | copy-start | bytes 786436
  47.6 9.2 %collective-permute-start.6 = (bf16[64,2048]{1,0:T(8,128)(2,1)S(1)}, bf16[64,2048]{1,0:T(8,128)(2,1)S(1)}, u32[]{:S(2)}, u32[]{:S(2)}) collective-permute-start(bf16[64,2048]{1,0:T(8,128)(2,1)S(1)} %get-tuple-element.162), channel_id=1, source_target_pairs={{0,8},{4,12},{8,16},{12,20},{1,9},{5,13},{9,17},{13,21},{2,10},{6,... | collective-permute-start | bytes 786440 | tf_op jit(solution)/shard_map/ppermute | solution.py:332
  55.2 55.7 %copy-start.2 = (bf16[64,2048]{1,0:T(8,128)(2,1)}, bf16[64,2048]{1,0:T(8,128)(2,1)S(1)}, u32[]{:S(2)}) copy-start(bf16[64,2048]{1,0:T(8,128)(2,1)S(1)} %get-tuple-element.164.refs_5_) | copy-start | bytes 786436
  55.2 20.6 %copy-start.37 = (f32[4,2560]{1,0:T(4,128)S(1)}, f32[4,2560]{1,0:T(4,128)}, u32[]{:S(2)}) copy-start(f32[4,2560]{1,0:T(4,128)} %copy-done.36) | copy-start | bytes 122884
  55.2 15.8 %collective-permute-start.7 = (bf16[64,2048]{1,0:T(8,128)(2,1)S(1)}, bf16[64,2048]{1,0:T(8,128)(2,1)S(1)}, u32[]{:S(2)}, u32[]{:S(2)}) collective-permute-start(bf16[64,2048]{1,0:T(8,128)(2,1)S(1)} %get-tuple-element.165), channel_id=1, source_target_pairs={{0,4},{4,0},{8,12},{12,8},{16,20},{20,16},{24,28},{28,24},{1,5},{5... | collective-permute-start | bytes 786440 | tf_op jit(solution)/shard_map/ppermute | solution.py:327
  59.0 45.3 %copy-start.6 = (bf16[64,2048]{1,0:T(8,128)(2,1)}, bf16[64,2048]{1,0:T(8,128)(2,1)S(1)}, u32[]{:S(2)}) copy-start(bf16[64,2048]{1,0:T(8,128)(2,1)S(1)} %get-tuple-element.163.refs_12_.refs_11_.refs_10_) | copy-start | bytes 786436
  59.0 12.1 %collective-permute-start.8 = (bf16[64,2048]{1,0:T(8,128)(2,1)S(1)}, bf16[64,2048]{1,0:T(8,128)(2,1)S(1)}, u32[]{:S(2)}, u32[]{:S(2)}) collective-permute-start(bf16[64,2048]{1,0:T(8,128)(2,1)S(1)} %get-tuple-element.166), channel_id=1, source_target_pairs={{0,8},{4,12},{8,16},{12,20},{16,24},{20,28},{1,9},{5,13},{9,17},{1... | collective-permute-start | bytes 786440 | tf_op jit(solution)/shard_map/ppermute | solution.py:332
  61.7 15.7 %collective-permute-start.9 = (bf16[64,2048]{1,0:T(8,128)(2,1)}, bf16[64,2048]{1,0:T(8,128)(2,1)}, u32[]{:S(2)}, u32[]{:S(2)}) collective-permute-start(bf16[64,2048]{1,0:T(8,128)(2,1)} %get-tuple-element.168), channel_id=1, source_target_pairs={{0,4},{4,0},{1,5},{5,1},{2,6},{6,2},{3,7},{7,3}} | collective-permute-start | bytes 786440 | tf_op jit(solution)/shard_map/ppermute | solution.py:327
  65.2 13.5 %collective-permute-start.10 = (bf16[64,2048]{1,0:T(8,128)(2,1)}, bf16[64,2048]{1,0:T(8,128)(2,1)S(1)}, u32[]{:S(2)}, u32[]{:S(2)}) collective-permute-start(bf16[64,2048]{1,0:T(8,128)(2,1)} %get-tuple-element.169), channel_id=1, source_target_pairs={{0,4},{4,0},{8,12},{12,8},{1,5},{5,1},{9,13},{13,9},{2,6},{6,2},{1... | collective-permute-start | bytes 786440 | tf_op jit(solution)/shard_map/ppermute | solution.py:327
  67.5 15.5 %collective-permute-start.11 = (bf16[64,2048]{1,0:T(8,128)(2,1)}, bf16[64,2048]{1,0:T(8,128)(2,1)S(1)}, u32[]{:S(2)}, u32[]{:S(2)}) collective-permute-start(bf16[64,2048]{1,0:T(8,128)(2,1)} %get-tuple-element.170), channel_id=1, source_target_pairs={{0,4},{4,0},{8,12},{12,8},{16,20},{20,16},{1,5},{5,1},{9,13},{13,9... | collective-permute-start | bytes 786440 | tf_op jit(solution)/shard_map/ppermute | solution.py:327
  71.0 24.4 %copy-start.4 = (bf16[64,2048]{1,0:T(8,128)(2,1)}, bf16[64,2048]{1,0:T(8,128)(2,1)S(1)}, u32[]{:S(2)}) copy-start(bf16[64,2048]{1,0:T(8,128)(2,1)S(1)} %collective-permute-done.7.refs_9_) | copy-start | bytes 786436
  73.3 12.5 %collective-permute-start.12 = (bf16[64,2048]{1,0:T(8,128)(2,1)}, bf16[64,2048]{1,0:T(8,128)(2,1)S(1)}, u32[]{:S(2)}, u32[]{:S(2)}) collective-permute-start(bf16[64,2048]{1,0:T(8,128)(2,1)} %get-tuple-element.171), channel_id=1, source_target_pairs={{0,4},{4,0},{8,12},{12,8},{16,20},{20,16},{24,28},{28,24},{1,5},{5... | collective-permute-start | bytes 786440 | tf_op jit(solution)/shard_map/ppermute | solution.py:327
  73.8 21.6 %collective-permute-start.14 = (bf16[64,2048]{1,0:T(8,128)(2,1)}, bf16[64,2048]{1,0:T(8,128)(2,1)}, u32[]{:S(2)}, u32[]{:S(2)}) collective-permute-start(bf16[64,2048]{1,0:T(8,128)(2,1)} %get-tuple-element.180), channel_id=1, source_target_pairs={{0,8},{4,12},{8,16},{12,20},{16,24},{20,28},{1,9},{5,13},{9,17},{1... | collective-permute-start | bytes 786440 | tf_op jit(solution)/shard_map/ppermute | solution.py:332
  83.0 11.1 %copy-start.8 = (bf16[64,2048]{1,0:T(8,128)(2,1)}, bf16[64,2048]{1,0:T(8,128)(2,1)S(1)}, u32[]{:S(2)}) copy-start(bf16[64,2048]{1,0:T(8,128)(2,1)S(1)} %collective-permute-done.11.refs_16_.refs_15_.refs_14_) | copy-start | bytes 786436
  85.8 33.8 %copy-start = (bf16[64,2048]{1,0:T(8,128)(2,1)}, bf16[64,2048]{1,0:T(8,128)(2,1)S(1)}, u32[]{:S(2)}) copy-start(bf16[64,2048]{1,0:T(8,128)(2,1)S(1)} %collective-permute-done.12.refs_17_.refs_16_.refs_15_.refs_14_) | copy-start | bytes 786436
  85.8 1.0 copy-start.17
  94.1 10.2 %copy-start.18 = (bf16[64,2048]{1,0:T(8,128)(2,1)S(1)}, bf16[64,2048]{1,0:T(8,128)(2,1)}, u32[]{:S(2)}) copy-start(bf16[64,2048]{1,0:T(8,128)(2,1)} %copy-done.16) | copy-start | bytes 786436
  94.1 10.2 %copy-start.21 = (bf16[64,2048]{1,0:T(8,128)(2,1)S(1)}, bf16[64,2048]{1,0:T(8,128)(2,1)}, u32[]{:S(2)}) copy-start(bf16[64,2048]{1,0:T(8,128)(2,1)} %copy-done.19) | copy-start | bytes 786436
  94.1 10.2 %copy-start.9 = (bf16[64,2048]{1,0:T(8,128)(2,1)S(1)}, bf16[64,2048]{1,0:T(8,128)(2,1)}, u32[]{:S(2)}) copy-start(bf16[64,2048]{1,0:T(8,128)(2,1)} %copy-done.8) | copy-start | bytes 786436
  94.1 6.4 %collective-permute-start.13 = (bf16[64,2048]{1,0:T(8,128)(2,1)S(1)}, bf16[64,2048]{1,0:T(8,128)(2,1)S(1)}, u32[]{:S(2)}, u32[]{:S(2)}) collective-permute-start(bf16[64,2048]{1,0:T(8,128)(2,1)S(1)} %get-tuple-element.176), channel_id=1, source_target_pairs={{0,4},{4,0},{8,12},{12,8},{16,20},{20,16},{24,28},{28,24},{1,5},{5... | collective-permute-start | bytes 786440 | tf_op jit(solution)/shard_map/ppermute | solution.py:327
  97.2 7.1 %collective-permute-start.15 = (bf16[64,2048]{1,0:T(8,128)(2,1)S(1)}, bf16[64,2048]{1,0:T(8,128)(2,1)S(1)}, u32[]{:S(2)}, u32[]{:S(2)}) collective-permute-start(bf16[64,2048]{1,0:T(8,128)(2,1)S(1)} %get-tuple-element.182), channel_id=1, source_target_pairs={{8,12},{12,8},{16,20},{20,16},{24,28},{28,24},{9,13},{13,9},{17,21... | collective-permute-start | bytes 786440 | tf_op jit(solution)/shard_map/ppermute | solution.py:327
  97.9 13.0 %collective-permute-start.19 = (bf16[64,2048]{1,0:T(8,128)(2,1)S(1)}, bf16[64,2048]{1,0:T(8,128)(2,1)S(1)}, u32[]{:S(2)}, u32[]{:S(2)}) collective-permute-start(bf16[64,2048]{1,0:T(8,128)(2,1)S(1)} %get-tuple-element.193), channel_id=1, source_target_pairs={{8,16},{12,20},{16,24},{20,28},{9,17},{13,21},{17,25},{21,29},{10,... | collective-permute-start | bytes 786440 | tf_op jit(solution)/shard_map/ppermute | solution.py:332
  102.7 11.1 %collective-permute-start.17 = (bf16[64,2048]{1,0:T(8,128)(2,1)S(1)}, bf16[64,2048]{1,0:T(8,128)(2,1)S(1)}, u32[]{:S(2)}, u32[]{:S(2)}) collective-permute-start(bf16[64,2048]{1,0:T(8,128)(2,1)S(1)} %get-tuple-element.187), channel_id=1, source_target_pairs={{28,20},{24,16},{29,21},{25,17},{30,22},{26,18},{31,23},{27,19}} | collective-permute-start | bytes 786440 | tf_op jit(solution)/shard_map/ppermute | solution.py:332
  103.4 10.5 %collective-permute-start.18 = (bf16[64,2048]{1,0:T(8,128)(2,1)S(1)}, bf16[64,2048]{1,0:T(8,128)(2,1)S(1)}, u32[]{:S(2)}, u32[]{:S(2)}) collective-permute-start(bf16[64,2048]{1,0:T(8,128)(2,1)S(1)} %get-tuple-element.188), channel_id=1, source_target_pairs={{28,24},{24,28},{29,25},{25,29},{30,26},{26,30},{31,27},{27,31}} | collective-permute-start | bytes 786440 | tf_op jit(solution)/shard_map/ppermute | solution.py:327
  104.3 6.6 %copy-start.5 = (bf16[64,2048]{1,0:T(8,128)(2,1)S(1)}, bf16[64,2048]{1,0:T(8,128)(2,1)}, u32[]{:S(2)}) copy-start(bf16[64,2048]{1,0:T(8,128)(2,1)} %copy-done.4) | copy-start | bytes 786436
  109.6 10.1 %copy-start.7 = (bf16[64,2048]{1,0:T(8,128)(2,1)S(1)}, bf16[64,2048]{1,0:T(8,128)(2,1)}, u32[]{:S(2)}) copy-start(bf16[64,2048]{1,0:T(8,128)(2,1)} %copy-done.6) | copy-start | bytes 786436
  109.6 6.4 %collective-permute-start.16 = (bf16[64,2048]{1,0:T(8,128)(2,1)S(1)}, bf16[64,2048]{1,0:T(8,128)(2,1)S(1)}, u32[]{:S(2)}, u32[]{:S(2)}) collective-permute-start(bf16[64,2048]{1,0:T(8,128)(2,1)S(1)} %get-tuple-element.186), channel_id=1, source_target_pairs={{0,4},{4,0},{8,12},{12,8},{16,20},{20,16},{24,28},{28,24},{1,5},{5... | collective-permute-start | bytes 786440 | tf_op jit(solution)/shard_map/ppermute | solution.py:327
  112.5 7.2 %collective-permute-start.20 = (bf16[64,2048]{1,0:T(8,128)(2,1)S(1)}, bf16[64,2048]{1,0:T(8,128)(2,1)S(1)}, u32[]{:S(2)}, u32[]{:S(2)}) collective-permute-start(bf16[64,2048]{1,0:T(8,128)(2,1)S(1)} %get-tuple-element.195), channel_id=1, source_target_pairs={{16,20},{20,16},{24,28},{28,24},{17,21},{21,17},{25,29},{29,25},{1... | collective-permute-start | bytes 786440 | tf_op jit(solution)/shard_map/ppermute | solution.py:327
  113.2 13.1 %collective-permute-start.24 = (bf16[64,2048]{1,0:T(8,128)(2,1)S(1)}, bf16[64,2048]{1,0:T(8,128)(2,1)S(1)}, u32[]{:S(2)}, u32[]{:S(2)}) collective-permute-start(bf16[64,2048]{1,0:T(8,128)(2,1)S(1)} %get-tuple-element.206), channel_id=1, source_target_pairs={{16,24},{20,28},{17,25},{21,29},{18,26},{22,30},{19,27},{23,31}} | collective-permute-start | bytes 786440 | tf_op jit(solution)/shard_map/ppermute | solution.py:332
  113.9 5.8 %copy-start.28 = (bf16[64,2048]{1,0:T(8,128)(2,1)}, bf16[64,2048]{1,0:T(8,128)(2,1)S(1)}, u32[]{:S(2)}) copy-start(bf16[64,2048]{1,0:T(8,128)(2,1)S(1)} %collective-permute-done.18.refs_17_) | copy-start | bytes 786436
  118.3 10.9 %collective-permute-start.22 = (bf16[64,2048]{1,0:T(8,128)(2,1)S(1)}, bf16[64,2048]{1,0:T(8,128)(2,1)S(1)}, u32[]{:S(2)}, u32[]{:S(2)}) collective-permute-start(bf16[64,2048]{1,0:T(8,128)(2,1)S(1)} %get-tuple-element.200), channel_id=1, source_target_pairs={{28,20},{24,16},{20,12},{16,8},{29,21},{25,17},{21,13},{17,9},{30,... | collective-permute-start | bytes 786440 | tf_op jit(solution)/shard_map/ppermute | solution.py:332
  119.0 10.2 %collective-permute-start.23 = (bf16[64,2048]{1,0:T(8,128)(2,1)S(1)}, bf16[64,2048]{1,0:T(8,128)(2,1)S(1)}, u32[]{:S(2)}, u32[]{:S(2)}) collective-permute-start(bf16[64,2048]{1,0:T(8,128)(2,1)S(1)} %get-tuple-element.201), channel_id=1, source_target_pairs={{28,24},{24,28},{20,16},{16,20},{29,25},{25,29},{21,17},{17,21},{3... | collective-permute-start | bytes 786440 | tf_op jit(solution)/shard_map/ppermute | solution.py:327
  119.7 6.6 %copy-start.3 = (bf16[64,2048]{1,0:T(8,128)(2,1)S(1)}, bf16[64,2048]{1,0:T(8,128)(2,1)}, u32[]{:S(2)}) copy-start(bf16[64,2048]{1,0:T(8,128)(2,1)} %copy-done.2) | copy-start | bytes 786436
  125.0 10.6 %copy-start.1 = (bf16[64,2048]{1,0:T(8,128)(2,1)S(1)}, bf16[64,2048]{1,0:T(8,128)(2,1)}, u32[]{:S(2)}) copy-start(bf16[64,2048]{1,0:T(8,128)(2,1)} %copy-done) | copy-start | bytes 786436
  125.0 6.4 %collective-permute-start.21 = (bf16[64,2048]{1,0:T(8,128)(2,1)S(1)}, bf16[64,2048]{1,0:T(8,128)(2,1)S(1)}, u32[]{:S(2)}, u32[]{:S(2)}) collective-permute-start(bf16[64,2048]{1,0:T(8,128)(2,1)S(1)} %get-tuple-element.199), channel_id=1, source_target_pairs={{0,4},{4,0},{8,12},{12,8},{16,20},{20,16},{24,28},{28,24},{1,5},{5... | collective-permute-start | bytes 786440 | tf_op jit(solution)/shard_map/ppermute | solution.py:327
  128.5 7.1 %collective-permute-start.25 = (bf16[64,2048]{1,0:T(8,128)(2,1)S(1)}, bf16[64,2048]{1,0:T(8,128)(2,1)S(1)}, u32[]{:S(2)}, u32[]{:S(2)}) collective-permute-start(bf16[64,2048]{1,0:T(8,128)(2,1)S(1)} %get-tuple-element.208), channel_id=1, source_target_pairs={{24,28},{28,24},{25,29},{29,25},{26,30},{30,26},{27,31},{31,27}} | collective-permute-start | bytes 786440 | tf_op jit(solution)/shard_map/ppermute | solution.py:327
  129.2 6.4 %copy-start.14 = (bf16[64,2048]{1,0:T(8,128)(2,1)}, bf16[64,2048]{1,0:T(8,128)(2,1)S(1)}, u32[]{:S(2)}) copy-start(bf16[64,2048]{1,0:T(8,128)(2,1)S(1)} %collective-permute-done.23.refs_18_.refs_17_) | copy-start | bytes 786436
  133.6 9.9 %collective-permute-start.27 = (bf16[64,2048]{1,0:T(8,128)(2,1)}, bf16[64,2048]{1,0:T(8,128)(2,1)S(1)}, u32[]{:S(2)}, u32[]{:S(2)}) collective-permute-start(bf16[64,2048]{1,0:T(8,128)(2,1)} %get-tuple-element.213), channel_id=1, source_target_pairs={{28,20},{24,16},{20,12},{16,8},{12,4},{8,0},{29,21},{25,17},{21,13... | collective-permute-start | bytes 786440 | tf_op jit(solution)/shard_map/ppermute | solution.py:332
  134.9 8.7 %collective-permute-start.28 = (bf16[64,2048]{1,0:T(8,128)(2,1)S(1)}, bf16[64,2048]{1,0:T(8,128)(2,1)S(1)}, u32[]{:S(2)}, u32[]{:S(2)}) collective-permute-start(bf16[64,2048]{1,0:T(8,128)(2,1)S(1)} %get-tuple-element.214), channel_id=1, source_target_pairs={{28,24},{24,28},{20,16},{16,20},{12,8},{8,12},{29,25},{25,29},{21,... | collective-permute-start | bytes 786440 | tf_op jit(solution)/shard_map/ppermute | solution.py:327
  140.9 9.3 %collective-permute-start.26 = (bf16[64,2048]{1,0:T(8,128)(2,1)}, bf16[64,2048]{1,0:T(8,128)(2,1)S(1)}, u32[]{:S(2)}, u32[]{:S(2)}) collective-permute-start(bf16[64,2048]{1,0:T(8,128)(2,1)} %get-tuple-element.212), channel_id=1, source_target_pairs={{0,4},{4,0},{8,12},{12,8},{16,20},{20,16},{24,28},{28,24},{1,5},{5... | collective-permute-start | bytes 786440 | tf_op jit(solution)/shard_map/ppermute | solution.py:327
  151.8 11.2 %collective-permute-start.29 = (bf16[64,2048]{1,0:T(8,128)(2,1)S(1)}, bf16[64,2048]{1,0:T(8,128)(2,1)S(1)}, u32[]{:S(2)}, u32[]{:S(2)}) collective-permute-start(bf16[64,2048]{1,0:T(8,128)(2,1)S(1)} %get-tuple-element.221), channel_id=1, source_target_pairs={{28,20},{24,16},{20,12},{16,8},{12,4},{8,0},{29,21},{25,17},{21,13... | collective-permute-start | bytes 786440 | tf_op jit(solution)/shard_map/ppermute | solution.py:332
  153.1 9.9 %collective-permute-start.30 = (bf16[64,2048]{1,0:T(8,128)(2,1)S(1)}, bf16[64,2048]{1,0:T(8,128)(2,1)S(1)}, u32[]{:S(2)}, u32[]{:S(2)}) collective-permute-start(bf16[64,2048]{1,0:T(8,128)(2,1)S(1)} %get-tuple-element.222), channel_id=1, source_target_pairs={{28,24},{24,28},{20,16},{16,20},{12,8},{8,12},{4,0},{0,4},{29,25},... | collective-permute-start | bytes 786440 | tf_op jit(solution)/shard_map/ppermute | solution.py:327
  164.5 14.7 %collective-permute-start.31 = (bf16[64,2048]{1,0:T(8,128)(2,1)S(1)}, bf16[64,2048]{1,0:T(8,128)(2,1)S(1)}, u32[]{:S(2)}, u32[]{:S(2)}) collective-permute-start(bf16[64,2048]{1,0:T(8,128)(2,1)S(1)} %get-tuple-element.230), channel_id=1, source_target_pairs={{20,12},{16,8},{12,4},{8,0},{21,13},{17,9},{13,5},{9,1},{22,14},{1... | collective-permute-start | bytes 786440 | tf_op jit(solution)/shard_map/ppermute | solution.py:332
  165.8 13.4 %collective-permute-start.32 = (bf16[64,2048]{1,0:T(8,128)(2,1)S(1)}, bf16[64,2048]{1,0:T(8,128)(2,1)S(1)}, u32[]{:S(2)}, u32[]{:S(2)}) collective-permute-start(bf16[64,2048]{1,0:T(8,128)(2,1)S(1)} %get-tuple-element.231), channel_id=1, source_target_pairs={{20,16},{16,20},{12,8},{8,12},{4,0},{0,4},{21,17},{17,21},{13,9},{... | collective-permute-start | bytes 786440 | tf_op jit(solution)/shard_map/ppermute | solution.py:327
  168.4 1.0 copy-start.13
  179.2 13.5 %copy-start.10 = (bf16[64,2048]{1,0:T(8,128)(2,1)}, bf16[64,2048]{1,0:T(8,128)(2,1)S(1)}, u32[]{:S(2)}) copy-start(bf16[64,2048]{1,0:T(8,128)(2,1)S(1)} %collective-permute-done.32.refs_20_.refs_19_.refs_18_) | copy-start | bytes 786436
  180.8 11.9 %copy-start.22 = (bf16[64,2048]{1,0:T(8,128)(2,1)}, bf16[64,2048]{1,0:T(8,128)(2,1)S(1)}, u32[]{:S(2)}) copy-start(bf16[64,2048]{1,0:T(8,128)(2,1)S(1)} %get-tuple-element.243.refs_16_.refs_15_) | copy-start | bytes 786436
  180.8 11.9 %collective-permute-start.33 = (bf16[64,2048]{1,0:T(8,128)(2,1)S(1)}, bf16[64,2048]{1,0:T(8,128)(2,1)S(1)}, u32[]{:S(2)}, u32[]{:S(2)}) collective-permute-start(bf16[64,2048]{1,0:T(8,128)(2,1)S(1)} %get-tuple-element.244), channel_id=1, source_target_pairs={{12,4},{8,0},{13,5},{9,1},{14,6},{10,2},{15,7},{11,3}} | collective-permute-start | bytes 786440 | tf_op jit(solution)/shard_map/ppermute | solution.py:332
  182.1 10.6 %collective-permute-start.34 = (bf16[64,2048]{1,0:T(8,128)(2,1)S(1)}, bf16[64,2048]{1,0:T(8,128)(2,1)S(1)}, u32[]{:S(2)}, u32[]{:S(2)}) collective-permute-start(bf16[64,2048]{1,0:T(8,128)(2,1)S(1)} %get-tuple-element.245), channel_id=1, source_target_pairs={{12,8},{8,12},{4,0},{0,4},{13,9},{9,13},{5,1},{1,5},{14,10},{10,14... | collective-permute-start | bytes 786440 | tf_op jit(solution)/shard_map/ppermute | solution.py:327
  196.5 12.6 %collective-permute-start.35 = (bf16[64,2048]{1,0:T(8,128)(2,1)}, bf16[64,2048]{1,0:T(8,128)(2,1)S(1)}, u32[]{:S(2)}, u32[]{:S(2)}) collective-permute-start(bf16[64,2048]{1,0:T(8,128)(2,1)} %get-tuple-element.258), channel_id=1, source_target_pairs={{4,0},{0,4},{5,1},{1,5},{6,2},{2,6},{7,3},{3,7}} | collective-permute-start | bytes 786440 | tf_op jit(solution)/shard_map/ppermute | solution.py:327
  199.1 1.0 copy-start.11
  202.0 7.1 %copy-start.33 = (bf16[64,2048]{1,0:T(8,128)(2,1)S(1)}, bf16[64,2048]{1,0:T(8,128)(2,1)}, u32[]{:S(2)}) copy-start(bf16[64,2048]{1,0:T(8,128)(2,1)} %copy-done.32) | copy-start | bytes 786436
  222.0 8.3 %collective-permute-start.36 = (f32[3,10240]{1,0:T(4,128)}, f32[3,10240]{1,0:T(4,128)S(1)}, u32[]{:S(2)}, u32[]{:S(2)}) collective-permute-start(f32[3,10240]{1,0:T(4,128)} %get-tuple-element.280), channel_id=1, source_target_pairs={{4,0},{8,4},{12,8},{16,12},{20,16},{24,20},{28,24},{5,1},{9,5},{13... | collective-permute-start | bytes 368648 | tf_op jit(solution)/shard_map/ppermute | solution.py:515
  225.8 16.5 %all-to-all-start = ((f32[32,1,2560]{2,1,0:T(1,128)}), f32[32,1,2560]{2,1,0:T(1,128)S(1)}, u32[]{:S(2)}, u32[]{:S(2)}) async-start(f32[32,1,2560]{2,1,0:T(1,128)} %all_to_all.13), calls=%async_computation | async-start | bytes 655360 | tf_op jit(solution)/shard_map/all_to_all | solution.py:531
  243.2 10.3 %all-to-all-start.1 = ((f32[8,1,2560]{2,1,0:T(1,128)}), f32[8,1,2560]{2,1,0:T(1,128)S(1)}, u32[]{:S(2)}, u32[]{:S(2)}) async-start(f32[8,1,2560]{2,1,0:T(1,128)} %broadcast_in_dim.49), calls=%async_computation.1 | async-start | bytes 163840 | tf_op jit(solution)/shard_map/all_to_all | solution.py:534
  (13 other events, 10.8 us)
